TPU v7x, 32 devices: a whole 2x2x4 slice. The times are simulated.
32 devices in a mesh: wide: 8 (over z, x), narrow: 4 (over y, core).
Axes of the slice: x: 2, y: 2, z: 4, core: 2. Of those that a mesh axis runs over, the one named last changes fastest.
Arguments:
- tokens: bfloat16 [24576, 768], P('wide'), may hold values from -6 to 6
- qkv_weight: bfloat16 [3, 768, 768], P(None, None, 'narrow'), may hold values from -0.21875 to 0.21875
- out_weight: bfloat16 [768, 768], P('narrow'), may hold values from -0.875 to 0.875
- norm_bias: float32 [6, 768], replicated, as said below
- up_weight: bfloat16 [2, 768, 3072], P(None, None, 'narrow'), may hold values from -0.21875 to 0.21875
- down_weight: bfloat16 [3072, 768], P('narrow'), may hold values from -0.15625 to 0.15625
- window_lengths: int32 [48], P('wide'), may hold values from 64 to 512, as said below
- cot_out: bfloat16 [24576, 768], P('wide'), may hold values from -6 to 6
Outputs:
- block_out: bfloat16 [24576, 768], P('wide')
- input_grad: float32 [24576, 768], P('wide')
- qkv_grad: float32 [3, 768, 768], P(None, 'wide', 'narrow')
- out_grad: float32 [768, 768], P('narrow', 'wide')
- up_grad: float32 [2, 768, 3072], P(None, 'wide', 'narrow')
- down_grad: float32 [3072, 768], P('narrow', 'wide')
- norm_bias_grad: float32 [6, 768], P(None, 'wide')
Inputs may be any that keep to these rules, and one draw needn't show every extreme that they name: `window_lengths`: keys at or past a window's length are padding; some window holds exactly 512 and some exactly 64. `norm_bias`: rows 0 and 3 lie between 0.5 and 2.
All inputs are finite; a program needn't handle non-finite values.
Results may differ from a plain program's by a relative error of at most 0.025.
Values may be sent and summed in bfloat16 or wider, within the bound.
A program may use at most 192 MiB of HBM per device.

v0:
```python
import math

import jax
import jax.numpy as jnp
from jax import lax
from jax.sharding import PartitionSpec as P

HEADS = 12
HEAD_DIM = 64


def norm_parts(value, gain, shift):
    center = value - jnp.mean(value, axis=-1, keepdims=True)
    spread = jnp.mean(center * center, axis=-1, keepdims=True)
    recip = lax.rsqrt(spread + 1e-05)
    normed = center * recip
    return (normed * gain + shift, normed, recip)


def norm_backward(grad_out, normed, recip, gain):
    scaled = grad_out * gain
    inner = jnp.mean(scaled * normed, axis=-1, keepdims=True)
    grad_in = recip * (scaled - jnp.mean(scaled, axis=-1, keepdims=True) - normed * inner)
    return (grad_in, jnp.sum(grad_out * normed, axis=0), jnp.sum(grad_out, axis=0))


def shards(
    tokens, qkv_weight, out_weight, norm_bias, up_weight, down_weight, window_lengths, cot_out
):
    head_count = qkv_weight.shape[2] // HEAD_DIM
    group_width = qkv_weight.shape[2]
    first_head = lax.axis_index("narrow") * head_count
    slopes = 2.0 ** (-8.0 * (first_head + jnp.arange(head_count) + 1).astype(jnp.float32) / HEADS)
    token_count = tokens.shape[0]
    windows = window_lengths.shape[0]
    window_len = token_count // windows
    score_scale = 1.0 / math.sqrt(HEAD_DIM)
    position = jnp.arange(window_len)
    distance = jnp.abs(position[:, None] - position[None, :]).astype(jnp.float32)

    def score_block(query, key_rows, key_limit):
        raw_scores = jnp.einsum("qhc,khc->hqk", query, key_rows, preferred_element_type=jnp.float32)
        logits = raw_scores * score_scale - slopes[:, None, None] * distance[None]
        return jnp.where(position[None, None, :] < key_limit, logits, -1e30)

    def window_forward(item):
        window_block, key_limit = item
        logits = score_block(window_block[0], window_block[1], key_limit)
        row_top = jnp.max(logits, axis=-1, keepdims=True)
        exponent = jnp.exp(logits - row_top)
        row_total = jnp.sum(exponent, axis=-1, keepdims=True)
        soft_low = (exponent / row_total).astype(jnp.bfloat16)
        log_total = (row_top + jnp.log(row_total))[..., 0]
        result = jnp.einsum(
            "hqk,khc->qhc", soft_low, window_block[2], preferred_element_type=jnp.float32
        )
        return (result.astype(jnp.bfloat16), log_total)

    def window_backward(item):
        window_block, grad_result, log_total, key_limit = item
        logits = score_block(window_block[0], window_block[1], key_limit)
        soft = jnp.exp(logits - log_total[..., None])
        grad_soft = jnp.einsum(
            "qhc,khc->hqk", grad_result, window_block[2], preferred_element_type=jnp.float32
        )
        row_inner = jnp.sum(soft * grad_soft, axis=-1, keepdims=True)
        grad_logit = (soft * (grad_soft - row_inner) * score_scale).astype(jnp.bfloat16)
        grad_query = jnp.einsum(
            "hqk,khc->qhc", grad_logit, window_block[1], preferred_element_type=jnp.float32
        )
        grad_key = jnp.einsum(
            "hqk,qhc->khc", grad_logit, window_block[0], preferred_element_type=jnp.float32
        )
        grad_value = jnp.einsum(
            "hqk,qhc->khc",
            soft.astype(jnp.bfloat16),
            grad_result,
            preferred_element_type=jnp.float32,
        )
        return jnp.stack([grad_query, grad_key, grad_value]).astype(jnp.bfloat16)

    source = tokens.astype(jnp.float32)
    projected = jnp.einsum(
        "td,kdf->ktf", tokens, qkv_weight, preferred_element_type=jnp.float32
    ).astype(jnp.bfloat16)
    window_blocks = jnp.moveaxis(
        projected.reshape(3, windows, window_len, head_count, HEAD_DIM), 1, 0
    )
    attended, log_totals = lax.map(window_forward, (window_blocks, window_lengths))
    attended = attended.reshape(token_count, group_width)
    attn_part = jnp.dot(attended, out_weight, preferred_element_type=jnp.float32)
    attn_branch = lax.psum(attn_part.astype(jnp.bfloat16), "narrow").astype(jnp.float32)
    hidden, normed_one, recip_one = norm_parts(
        attn_branch + norm_bias[2] + source, norm_bias[0], norm_bias[1]
    )
    hidden_low = hidden.astype(jnp.bfloat16)
    gate_up = jnp.einsum("td,kdf->ktf", hidden_low, up_weight, preferred_element_type=jnp.float32)

    def geglu(gate_val, up_val):
        return jax.nn.gelu(gate_val, approximate=False) * up_val

    activation_full, geglu_pull = jax.vjp(geglu, gate_up[0], gate_up[1])
    activation = activation_full.astype(jnp.bfloat16)
    ffn_part = jnp.dot(activation, down_weight, preferred_element_type=jnp.float32)
    ffn_branch = lax.psum(ffn_part.astype(jnp.bfloat16), "narrow").astype(jnp.float32)
    output, normed_two, recip_two = norm_parts(
        ffn_branch + norm_bias[5] + hidden, norm_bias[3], norm_bias[4]
    )
    block_out = output.astype(jnp.bfloat16)
    cotangent = cot_out.astype(jnp.float32)
    grad_second, grad_gain_two, grad_shift_two = norm_backward(
        cotangent, normed_two, recip_two, norm_bias[3]
    )
    grad_down_bias = jnp.sum(grad_second, axis=0)
    grad_second_low = grad_second.astype(jnp.bfloat16)
    down_grad = jnp.einsum(
        "tf,td->fd", activation, grad_second_low, preferred_element_type=jnp.float32
    )
    grad_activation = jnp.einsum(
        "td,fd->tf", grad_second_low, down_weight, preferred_element_type=jnp.float32
    )
    grad_gate, grad_up_val = geglu_pull(grad_activation)
    grad_gate_up = jnp.stack([grad_gate, grad_up_val]).astype(jnp.bfloat16)
    up_grad = jnp.einsum(
        "td,ktf->kdf", hidden_low, grad_gate_up, preferred_element_type=jnp.float32
    )
    hidden_part = jnp.einsum(
        "ktf,kdf->td", grad_gate_up, up_weight, preferred_element_type=jnp.float32
    )
    small_ffn = jnp.stack([grad_gain_two, grad_shift_two, grad_down_bias])
    grad_hidden = grad_second + lax.psum(hidden_part.astype(jnp.bfloat16), "narrow").astype(
        jnp.float32
    )
    grad_first, grad_gain_one, grad_shift_one = norm_backward(
        grad_hidden, normed_one, recip_one, norm_bias[0]
    )
    grad_out_bias = jnp.sum(grad_first, axis=0)
    grad_first_low = grad_first.astype(jnp.bfloat16)
    out_grad = jnp.einsum("tf,td->fd", attended, grad_first_low, preferred_element_type=jnp.float32)
    grad_attended = jnp.einsum(
        "td,fd->tf", grad_first_low, out_weight, preferred_element_type=jnp.float32
    )
    grad_attended = grad_attended.astype(jnp.bfloat16).reshape(
        windows, window_len, head_count, HEAD_DIM
    )
    grad_blocks = lax.map(
        window_backward, (window_blocks, grad_attended, log_totals, window_lengths)
    )
    grad_projected = jnp.moveaxis(grad_blocks, 1, 0).reshape(3, token_count, group_width)
    qkv_grad = jnp.einsum("td,ktf->kdf", tokens, grad_projected, preferred_element_type=jnp.float32)
    source_part = jnp.einsum(
        "ktf,kdf->td", grad_projected, qkv_weight, preferred_element_type=jnp.float32
    )
    small_attn = jnp.stack([grad_gain_one, grad_shift_one, grad_out_bias])
    input_grad = grad_first + lax.psum(source_part.astype(jnp.bfloat16), "narrow").astype(
        jnp.float32
    )
    small_all = jnp.concatenate([small_attn, small_ffn], axis=0)
    qkv_share, out_share, up_share, down_share, small_share = (
        lax.psum_scatter(qkv_grad, "wide", scatter_dimension=1, tiled=True),
        lax.psum_scatter(out_grad, "wide", scatter_dimension=1, tiled=True),
        lax.psum_scatter(up_grad, "wide", scatter_dimension=1, tiled=True),
        lax.psum_scatter(down_grad, "wide", scatter_dimension=1, tiled=True),
        lax.psum_scatter(small_all, "wide", scatter_dimension=1, tiled=True),
    )
    return (block_out, input_grad, qkv_share, out_share, up_share, down_share, small_share)


def solution(mesh):
    placed = (
        P("wide", None),
        P(None, None, "narrow"),
        P("narrow", None),
        P(),
        P(None, None, "narrow"),
        P("narrow", None),
        P("wide"),
        P("wide", None),
    )
    return jax.shard_map(
        shards,
        mesh=mesh,
        in_specs=placed,
        out_specs=(
            P("wide", None),
            P("wide", None),
            P(None, "wide", "narrow"),
            P("narrow", "wide"),
            P(None, "wide", "narrow"),
            P("narrow", "wide"),
            P(None, "wide"),
        ),
        check_vma=False,
    )
```

profile of v0, /device:TPU:0, one launch (start us, length us, event | category | flops | bytes accessed | tf_op | source)
XLA Modules:
  0.0 1051.4 jit_solution(7509393685170289483)
XLA Ops:
  7.2 7.5 fusion.106
  14.7 8.1 reshape.169
  28.1 56.5 %while.24 = (s32[]{:T(128)}, bf16[6,512,3,64]{1,3,2,0:T(8,128)(2,1)}, f32[6,3,512]{2,1,0:T(4,128)}, bf16[6,3,512,3,64]{2,4,3,1,0:T(8,128)(2,1)}, s32[6]{0:T(128)...) while((s32[]{:T(128)}, bf16[6,512,3,64]{1,3,2,0:T(8,128)(2,1)}, ...), condition=%wide.region_3.4_spmd.clone, body=%wide.region_0.3_spmd.clone.sunk | while | flops 210074640 | bytes 24958668 | solution.py:89
  93.0 96.5 %all-reduce.7.cloned.1.call-done = bf16[3072,768]{1,0:T(8,128)(2,1)} async-done(((bf16[3072,768]{1,0:T(8,128)(2,1)}), bf16[3072,768]{1,0:T(8,128)(2,1)}) %all-reduce.7.cloned.1.call-update) | async-done | bytes 4718608 | tf_op jit(solution)/shard_map/psum | solution.py:92
  199.4 11.3 %convolution_bitcast_fusion = f32[2,3072,768]{2,1,0:T(8,128)} fusion(bf16[2,768,768]{2,1,0:T(8,128)(2,1)S(1)} %copy-done, f32[768]{0:T(1024)S(1)} %get-tuple-element.201, f32[768]{0:T(1024)S(1)} %get-tuple-element.202, bf16[3072,768]{1,0:T(8,128)(2,1)S(1)} %bitcast.244, bf16[3072,768]{1,0:T(8,128)(2,1)S(1)} %copy-done.2, f32[3072]{0:T(1024)S(1)} %add_rsqrt_fusion.1, ...), kind=kOutput, calls=%fused_computation.122 | convolution fusion | flops 7268990976 | bytes 30704640 | tf_op jit(solution)/shard_map/td,kdf->ktf/dot_general | solution.py:97
  210.7 22.9 %multiply_convert_fusion.2 = (bf16[3072,768]{1,0:T(8,128)(2,1)S(1)}, f32[3072,768]{1,0:T(8,128)}) fusion(f32[2,3072,768]{2,1,0:T(8,128)} %convolution_bitcast_fusion), kind=kLoop, calls=%fused_computation.100 | loop fusion | flops 155713536 | bytes 33030144 | tf_op jit(solution)/shard_map/convert_element_type | solution.py:103
  241.7 93.8 %all-reduce.9.cloned.1.call-done = bf16[3072,768]{1,0:T(8,128)(2,1)} async-done(((bf16[3072,768]{1,0:T(8,128)(2,1)}), bf16[3072,768]{1,0:T(8,128)(2,1)}) %all-reduce.9.cloned.1.call-update) | async-done | bytes 4718608 | tf_op jit(solution)/shard_map/psum | solution.py:105
  335.5 7.6 fusion.129
  356.8 19.1 %fusion.102 = (bf16[1,3072,768]{2,1,0:T(8,128)(2,1)}, bf16[1,3072,768]{2,1,0:T(8,128)(2,1)}) fusion(f32[3072,768]{1,0:T(8,128)} %get-tuple-element.236, f32[2,3072,768]{2,1,0:T(8,128)} %convolution_bitcast_fusion, bf16[768,768]{1,0:T(8,128)(2,1)} %param.17, f32[3072,768]{1,0:T(8,128)} %get-tuple-element.241), kind=kOutput, calls=%fused_computation.134 | convolution fusion | flops 3668705280 | bytes 48365568 | tf_op jit(solution)/shard_map/td,fd->tf/dot_general | solution.py:119
  376.0 11.6 %bitcast_convert_fusion.1 = bf16[3072,768]{1,0:T(8,128)(2,1)} fusion(bf16[2,768,768]{2,1,0:T(8,128)(2,1)S(1)} %copy-done, bf16[1,3072,768]{2,1,0:T(8,128)(2,1)} %get-tuple-element.240, bf16[1,3072,768]{2,1,0:T(8,128)(2,1)} %get-tuple-element.239), kind=kOutput, calls=%fused_computation.77 | convolution fusion | flops 7254835200 | bytes 16515072 | tf_op jit(solution)/shard_map/ktf,kdf->td/dot_general | solution.py:127
  387.8 94.1 %all-reduce.11.cloned.1.call-done = bf16[3072,768]{1,0:T(8,128)(2,1)} async-done(((bf16[3072,768]{1,0:T(8,128)(2,1)}), bf16[3072,768]{1,0:T(8,128)(2,1)}) %all-reduce.11.cloned.1.call-update) | async-done | bytes 4718608 | tf_op jit(solution)/shard_map/psum | solution.py:131
  481.9 11.2 %multiply_reduce_fusion.1 = (f32[768]{0:T(1024)S(1)}, f32[3072]{0:T(1024)S(1)}, f32[3072]{0:T(1024)S(1)}, f32[768]{0:T(1024)S(1)}, f32[768]{0:T(1024)S(1)}) fusion(f32[3072,768]{1,0:T(8,128)} %get-tuple-element.241, bf16[3072,768]{1,0:T(8,128)(2,1)} %all-reduce.11.cloned.1.call-done, f32[3072]{0:T(1024)S(1)} %add_rsqrt_fusion.1, ...), kind=kLoop, calls=%fused_computation.91 | loop fusion | flops 37740288 | bytes 23657472 | tf_op jit(solution)/shard_map/reduce_sum | solution.py:24
  493.2 12.8 %fusion.128 = (f32[768]{0:T(1024)S(1)}, f32[3072,768]{1,0:T(8,128)}) fusion(f32[3072]{0:T(1024)S(1)} %broadcast_multiply_fusion, f32[3072]{0:T(1024)S(1)} %broadcast_multiply_fusion.5, bf16[3072,768]{1,0:T(8,128)(2,1)} %param.12, f32[768]{0:T(1024)S(1)} %get-tuple-element.203, bf16[3072,768]{1,0:T(8,128)(2,1)} %all-reduce.7.cloned.1.call-done, ...), kind=kLoop, calls=%fused_computation.166 | loop fusion | flops 33029376 | bytes 33088512 | tf_op jit(solution)/shard_map/reduce_sum | solution.py:137
  513.7 17.7 %fusion.116 = f32[2,768,768]{1,2,0:T(8,128)} fusion(bf16[1,3072,768]{2,1,0:T(8,128)(2,1)} %get-tuple-element.240, bf16[1,3072,768]{2,1,0:T(8,128)(2,1)} %get-tuple-element.239, f32[768]{0:T(1024)S(1)} %get-tuple-element.201, f32[768]{0:T(1024)S(1)} %get-tuple-element.202, bf16[3072,768]{1,0:T(8,128)(2,1)} %param.12, ...), kind=kOutput, calls=%fused_computation.145 | convolution fusion | flops 7273709568 | bytes 23626752 | tf_op jit(solution)/shard_map/td,ktf->kdf/dot_general | solution.py:124
  531.4 8.2 copy.46
  549.5 143.8 %while.25 = (s32[]{:T(128)}, bf16[6,3,512,3,64]{2,4,3,1,0:T(8,128)(2,1)}, bf16[6,3,512,3,64]{2,4,3,1,0:T(8,128)(2,1)}, s32[6]{0:T(128)S(1)}, f32[6,3,512]{2,1,0:...) while((s32[]{:T(128)}, ...), condition=%wide.region_17.18_spmd.clone, body=%wide.region_15.17_spmd.clone.sunk | while | flops 518754816 | bytes 39869124 | solution.py:146
  699.9 8.2 reshape.172
  708.1 7.7 bitcast_convert_fusion
  730.1 10.4 fusion.112
  745.0 61.0 %all-reduce.15.cloned.1.call-done = f32[2,768,768]{2,0,1:T(2,128)} async-done(((f32[2,768,768]{2,0,1:T(2,128)}), f32[2,768,768]{2,0,1:T(2,128)}) %all-reduce.15.cloned.1.call-update) | async-done | bytes 4718608
  807.9 93.6 %all-reduce.13.cloned.1.call-done = bf16[3072,768]{1,0:T(8,128)(2,1)} async-done(((bf16[3072,768]{1,0:T(8,128)(2,1)}), bf16[3072,768]{1,0:T(8,128)(2,1)}) %all-reduce.13.cloned.1.call-update) | async-done | bytes 4718608 | tf_op jit(solution)/shard_map/psum | solution.py:155
  901.5 9.7 convert_add_fusion
  911.1 61.2 %reduce-scatter.13.cloned.1.call-done = f32[96,576]{1,0:T(8,128)} async-done(((f32[768,576]{1,0:T(8,128)}), f32[96,576]{1,0:T(8,128)}) %reduce-scatter.13.cloned.1.call-update) | async-done | bytes 221200
  974.2 70.2 %reduce-scatter.11.cloned.1.call-done = f32[768,96]{0,1:T(8,128)} async-done(((f32[768,768]{0,1:T(8,128)}), f32[768,96]{0,1:T(8,128)}) %reduce-scatter.11.cloned.1.call-update) | async-done | bytes 294928 | tf_op jit(solution)/shard_map/reduce_scatter | solution.py:163
  (228 shorter events, 291.3 us)
Async XLA Ops:
  7.2 192.2 %copy-start = (bf16[2,768,768]{2,1,0:T(8,128)(2,1)S(1)}, bf16[2,768,768]{2,1,0:T(8,128)(2,1)}, u32[]{:S(2)}) copy-start(bf16[2,768,768]{2,1,0:T(8,128)(2,1)} %param.16) | copy-start | bytes 7077892
  7.2 182.4 %all-reduce.7.cloned.1.call-start = ((), (), s32[]{:S(2)}) async-start(), calls=%async_computation.4 | async-start | bytes 9437184 | tf_op jit(solution)/shard_map/psum | solution.py:92
  14.7 13.4 %copy-start.12 = (s32[6]{0:T(128)S(1)}, s32[6]{0:T(128)}, u32[]{:S(2)}) copy-start(s32[6]{0:T(128)} %param.18) | copy-start | bytes 76
  86.6 6.4 copy-start.9
  92.7 102.4 %slice-start = ((s8[4718592]{0:T(1024)(128)(4,1)}), s8[524288]{0:T(1024)(128)(4,1)S(1)}, s32[]{:S(2)}) async-start(s8[4718592]{0:T(1024)(128)(4,1)} %bitcast.243), calls=%async_computation.13 | async-start | bytes 1048576
  92.7 242.8 %all-reduce.9.cloned.1.call-start = ((), (), s32[]{:S(2)}) async-start(), calls=%async_computation.5 | async-start | bytes 9437184 | tf_op jit(solution)/shard_map/psum | solution.py:105
  189.6 5.5 copy-start.2
  189.6 6.4 slice-start.1
  210.6 25.0 %copy-start.10 = (bf16[768,768]{1,0:T(8,128)(2,1)S(1)}, bf16[768,768]{1,0:T(8,128)(2,1)}, u32[]{:S(2)}) copy-start(bf16[768,768]{1,0:T(8,128)(2,1)} %param.17) | copy-start | bytes 3538948
  241.1 240.8 %all-reduce.11.cloned.1.call-start = ((), (), s32[]{:S(2)}) async-start(), calls=%async_computation.6 | async-start | bytes 9437184 | tf_op jit(solution)/shard_map/psum | solution.py:131
  343.1 2.3 slice-start.3
  387.6 354.3 %reduce-scatter.17.cloned.1.call-start = ((), (), s32[]{:S(2)}) async-start(), calls=%async_computation.11 | async-start | bytes 442368
  481.9 11.3 %copy-start.4 = (bf16[3072,768]{1,0:T(8,128)(2,1)S(1)}, bf16[3072,768]{1,0:T(8,128)(2,1)}, u32[]{:S(2)}) copy-start(bf16[3072,768]{1,0:T(8,128)(2,1)} %all-reduce.11.cloned.1.call-done) | copy-start | bytes 14155780
  493.2 13.9 %copy-start.6 = (bf16[24,8,6,512]{3,1,2,0:T(8,128)(2,1)S(1)}, bf16[24,8,6,512]{3,1,2,0:T(8,128)(2,1)}, u32[]{:S(2)}) copy-start(bf16[24,8,6,512]{3,1,2,0:T(8,128)(2,1)} %copy-done.5) | copy-start | bytes 3538948
  507.0 236.3 %reduce-scatter.15.cloned.1.call-start = ((), (), s32[]{:S(2)}) async-start(), calls=%async_computation.10 | async-start | bytes 884736
  513.6 292.3 %all-reduce.15.cloned.1.call-start = ((), (), s32[]{:S(2)}) async-start(), calls=%async_computation.12 | async-start | bytes 9437184
  531.4 8.5 copy-start.8
  539.7 9.8 copy-start.13
  539.7 361.8 %all-reduce.13.cloned.1.call-start = ((), (), s32[]{:S(2)}) async-start(), calls=%async_computation.7 | async-start | bytes 9437184 | tf_op jit(solution)/shard_map/psum | solution.py:155
  693.3 14.9 %copy-start.11 = (bf16[3,768,192]{1,2,0:T(8,128)(2,1)S(1)}, bf16[3,768,192]{1,2,0:T(8,128)(2,1)}, u32[]{:S(2)}) copy-start(bf16[3,768,192]{1,2,0:T(8,128)(2,1)} %param.13) | copy-start | bytes 2654212
  715.9 256.4 %reduce-scatter.13.cloned.1.call-start = ((), (), s32[]{:S(2)}) async-start(), calls=%async_computation.9 | async-start | bytes 2211840
  730.1 10.5 %copy-start.14 = (u32[32]{0:T(128)S(1)}, u32[32]{0:T(128)}, u32[]{:S(2)}) copy-start(u32[32]{0:T(128)} %constant.135) | copy-start | bytes 388
  730.1 314.3 %reduce-scatter.11.cloned.1.call-start = ((), (), s32[]{:S(2)}) async-start(), calls=%async_computation.8 | async-start | bytes 2654208 | tf_op jit(solution)/shard_map/reduce_scatter | solution.py:163
  807.1 237.3 %copy-start.1 = (bf16[2,768,768]{2,1,0:T(8,128)(2,1)S(1)}, bf16[2,768,768]{2,1,0:T(8,128)(2,1)}, u32[]{:S(2)}) copy-start(bf16[2,768,768]{2,1,0:T(8,128)(2,1)} %param.16) | copy-start | bytes 7077892
  (9 other events, 15.4 us)
Sparse Core Ops, SparseCore 0:
  92.8 96.7 all-reduce.6
  241.3 94.1 all-reduce.8
  387.7 94.1 all-reduce.10
  507.1 61.5 reduce-scatter.16
  571.9 61.4 reduce-scatter.14
  637.3 168.6 all-reduce.14
  808.4 93.0 all-reduce.12
  905.4 66.9 reduce-scatter.12
  976.4 67.9 reduce-scatter.10
where the time goes:
time: 1060 us; the launch traced here: 1050 us
  waiting for transfers between devices  570 us (54%)
  matrix products  271 us (26%)
  other arithmetic  108 us (10%)
  local copies, waits for them, and re-layouts  84.4 us (8%)
  between operations  15.3 us (1%)
    unnamed x13, waiting for transfers between devices  122 us
    psum x1, waiting for transfers between devices, shards(): lax.psum(attn_part.astype(jnp.bfloat16), 'narrow').astype(jnp.float32)  96.5 us
    psum x1, waiting for transfers between devices, shards(): lax.psum(hidden_part.astype(jnp.bfloat16), 'narrow').astype(jnp.float32)  94.1 us
    psum x1, waiting for transfers between devices, shards(): lax.psum(ffn_part.astype(jnp.bfloat16), 'narrow').astype(jnp.float32)  93.8 us
    psum x1, waiting for transfers between devices, shards(): lax.psum(source_part.astype(jnp.bfloat16), 'narrow').astype(jnp.float32)  93.6 us
    reduce_scatter x1, waiting for transfers between devices, shards(): lax.psum_scatter(down_grad, 'wide', scatter_dimension=1, tiled=True)  70.2 us
    dot_general x6, matrix products, window_backward(): jnp.einsum('hqk,khc->qhc', grad_logit, window_block[1], preferred_element...  34.7 us
    dot_general x6, matrix products, window_backward(): jnp.einsum('hqk,qhc->khc', grad_logit, window_block[0], preferred_element...  34.3 us
  transfers between devices with their start and end apart: 9, of which 7 were waited for; matrix products, arithmetic and copies ran while one was open for 24% of the time, Pallas kernels for 0%

commit v1 on v0

v1 whole, which is shorter than its diff:
```python
import functools
import math

import jax
import jax.numpy as jnp
from jax import lax
from jax.experimental import pallas as pl
from jax.experimental.pallas import tpu as pltpu
from jax.sharding import Mesh, PartitionSpec as P

HEADS = 12
HEAD_DIM = 64
EPS = 1e-05
F32 = jnp.float32
BF16 = jnp.bfloat16
SCALE = 1.0 / math.sqrt(HEAD_DIM)
NEG = -1e30
VMEM_LIMIT = 56 * 1024 * 1024


def dot(a, b):
    return lax.dot_general(a, b, (((1,), (0,)), ((), ())), preferred_element_type=F32)


def dot_nt(a, b):
    return lax.dot_general(a, b, (((1,), (1,)), ((), ())), preferred_element_type=F32)


def dot_tn(a, b):
    return lax.dot_general(a, b, (((0,), (0,)), ((), ())), preferred_element_type=F32)


def whole(shape):
    return pl.BlockSpec(shape, lambda i, *_: (0,) * len(shape))


def head_lanes(width):
    lane = lax.broadcasted_iota(jnp.int32, (1, width), 1)
    return [(lane >= h * HEAD_DIM) & (lane < (h + 1) * HEAD_DIM) for h in range(width // HEAD_DIM)]


def fill_distance(ref):
    n = ref.shape[0]
    row = lax.broadcasted_iota(jnp.int32, (n, n), 0)
    col = lax.broadcasted_iota(jnp.int32, (n, n), 1)
    ref[...] = jnp.abs(row - col).astype(F32)


def params():
    return pltpu.CompilerParams(vmem_limit_bytes=VMEM_LIMIT, dimension_semantics=("arbitrary",))


def attn_fwd_kernel(last, info, slopes, x_ref, wqkv, wout, *rest):
    if last:
        prev, proj, att_ref, lse_ref, part, dist = rest
    else:
        proj, att_ref, lse_ref, part, dist = rest
    step = pl.program_id(0)
    win = x_ref.shape[0]
    width = wqkv.shape[2]
    heads = width // HEAD_DIM

    @pl.when(step == 0)
    def _():
        fill_distance(dist)

    x = x_ref[...]
    q = dot(x, wqkv[0]).astype(BF16)
    k = dot(x, wqkv[1]).astype(BF16)
    v = dot(x, wqkv[2]).astype(BF16)
    proj[0], proj[1], proj[2] = q, k, v
    limit = info[1 + info[0] * pl.num_programs(0) + step]
    lanes = head_lanes(width)
    key_on = lax.broadcasted_iota(jnp.int32, (1, win), 1) < limit
    rows = win // 2
    stat_lane = lax.broadcasted_iota(jnp.int32, (1, 128), 1)
    for b in range(win // rows):
        at = slice(b * rows, (b + 1) * rows)
        qb = q[at] * jnp.asarray(SCALE, BF16)
        att = jnp.zeros((rows, width), F32)
        stat = jnp.zeros((rows, 128), F32)
        for h in range(heads):
            qh = jnp.where(lanes[h], qb, jnp.zeros_like(qb))
            s = dot_nt(qh, k) - slopes[h] * dist[at]
            s = jnp.where(key_on, s, NEG)
            top = jnp.max(s, axis=1, keepdims=True)
            p = jnp.exp(s - top)
            total = jnp.sum(p, axis=1, keepdims=True)
            o = dot(p.astype(BF16), v) * (1.0 / total)
            att = jnp.where(lanes[h], o, att)
            stat = jnp.where(stat_lane == h, top + jnp.log(total), stat)
        attb = att.astype(BF16)
        att_ref[at] = attb
        lse_ref[0, :, at] = stat.T[0:8]
        out = dot(attb, wout[...])
        if last:
            out = out + prev[at].astype(F32)
        part[at] = out.astype(BF16)


def attn_fwd(info, slopes, tokens, wqkv, wout, prev):
    _, d, width = wqkv.shape
    nwin = (info.shape[0] - 1) // 2
    win = tokens.shape[0] // (2 * nwin)
    half = nwin * win
    last = prev is not None
    heads = width // HEAD_DIM
    row = lambda w: pl.BlockSpec((win, w), lambda i, *_: (i, 0))
    specs = [
        pl.BlockSpec((win, d), lambda i, info, sl: (info[0] * nwin + i, 0)),
        whole(wqkv.shape),
        whole(wout.shape),
    ]
    args = [tokens, wqkv, wout]
    if last:
        specs.append(row(d))
        args.append(prev)
    return pl.pallas_call(
        functools.partial(attn_fwd_kernel, last),
        grid_spec=pltpu.PrefetchScalarGridSpec(
            num_scalar_prefetch=2,
            grid=(nwin,),
            in_specs=specs,
            out_specs=[
                pl.BlockSpec((3, win, width), lambda i, *_: (0, i, 0)),
                row(width),
                pl.BlockSpec((1, 8, win), lambda i, *_: (i, 0, 0)),
                row(d),
            ],
            scratch_shapes=[pltpu.VMEM((win, win), F32)],
        ),
        out_shape=[
            jax.ShapeDtypeStruct((3, half, width), BF16),
            jax.ShapeDtypeStruct((half, width), BF16),
            jax.ShapeDtypeStruct((nwin, 8, win), F32),
            jax.ShapeDtypeStruct((half, d), BF16),
        ],
        compiler_params=params(),
        cost_estimate=pl.CostEstimate(
            flops=2 * half * d * width * 4 + 4 * nwin * heads * win * win * 256,
            bytes_accessed=2 * (half * d * 2 + half * width * 4 + d * width * 4),
            transcendentals=nwin * heads * win * win,
        ),
        name="attn_fwd_last" if last else "attn_fwd_first",
    )(info, slopes, *args)


def standardize(value):
    center = value - jnp.mean(value, axis=1, keepdims=True)
    recip = lax.rsqrt(jnp.mean(center * center, axis=1, keepdims=True) + EPS)
    return center * recip, recip


def norm_grad(grad, normed, recip, gain):
    e = grad * gain
    inner = jnp.mean(e * normed, axis=1, keepdims=True)
    return recip * (e - jnp.mean(e, axis=1, keepdims=True) - normed * inner)


def rows_of_sums(values):
    width = values[0].shape[1]
    sums = [jnp.sum(v, axis=0, keepdims=True) for v in values]
    return jnp.concatenate(sums + [jnp.zeros((8 - len(sums), width), F32)], axis=0)


def feed(hb, up, down, a_ref, b_ref, act_ref):
    hidden = down.shape[0]
    step = 256
    total = None
    for at in range(0, hidden, step):
        cols = slice(at, at + step)
        gate = dot(hb, up[0, :, cols])
        lift = dot(hb, up[1, :, cols])
        cdf = 0.5 * (1.0 + lax.erf(gate * (1.0 / math.sqrt(2.0))))
        pdf = jnp.exp(-0.5 * gate * gate) * (1.0 / math.sqrt(2.0 * math.pi))
        gelu = gate * cdf
        act = (gelu * lift).astype(BF16)
        a_ref[:, cols] = (lift * (cdf + gate * pdf)).astype(BF16)
        b_ref[:, cols] = gelu.astype(BF16)
        act_ref[:, cols] = act
        term = dot(act, down[cols, :])
        total = term if total is None else total + term
    return total


def ffn_first_kernel(pa, pb, x_ref, nb, up, down, normed_ref, recip_ref, h_ref, a_ref, b_ref, act_ref, part):
    first = pa[...].astype(F32) + pb[...].astype(F32) + nb[2:3] + x_ref[...].astype(F32)
    normed, recip = standardize(first)
    normed_ref[...] = normed
    recip_ref[...] = jnp.broadcast_to(recip, recip_ref.shape)
    hb = (normed * nb[0:1] + nb[1:2]).astype(BF16)
    h_ref[...] = hb
    part[...] = feed(hb, up, down, a_ref, b_ref, act_ref).astype(BF16)


def ffn_second_kernel(hb, prev, up, down, a_ref, b_ref, act_ref, part):
    total = feed(hb[...], up, down, a_ref, b_ref, act_ref)
    part[...] = (total + prev[...].astype(F32)).astype(BF16)


def ffn_first(half_block, pa, pb, tokens, nb, up, down, tile=256):
    half, d = pa.shape
    hidden = down.shape[0]
    n = half // tile
    row = lambda w: pl.BlockSpec((tile, w), lambda i, *_: (i, 0))

    def kernel(info, *refs):
        ffn_first_kernel(*refs)

    return pl.pallas_call(
        kernel,
        grid_spec=pltpu.PrefetchScalarGridSpec(
            num_scalar_prefetch=1,
            grid=(n,),
            in_specs=[
                row(d),
                row(d),
                pl.BlockSpec((tile, d), lambda i, info: (info[0] * n + i, 0)),
                whole(nb.shape),
                whole(up.shape),
                whole(down.shape),
            ],
            out_specs=[row(d), row(128), row(d), row(hidden), row(hidden), row(hidden), row(d)],
        ),
        out_shape=[
            jax.ShapeDtypeStruct((half, d), F32),
            jax.ShapeDtypeStruct((half, 128), F32),
            jax.ShapeDtypeStruct((half, d), BF16),
            jax.ShapeDtypeStruct((half, hidden), BF16),
            jax.ShapeDtypeStruct((half, hidden), BF16),
            jax.ShapeDtypeStruct((half, hidden), BF16),
            jax.ShapeDtypeStruct((half, d), BF16),
        ],
        compiler_params=params(),
        cost_estimate=pl.CostEstimate(
            flops=6 * half * d * hidden, bytes_accessed=half * d * 14 + half * hidden * 6 + 6 * d * hidden,
            transcendentals=half * hidden * 2,
        ),
        name="ffn_first",
    )(half_block, pa, pb, tokens, nb, up, down)


def ffn_second(hb, prev, up, down, tile=256):
    half, d = hb.shape
    hidden = down.shape[0]
    row = lambda w: pl.BlockSpec((tile, w), lambda i: (i, 0))
    return pl.pallas_call(
        ffn_second_kernel,
        grid=(half // tile,),
        in_specs=[row(d), row(d), whole(up.shape), whole(down.shape)],
        out_specs=[row(hidden), row(hidden), row(hidden), row(d)],
        out_shape=[jax.ShapeDtypeStruct((half, hidden), BF16)] * 3 + [jax.ShapeDtypeStruct((half, d), BF16)],
        compiler_params=params(),
        cost_estimate=pl.CostEstimate(
            flops=6 * half * d * hidden, bytes_accessed=half * d * 6 + half * hidden * 6 + 6 * d * hidden,
            transcendentals=half * hidden * 2,
        ),
        name="ffn_second",
    )(hb, prev, up, down)


def ffn_bwd_kernel(info, pa, pb, normed_ref, cot, nb, up0, up1, down0, down1, a0, a1, b0, b1,
                   out_ref, d2_ref, d2b_ref, dgu0, dgu1, dh_ref, sums_ref):
    hidden = down0.shape[0]
    h = normed_ref[...] * nb[0:1] + nb[1:2]
    second = pa[...].astype(F32) + pb[...].astype(F32) + nb[5:6] + h
    normed, recip = standardize(second)
    gain = nb[3:4]
    out_ref[...] = (normed * gain + nb[4:5]).astype(BF16)
    c = cot[...].astype(F32)
    d2 = norm_grad(c, normed, recip, gain)
    d2_ref[...] = d2
    d2b = d2.astype(BF16)
    d2b_ref[...] = d2b
    sums = rows_of_sums([c * normed, c, d2])

    @pl.when(pl.program_id(0) == 0)
    def _():
        sums_ref[...] = sums

    @pl.when(pl.program_id(0) > 0)
    def _():
        sums_ref[...] += sums

    total = None
    step = 256
    for up, down, a_ref, b_ref, dgu in ((up0, down0, a0, b0, dgu0), (up1, down1, a1, b1, dgu1)):
        for at in range(0, hidden, step):
            cols = slice(at, at + step)
            dact = dot_nt(d2b, down[cols, :])
            dg = (dact * a_ref[:, cols].astype(F32)).astype(BF16)
            du = (dact * b_ref[:, cols].astype(F32)).astype(BF16)
            dgu[:, cols] = dg
            dgu[:, slice(hidden + at, hidden + at + step)] = du
            term = dot_nt(dg, up[0, :, cols]) + dot_nt(du, up[1, :, cols])
            total = term if total is None else total + term
    dh_ref[...] = total.astype(BF16)


def ffn_bwd(info, pa, pb, normed, cot, nb, up0, up1, down0, down1, a0, a1, b0, b1, tile=256):
    half, d = pa.shape
    hidden = down0.shape[0]
    n = half // tile
    row = lambda w: pl.BlockSpec((tile, w), lambda i, *_: (i, 0))
    return pl.pallas_call(
        ffn_bwd_kernel,
        grid_spec=pltpu.PrefetchScalarGridSpec(
            num_scalar_prefetch=1,
            grid=(n,),
            in_specs=[
                row(d), row(d), row(d),
                pl.BlockSpec((tile, d), lambda i, info: (info[0] * n + i, 0)),
                whole(nb.shape),
                whole(up0.shape), whole(up1.shape), whole(down0.shape), whole(down1.shape),
                row(hidden), row(hidden), row(hidden), row(hidden),
            ],
            out_specs=[row(d), row(d), row(d), row(2 * hidden), row(2 * hidden), row(d), whole((8, d))],
        ),
        out_shape=[
            jax.ShapeDtypeStruct((half, d), BF16),
            jax.ShapeDtypeStruct((half, d), F32),
            jax.ShapeDtypeStruct((half, d), BF16),
            jax.ShapeDtypeStruct((half, 2 * hidden), BF16),
            jax.ShapeDtypeStruct((half, 2 * hidden), BF16),
            jax.ShapeDtypeStruct((half, d), BF16),
            jax.ShapeDtypeStruct((8, d), F32),
        ],
        compiler_params=params(),
        cost_estimate=pl.CostEstimate(
            flops=12 * half * d * hidden, bytes_accessed=half * d * 20 + half * hidden * 16 + 12 * d * hidden,
            transcendentals=half,
        ),
        name="ffn_bwd",
    )(info, pa, pb, normed, cot, nb, up0, up1, down0, down1, a0, a1, b0, b1)


def attn_bwd_kernel(info, slopes, d2_ref, ha, hb, normed_ref, recip_ref, nb, wqkv0, wqkv1, wout0, wout1,
                    proj0, proj1, att0, att1, lse0, lse1,
                    d1_ref, d1b_ref, dproj0, dproj1, part, sums_ref, dist):
    step = pl.program_id(0)
    win = d2_ref.shape[0]
    width = wout0.shape[0]
    heads = width // HEAD_DIM

    @pl.when(step == 0)
    def _():
        fill_distance(dist)

    normed = normed_ref[...]
    dh = d2_ref[...] + (ha[...].astype(F32) + hb[...].astype(F32))
    d1 = norm_grad(dh, normed, recip_ref[:, 0:1], nb[0:1])
    d1_ref[...] = d1
    d1b = d1.astype(BF16)
    d1b_ref[...] = d1b
    sums = rows_of_sums([dh * normed, dh, d1])

    @pl.when(step == 0)
    def _():
        sums_ref[...] = sums

    @pl.when(step > 0)
    def _():
        sums_ref[...] += sums

    limit = info[1 + info[0] * pl.num_programs(0) + step]
    lanes = head_lanes(width)
    key_on = lax.broadcasted_iota(jnp.int32, (win, 1), 0) < limit
    stat_lane = lax.broadcasted_iota(jnp.int32, (1, 128), 1)
    total = None
    for g, (wqkv, wout, proj, att_ref, lse, dproj) in enumerate(
        ((wqkv0, wout0, proj0, att0, lse0, dproj0), (wqkv1, wout1, proj1, att1, lse1, dproj1))
    ):
        q, k, v = proj[0], proj[1], proj[2]
        datt = dot_nt(d1b, wout[...]).astype(BF16)
        product = datt.astype(F32) * att_ref[...].astype(F32)
        stat = jnp.zeros((win, 128), F32)
        for h in range(heads):
            inner = jnp.sum(jnp.where(lanes[h], product, 0.0), axis=1, keepdims=True)
            stat = jnp.where(stat_lane == h, inner, stat)
        inner_rows = stat.T[0:8]
        qs = q * jnp.asarray(SCALE, BF16)
        dq = jnp.zeros((win, width), F32)
        dk = jnp.zeros((win, width), F32)
        dv = jnp.zeros((win, width), F32)
        for h in range(heads):
            qh = jnp.where(lanes[h], qs, jnp.zeros_like(qs))
            oh = jnp.where(lanes[h], datt, jnp.zeros_like(datt))
            s = dot_nt(k, qh) - slopes[g * heads + h] * dist[...]
            s = jnp.where(key_on, s, NEG)
            p = jnp.exp(s - lse[0, h:h + 1, :])
            dp = dot_nt(v, oh)
            ds = (p * (dp - inner_rows[h:h + 1, :])).astype(BF16)
            dv = jnp.where(lanes[h], dot(p.astype(BF16), datt), dv)
            dk = jnp.where(lanes[h], dot(ds, q), dk)
            dq = jnp.where(lanes[h], dot_tn(ds, k), dq)
        dqb = (dq * SCALE).astype(BF16)
        dkb = (dk * SCALE).astype(BF16)
        dvb = dv.astype(BF16)
        dproj[0], dproj[1], dproj[2] = dqb, dkb, dvb
        term = dot_nt(dqb, wqkv[0]) + dot_nt(dkb, wqkv[1]) + dot_nt(dvb, wqkv[2])
        total = term if total is None else total + term
    part[...] = total.astype(BF16)


def attn_bwd(info, slopes, d2, ha, hb, normed, recip, nb, wqkv0, wqkv1, wout0, wout1,
             proj0, proj1, att0, att1, lse0, lse1):
    half, d = d2.shape
    width = wout0.shape[0]
    nwin, _, win = lse0.shape
    heads = 2 * width // HEAD_DIM
    row = lambda w: pl.BlockSpec((win, w), lambda i, *_: (i, 0))
    deep = pl.BlockSpec((3, win, width), lambda i, *_: (0, i, 0))
    stat = pl.BlockSpec((1, 8, win), lambda i, *_: (i, 0, 0))
    return pl.pallas_call(
        attn_bwd_kernel,
        grid_spec=pltpu.PrefetchScalarGridSpec(
            num_scalar_prefetch=2,
            grid=(nwin,),
            in_specs=[
                row(d), row(d), row(d), row(d), row(128), whole(nb.shape),
                whole(wqkv0.shape), whole(wqkv1.shape), whole(wout0.shape), whole(wout1.shape),
                deep, deep, row(width), row(width), stat, stat,
            ],
            out_specs=[row(d), row(d), deep, deep, row(d), whole((8, d))],
            scratch_shapes=[pltpu.VMEM((win, win), F32)],
        ),
        out_shape=[
            jax.ShapeDtypeStruct((half, d), F32),
            jax.ShapeDtypeStruct((half, d), BF16),
            jax.ShapeDtypeStruct((3, half, width), BF16),
            jax.ShapeDtypeStruct((3, half, width), BF16),
            jax.ShapeDtypeStruct((half, d), BF16),
            jax.ShapeDtypeStruct((8, d), F32),
        ],
        compiler_params=params(),
        cost_estimate=pl.CostEstimate(
            flops=2 * half * d * width * 8 + 10 * nwin * heads * win * win * 256,
            bytes_accessed=half * d * 20 + half * width * 32 + d * width * 16,
            transcendentals=nwin * heads * win * win,
        ),
        name="attn_bwd",
    )(info, slopes, d2, ha, hb, normed, recip, nb, wqkv0, wqkv1, wout0, wout1,
      proj0, proj1, att0, att1, lse0, lse1)


def place_kernel(order, mine, near, far, out):
    step = pl.program_id(0)

    @pl.when(step < 2)
    def _():
        out[...] = mine[...].astype(out.dtype)

    @pl.when(step == 2)
    def _():
        out[...] = near[...].astype(out.dtype)

    @pl.when(step == 3)
    def _():
        out[...] = far[...].astype(out.dtype)


def place(order, mine, near, far, dtype):
    quarter, d = near.shape
    return pl.pallas_call(
        place_kernel,
        grid_spec=pltpu.PrefetchScalarGridSpec(
            num_scalar_prefetch=1,
            grid=(4,),
            in_specs=[
                pl.BlockSpec((quarter, d), lambda i, o: (jnp.minimum(i, 1), 0)),
                whole((quarter, d)),
                whole((quarter, d)),
            ],
            out_specs=pl.BlockSpec((quarter, d), lambda i, o: (o[i], 0)),
        ),
        out_shape=jax.ShapeDtypeStruct((4 * quarter, d), dtype),
        compiler_params=params(),
        cost_estimate=pl.CostEstimate(flops=0, bytes_accessed=24 * quarter * d, transcendentals=0),
        name="place",
    )(order, mine, near, far)


SWAP = [(0, 1), (1, 0)]
WIDE = ("wo", "x")


def swap(value, axis):
    return lax.ppermute(value, axis, SWAP)


def shards(tokens, wqkv, wout, nb, up, down, lengths, cot):
    x_at, y_at, c_at = (lax.axis_index(name) for name in ("x", "y", "core"))
    group_heads = wqkv.shape[2] // HEAD_DIM
    own = 2 * y_at + c_at
    heads = jnp.concatenate([own * group_heads + jnp.arange(group_heads), (own ^ 2) * group_heads + jnp.arange(group_heads)])
    slopes = 2.0 ** (-8.0 * (heads + 1).astype(F32) / HEADS)
    info = jnp.concatenate([y_at[None].astype(jnp.int32), lengths])

    wqkv1 = swap(wqkv, "y")
    wout1 = swap(wout, "y")
    half_up = swap(lax.dynamic_index_in_dim(up, x_at, 0, keepdims=False), "y")
    other_up = swap(half_up, "x")
    up1 = jnp.stack([jnp.where(x_at == 0, half_up, other_up), jnp.where(x_at == 0, other_up, half_up)])
    rows = down.shape[0] // 2
    half_down = swap(lax.dynamic_slice_in_dim(down, x_at * rows, rows, 0), "y")
    other_down = swap(half_down, "x")
    down1 = jnp.concatenate(
        [jnp.where(x_at == 0, half_down, other_down), jnp.where(x_at == 0, other_down, half_down)], axis=0
    )

    proj0, att0, lse0, part0 = attn_fwd(info, slopes[:group_heads], tokens, wqkv, wout, None)
    proj1, att1, lse1, part = attn_fwd(info, slopes[group_heads:], tokens, wqkv1, wout1, part0)
    part_other = swap(part, "core")
    normed, recip, hb, a0, b0, act0, fpart0 = ffn_first(info, part, part_other, tokens, nb, up, down)
    a1, b1, act1, fpart = ffn_second(hb, fpart0, up1, down1)
    fpart_other = swap(fpart, "core")
    out, d2, d2b, dgu0, dgu1, dh, sums2 = ffn_bwd(
        info, fpart, fpart_other, normed, cot, nb, up, up1, down, down1, a0, a1, b0, b1
    )
    dh_other = swap(dh, "core")

    def grad(a, b):
        return lax.dot_general(a, b, (((0,), (0,)), ((), ())), preferred_element_type=F32)

    down_peer = swap(grad(d2b, act1).astype(BF16), "y")
    up_peer = swap(grad(hb, dgu1).astype(BF16), "y")
    down_all = (grad(d2b, act0) + down_peer.astype(F32)).astype(BF16)
    up_all = (grad(hb, dgu0) + up_peer.astype(F32)).astype(BF16)
    scatter = functools.partial(lax.psum_scatter, axis_name=WIDE, scatter_dimension=0, tiled=True)
    down_share = scatter(down_all).astype(F32).T
    up_share = scatter(up_all).astype(F32)
    hidden = down.shape[0]
    up_share = jnp.stack([up_share[:, :hidden], up_share[:, hidden:]])

    d1, d1b, dproj0, dproj1, ipart, sums1 = attn_bwd(
        info, slopes, d2, dh, dh_other, normed, recip, nb, wqkv, wqkv1, wout, wout1,
        proj0, proj1, att0, att1, lse0, lse1,
    )
    half = d1.shape[0]
    mine = lax.dynamic_slice_in_dim(tokens, y_at * half, half, 0)

    def attn_grads(dproj, att):
        pieces = [grad(mine, dproj[i]) for i in range(3)] + [grad(d1b, att)]
        return jnp.concatenate(pieces, axis=1)

    attn_peer = swap(attn_grads(dproj1, att1).astype(BF16), "y")
    attn_all = (attn_grads(dproj0, att0) + attn_peer.astype(F32)).astype(BF16)
    attn_share = scatter(attn_all).astype(F32)
    width = wqkv.shape[2]
    qkv_share = jnp.stack([attn_share[:, i * width:(i + 1) * width] for i in range(3)])
    out_share = attn_share[:, 3 * width:].T

    small = jnp.concatenate([sums1[:3], sums2[:3]], axis=0)
    small_share = lax.psum_scatter(lax.psum(small, "y"), WIDE, scatter_dimension=1, tiled=True)

    quarter = half // 2
    order = jnp.stack([2 * y_at, 2 * y_at + 1, 2 * (1 - y_at) + c_at, 2 * (1 - y_at) + 1 - c_at]).astype(jnp.int32)

    def share(value, dtype):
        near = swap(lax.dynamic_slice_in_dim(value, c_at * quarter, quarter, 0), "y")
        far = swap(near, "core")
        return place(order, value, near, far, dtype)

    block_out = share(out, BF16)
    ipart_other = swap(ipart, "core")
    total = (d1 + (ipart.astype(F32) + ipart_other.astype(F32))).astype(BF16)
    input_grad = share(total, F32)
    return (block_out, input_grad, qkv_share, out_share, up_share, down_share, small_share)


def solution(mesh):
    wide = mesh.shape["wide"]
    grid = Mesh(mesh.devices.reshape(wide // 2, 2, 2, 2), ("wo", "x", "y", "core"))
    narrow = ("y", "core")
    placed = (
        P(WIDE, None),
        P(None, None, narrow),
        P(narrow, None),
        P(),
        P(None, None, narrow),
        P(narrow, None),
        P(WIDE),
        P(WIDE, None),
    )
    return jax.shard_map(
        shards,
        mesh=grid,
        in_specs=placed,
        out_specs=(
            P(WIDE, None),
            P(WIDE, None),
            P(None, WIDE, narrow),
            P(narrow, WIDE),
            P(None, WIDE, narrow),
            P(narrow, WIDE),
            P(None, WIDE),
        ),
        check_vma=False,
    )
```

time: 1060 us -> 501 us (0.47)
  waiting for transfers between devices: 570 us -> 256 us
  matrix products: 271 us -> 34.7 us
  Pallas kernels: 0 us -> 136 us
  other arithmetic: 108 us -> 13.3 us
  local copies, waits for them, and re-layouts: 84.4 us -> 20.6 us
  starting transfers between devices: 1.69 us -> 16.8 us
    psum x4 -> x0, waiting for transfers between devices: 378 us -> none  [the longest x1 96.5 us: shards(): lax.psum(attn_part.astype(jnp.bfloat16), 'narrow').astype(jnp.float32)]
    dot_general x53 -> x12, matrix products: 265 us -> 34.7 us  [grad(): lax.dot_general(a, b, (((0,), (0,)), ((), ())), preferred_element_type=F32)]
    ppermute x0 -> x17, waiting for transfers between devices: none -> 167 us  [swap(): return lax.ppermute(value, axis, SWAP)]
    pallas_call x0 -> x8, Pallas kernels: none -> 136 us  [the longest x1 41.3 us: ffn_bwd(): pl.pallas_call(ffn_bwd_kernel, grid_spec=pltpu.PrefetchScalarGridSpec(num...]
    unnamed x13 -> x6, waiting for transfers between devices: 122 us -> 26.1 us
    reduce_sum x13 -> x0, other arithmetic: 49.8 us -> none  [the longest x2 15.8 us: norm_backward(): jnp.sum(grad_out * normed, axis=0)]
    convert_element_type x13 -> x4, other arithmetic: 24.7 us -> 5.74 us  [the longest x1 4.46 us: shards(): total = (d1 + (ipart.astype(F32) + ipart_other.astype(F32))).astype(BF16)]
    reshape x3 -> x0, local copies, waits for them, and re-layouts: 18.6 us -> none  [the longest x1 8.19 us: shards(): jnp.moveaxis(grad_blocks, 1, 0).reshape(3, token_count, group_width)]
  transfers between devices with their start and end apart: 9 -> 21, of which waited for: 7 -> 11; matrix products, arithmetic and copies ran while one was open for 24% -> 12% of each run, Pallas kernels for 0% -> 14%
where the time goes in v1:
time: 501 us; the launch traced here: 497 us
  waiting for transfers between devices  256 us (51%)
  Pallas kernels  136 us (27%)
  matrix products  34.7 us (7%)
  local copies, waits for them, and re-layouts  20.6 us (4%)
  starting transfers between devices  16.8 us (3%)
  between operations  14.5 us (3%)
  other arithmetic  13.3 us (3%)
  blocking collectives  5.52 us (1%)
    ppermute x17, waiting for transfers between devices, swap(): return lax.ppermute(value, axis, SWAP)  167 us
    reduce_scatter x1, waiting for transfers between devices, shards(): up_share = scatter(up_all).astype(F32)  62.1 us
    pallas_call x1, Pallas kernels, ffn_bwd(): pl.pallas_call(ffn_bwd_kernel, grid_spec=pltpu.PrefetchScalarGridSpec(num...  41.3 us
    dot_general x12, matrix products, grad(): lax.dot_general(a, b, (((0,), (0,)), ((), ())), preferred_element_type=F32)  34.7 us
    pallas_call x1, Pallas kernels, attn_bwd(): pl.pallas_call(attn_bwd_kernel, grid_spec=pltpu.PrefetchScalarGridSpec(nu...  30.2 us
    unnamed x6, waiting for transfers between devices  26.1 us
    pallas_call x2, Pallas kernels, attn_fwd(): pl.pallas_call(functools.partial(attn_fwd_kernel, last), grid_spec=pltpu....  25.3 us
    ppermute x17, starting transfers between devices, swap(): return lax.ppermute(value, axis, SWAP)  16.2 us
  transfers between devices with their start and end apart: 21, of which 11 were waited for; matrix products, arithmetic and copies ran while one was open for 12% of the time, Pallas kernels for 14%

profile of v1, /device:TPU:0, one launch (start us, length us, event | category | flops | bytes accessed | tf_op | source)
XLA Modules:
  0.0 497.4 jit_solution(16811666474310721668)
XLA Ops:
  16.5 12.4 %attn_fwd_first.1 = (bf16[3,1536,192]{2,1,0:T(8,128)(2,1)}, bf16[1536,192]{1,0:T(8,128)(2,1)}, f32[3,8,512]{2,1,0:T(8,128)}, bf16[1536,768]{1,0:T(8,128)(2,1)}) custom-call(s32[7]{0:T(128)} %pad_add_fusion.1.info, f32[3]{0:T(128)} %get-tuple-element.95.slopes, bf16[3072,768]{1,0:T(8,128)(2,1)} %refs_2_.1, bf16[3,768,192]{2,1,0:T(8,128)(2,1)} %copy.19.wqkv.wqkv0, ...), custom_call_target="tpu_custom_call" | custom-call | flops 4227858432 | bytes 8257536 | tf_op jit(solution)/shard_map/attn_fwd_first/pallas_call | solution.py:118
  28.9 8.5 %collective-permute-done = bf16[3,768,192]{1,2,0:T(8,128)(2,1)} collective-permute-done((bf16[3,768,192]{1,2,0:T(8,128)(2,1)}, bf16[3,768,192]{1,2,0:T(8,128)(2,1)}, u32[]{:S(2)}, u32[]{:S(2)}) %collective-permute-start) | collective-permute-done | bytes 884768 | tf_op jit(solution)/shard_map/ppermute | solution.py:488
  40.5 12.8 %attn_fwd_last.1 = (bf16[3,1536,192]{2,1,0:T(8,128)(2,1)}, bf16[1536,192]{1,0:T(8,128)(2,1)}, f32[3,8,512]{2,1,0:T(8,128)}, bf16[1536,768]{1,0:T(8,128)(2,1)}) custom-call(s32[7]{0:T(128)} %pad_add_fusion.1.info, f32[3]{0:T(128)} %get-tuple-element.96.slopes, bf16[3072,768]{1,0:T(8,128)(2,1)} %refs_2_.1, bf16[3,768,192]{2,1,0:T(8,128)(2,1)} %copy.20.wqkv.wqkv1, ...), custom_call_target="tpu_custom_call" | custom-call | flops 4227858432 | bytes 8257536 | tf_op jit(solution)/shard_map/attn_fwd_last/pallas_call | solution.py:118
  55.5 7.1 %collective-permute-done.3 = bf16[768,768]{1,0:T(8,128)(2,1)S(1)} collective-permute-done((bf16[768,768]{1,0:T(8,128)(2,1)S(1)}, bf16[768,768]{1,0:T(8,128)(2,1)S(1)}, u32[]{:S(2)}, u32[]{:S(2)}) %collective-permute-start.3) | collective-permute-done | bytes 1179680 | tf_op jit(solution)/shard_map/ppermute | solution.py:488
  64.6 9.8 %collective-permute-done.5 = bf16[384,768]{1,0:T(8,128)(2,1)S(1)} collective-permute-done((bf16[384,768]{1,0:T(8,128)(2,1)S(1)}, bf16[384,768]{1,0:T(8,128)(2,1)S(1)}, u32[]{:S(2)}, u32[]{:S(2)}) %collective-permute-start.5) | collective-permute-done | bytes 589856 | tf_op jit(solution)/shard_map/ppermute | solution.py:488
  76.1 25.4 %collective-permute-done.6 = bf16[384,768]{1,0:T(8,128)(2,1)S(1)} collective-permute-done((bf16[384,768]{1,0:T(8,128)(2,1)S(1)}, bf16[384,768]{1,0:T(8,128)(2,1)S(1)}, u32[]{:S(2)}, u32[]{:S(2)}) %collective-permute-start.6) | collective-permute-done | bytes 589856 | tf_op jit(solution)/shard_map/ppermute | solution.py:488
  104.5 15.8 %ffn_first.1 = (f32[1536,768]{1,0:T(8,128)}, f32[1536,128]{1,0:T(8,128)}, bf16[1536,768]{1,0:T(8,128)(2,1)}, bf16[1536,768]{1,0:T(8,128)(2,1)}, bf16[1536,768]{1...) custom-call(s32[7]{0:T(128)} %pad_add_fusion.1.info, ...), custom_call_target="tpu_custom_call" | custom-call | flops 5435817984 | bytes 27131904 | tf_op jit(solution)/shard_map/ffn_first/pallas_call | solution.py:210
  120.3 12.0 %ffn_second.1 = (bf16[1536,768]{1,0:T(8,128)(2,1)}, bf16[1536,768]{1,0:T(8,128)(2,1)}, bf16[1536,768]{1,0:T(8,128)(2,1)}, bf16[1536,768]{1,0:T(8,128)(2,1)}) custom-call(bf16[1536,768]{1,0:T(8,128)(2,1)} %get-tuple-element.41.hb, bf16[1536,768]{1,0:T(8,128)(2,1)} %get-tuple-element.42.prev, bf16[2,768,768]{2,1,0:T(8,128)(2,1)} %pad_maximum_fusion.up.up1, ...), custom_call_target="tpu_custom_call" | custom-call | flops 5435817984 | bytes 17694720 | tf_op jit(solution)/shard_map/ffn_second/pallas_call | solution.py:247
  132.4 4.7 collective-permute-done.7.pb
  138.5 41.3 %ffn_bwd.1 = (bf16[1536,768]{1,0:T(8,128)(2,1)}, f32[1536,768]{1,0:T(8,128)}, bf16[1536,768]{1,0:T(8,128)(2,1)}, bf16[1536,1536]{1,0:T(8,128)(2,1)}, bf16[1536,1...) custom-call(s32[7]{0:T(128)} %pad_add_fusion.1.info, bf16[1536,768]{1,0:T(8,128)(2,1)} %get-tuple-element.43.pa, ...), custom_call_target="tpu_custom_call" | custom-call | flops 10871635968 | bytes 49545216 | tf_op jit(solution)/shard_map/ffn_bwd/pallas_call | solution.py:305
  180.7 5.5 %convolution_convert_fusion.1 = bf16[768,768]{1,0:T(8,128)(2,1)} fusion(bf16[1536,768]{1,0:T(8,128)(2,1)} %get-tuple-element.66, bf16[1536,768]{1,0:T(8,128)(2,1)} %get-tuple-element.68), kind=kOutput, calls=%fused_computation.7 | convolution fusion | flops 1812529152 | bytes 5898240 | tf_op jit(solution)/shard_map/dot_general | solution.py:523
  189.1 30.2 %attn_bwd.1 = (f32[1536,768]{1,0:T(8,128)}, bf16[1536,768]{1,0:T(8,128)(2,1)}, bf16[3,1536,192]{2,1,0:T(8,128)(2,1)}, bf16[3,1536,192]{2,1,0:T(8,128)(2,1)}, bf1...) custom-call(s32[7]{0:T(128)} %pad_add_fusion.1.info, f32[6]{0:T(128)} %copy-done.6, f32[1536,768]{1,0:T(8,128)} %get-tuple-element.50.d2_ref, ...), custom_call_target="tpu_custom_call" | custom-call | flops 15703474176 | bytes 35389440 | tf_op jit(solution)/shard_map/attn_bwd/pallas_call | solution.py:414
  222.5 4.8 add_convert_fusion.2
  237.5 5.1 %convolution_convert_fusion = bf16[768,1536]{1,0:T(8,128)(2,1)} fusion(bf16[1536,768]{1,0:T(8,128)(2,1)S(1)} %copy-done.16, bf16[1536,1536]{1,0:T(8,128)(2,1)S(1)} %copy-done.17), kind=kOutput, calls=%fused_computation.2 | convolution fusion | flops 3625058304 | bytes 9437184 | tf_op jit(solution)/shard_map/dot_general | solution.py:523
  246.4 18.3 %collective-permute-done.14 = bf16[768,768]{0,1:T(8,128)(2,1)S(1)} collective-permute-done((bf16[768,768]{0,1:T(8,128)(2,1)S(1)}, bf16[768,768]{0,1:T(8,128)(2,1)S(1)}, u32[]{:S(2)}, u32[]{:S(2)}) %collective-permute-start.14) | collective-permute-done | bytes 1179680 | tf_op jit(solution)/shard_map/ppermute | solution.py:488
  266.9 47.6 %collective-permute-done.15 = bf16[768,1536]{1,0:T(8,128)(2,1)S(1)} collective-permute-done((bf16[768,1536]{1,0:T(8,128)(2,1)}, bf16[768,1536]{1,0:T(8,128)(2,1)S(1)}, u32[]{:S(2)}, u32[]{:S(2)}) %collective-permute-start.15) | collective-permute-done | bytes 2359328 | tf_op jit(solution)/shard_map/ppermute | solution.py:488
  314.5 8.4 %add_convert_fusion = bf16[768,1536]{1,0:T(8,128)(2,1)} fusion(bf16[768,1536]{1,0:T(8,128)(2,1)S(1)} %collective-permute-done.15, bf16[1536,768]{1,0:T(8,128)(2,1)} %get-tuple-element.41.hb, bf16[1536,1536]{1,0:T(8,128)(2,1)} %get-tuple-element.64), kind=kOutput, calls=%fused_computation | convolution fusion | flops 3627417600 | bytes 11796480 | tf_op jit(solution)/shard_map/dot_general | solution.py:523
  331.4 22.2 %collective-permute-done.8.near = bf16[768,768]{1,0:T(8,128)(2,1)S(1)} collective-permute-done((bf16[768,768]{1,0:T(8,128)(2,1)S(1)}, bf16[768,768]{1,0:T(8,128)(2,1)S(1)}, u32[]{:S(2)}, u32[]{:S(2)}) %collective-permute-start.8) | collective-permute-done | bytes 1179680 | tf_op jit(solution)/shard_map/ppermute | solution.py:488
  353.6 23.6 %collective-permute-done.12.near = bf16[768,768]{1,0:T(8,128)(2,1)} collective-permute-done((bf16[768,768]{1,0:T(8,128)(2,1)S(1)}, bf16[768,768]{1,0:T(8,128)(2,1)}, u32[]{:S(2)}, u32[]{:S(2)}) %collective-permute-start.12) | collective-permute-done | bytes 1179680 | tf_op jit(solution)/shard_map/ppermute | solution.py:488
  377.8 5.3 %place.2 = bf16[3072,768]{1,0:T(8,128)(2,1)} custom-call(s32[4]{0:T(128)} %pad_add_fusion.order, bf16[1536,768]{1,0:T(8,128)(2,1)} %get-tuple-element.49.mine, bf16[768,768]{1,0:T(8,128)(2,1)} %copy-done.3, bf16[768,768]{1,0:T(8,128)(2,1)} %collective-permute-done.9.far), custom_call_target="tpu_custom_call" | custom-call | bytes 14155776 | tf_op jit(solution)/shard_map/place/pallas_call | solution.py:464
  384.0 5.5 %psum.8 = f32[6,96]{1,0:T(8,128)} all-reduce(f32[6,96]{1,0:T(8,128)S(1)} %copy.27), channel_id=1, replica_groups=mesh['wo'=4,'x'=2,'y'=2,'core'=2] {'y'}, use_global_device_ids=true, to_apply=%region_3.4 | all-reduce | flops 576 | bytes 4608 | tf_op jit(solution)/shard_map/psum | solution.py:554
  391.1 26.1 %reduce-scatter.13.cloned.1.call-done = bf16[96,768]{1,0:T(8,128)(2,1)} async-done(((bf16[768,768]{1,0:T(8,128)(2,1)}), bf16[96,768]{1,0:T(8,128)(2,1)}) %reduce-scatter.13.cloned.1.call-update) | async-done | bytes 147472
  419.9 6.6 %place.3 = f32[3072,768]{1,0:T(8,128)} custom-call(s32[4]{0:T(128)} %pad_add_fusion.order, bf16[1536,768]{1,0:T(8,128)(2,1)} %copy-done, bf16[768,768]{1,0:T(8,128)(2,1)} %collective-permute-done.12.near, bf16[768,768]{1,0:T(8,128)(2,1)} %collective-permute-done.13.far), custom_call_target="tpu_custom_call" | custom-call | bytes 14155776 | tf_op jit(solution)/shard_map/place/pallas_call | solution.py:464
  426.4 62.1 %reduce-scatter.9.cloned.1.call-done = bf16[96,1536]{1,0:T(8,128)(2,1)} async-done(((bf16[768,1536]{1,0:T(8,128)(2,1)}), bf16[96,1536]{1,0:T(8,128)(2,1)}) %reduce-scatter.9.cloned.1.call-update) | async-done | bytes 294928 | tf_op jit(solution)/shard_map/reduce_scatter | solution.py:531
  (117 shorter events, 61.6 us)
Async XLA Ops:
  7.2 375.9 %reduce-scatter.15.cloned.1.call-start = ((), (), s32[]{:S(2)}) async-start(), calls=%async_computation.7 | async-start | bytes 442368
  7.2 32.5 %collective-permute-start.1 = (bf16[192,768]{1,0:T(8,128)(2,1)}, bf16[192,768]{1,0:T(8,128)(2,1)S(1)}, u32[]{:S(2)}, u32[]{:S(2)}) collective-permute-start(bf16[192,768]{1,0:T(8,128)(2,1)} %wout0.1), channel_id=1, source_target_pairs={{0,2},{2,0},{1,3},{3,1},{4,6},{6,4},{5,7},{7,5},{8,10},{10,8},{9,1... | collective-permute-start | bytes 884744 | tf_op jit(solution)/shard_map/ppermute | solution.py:488
  10.3 27.1 %collective-permute-start = (bf16[3,768,192]{1,2,0:T(8,128)(2,1)}, bf16[3,768,192]{1,2,0:T(8,128)(2,1)}, u32[]{:S(2)}, u32[]{:S(2)}) collective-permute-start(bf16[3,768,192]{1,2,0:T(8,128)(2,1)} %param.9), channel_id=1, source_target_pairs={{0,2},{2,0},{1,3},{3,1},{4,6},{6,4},{5,7},{7,5},{8,10},{10,8},{9,1... | collective-permute-start | bytes 2654216 | tf_op jit(solution)/shard_map/ppermute | solution.py:488
  11.7 50.9 %collective-permute-start.3 = (bf16[768,768]{1,0:T(8,128)(2,1)S(1)}, bf16[768,768]{1,0:T(8,128)(2,1)S(1)}, u32[]{:S(2)}, u32[]{:S(2)}) collective-permute-start(bf16[768,768]{1,0:T(8,128)(2,1)S(1)} %dynamic-slice_bitcast_fusion), channel_id=1, source_target_pairs={{0,2},{2,0},{1,3},{3,1},{4,6},{6,4},{5,7},{7,5},{8,10},{10,8},{9,1... | collective-permute-start | bytes 3538952 | tf_op jit(solution)/shard_map/ppermute | solution.py:488
  53.3 51.2 %collective-permute-start.2 = (bf16[1536,768]{1,0:T(8,128)(2,1)}, bf16[1536,768]{1,0:T(8,128)(2,1)}, u32[]{:S(2)}, u32[]{:S(2)}) collective-permute-start(bf16[1536,768]{1,0:T(8,128)(2,1)} %get-tuple-element.40.refs_0_), channel_id=1, source_target_pairs={{0,1},{1,0},{2,3},{3,2},{4,5},{5,4},{6,7},{7,6},{8,9},{9,8},{10,11... | collective-permute-start | bytes 7077896 | tf_op jit(solution)/shard_map/ppermute | solution.py:488
  53.4 21.0 %collective-permute-start.5 = (bf16[384,768]{1,0:T(8,128)(2,1)S(1)}, bf16[384,768]{1,0:T(8,128)(2,1)S(1)}, u32[]{:S(2)}, u32[]{:S(2)}) collective-permute-start(bf16[384,768]{1,0:T(8,128)(2,1)S(1)} %constant_dynamic-slice_fusion.2), channel_id=1, source_target_pairs={{0,2},{2,0},{1,3},{3,1},{4,6},{6,4},{5,7},{7,5},{8,10},{10,8},{9,1... | collective-permute-start | bytes 1769480 | tf_op jit(solution)/shard_map/ppermute | solution.py:488
  62.6 40.1 %collective-permute-start.4 = (bf16[768,768]{1,0:T(8,128)(2,1)S(1)}, bf16[768,768]{1,0:T(8,128)(2,1)S(1)}, u32[]{:S(2)}, u32[]{:S(2)}) collective-permute-start(bf16[768,768]{1,0:T(8,128)(2,1)S(1)} %collective-permute-done.3), channel_id=1, source_target_pairs={{0,4},{4,0},{1,5},{5,1},{2,6},{6,2},{3,7},{7,3},{8,12},{12,8},{9,1... | collective-permute-start | bytes 3538952 | tf_op jit(solution)/shard_map/ppermute | solution.py:488
  74.4 27.2 %collective-permute-start.6 = (bf16[384,768]{1,0:T(8,128)(2,1)S(1)}, bf16[384,768]{1,0:T(8,128)(2,1)S(1)}, u32[]{:S(2)}, u32[]{:S(2)}) collective-permute-start(bf16[384,768]{1,0:T(8,128)(2,1)S(1)} %collective-permute-done.5), channel_id=1, source_target_pairs={{0,4},{4,0},{1,5},{5,1},{2,6},{6,2},{3,7},{7,3},{8,12},{12,8},{9,1... | collective-permute-start | bytes 1769480 | tf_op jit(solution)/shard_map/ppermute | solution.py:488
  132.4 4.7 collective-permute-start.7
  179.8 7.9 %collective-permute-start.10 = (bf16[1536,768]{1,0:T(8,128)(2,1)}, bf16[1536,768]{1,0:T(8,128)(2,1)S(1)}, u32[]{:S(2)}, u32[]{:S(2)}) collective-permute-start(bf16[1536,768]{1,0:T(8,128)(2,1)} %get-tuple-element.51.ha), channel_id=1, source_target_pairs={{0,1},{1,0},{2,3},{3,2},{4,5},{5,4},{6,7},{7,6},{8,9},{9,8},{10,11... | collective-permute-start | bytes 7077896 | tf_op jit(solution)/shard_map/ppermute | solution.py:488
  186.2 36.2 %collective-permute-start.16 = (bf16[768,768]{1,0:T(8,128)(2,1)}, bf16[768,768]{1,0:T(8,128)(2,1)S(1)}, u32[]{:S(2)}, u32[]{:S(2)}) collective-permute-start(bf16[768,768]{1,0:T(8,128)(2,1)} %convolution_convert_fusion.1), channel_id=1, source_target_pairs={{0,2},{2,0},{1,3},{3,1},{4,6},{6,4},{5,7},{7,5},{8,10},{10,8},{9,1... | collective-permute-start | bytes 3538952 | tf_op jit(solution)/shard_map/ppermute | solution.py:488
  189.1 33.4 %copy-start.2 = (bf16[1536,768]{1,0:T(8,128)(2,1)S(1)}, bf16[1536,768]{1,0:T(8,128)(2,1)}, u32[]{:S(2)}) copy-start(bf16[1536,768]{1,0:T(8,128)(2,1)} %get-tuple-element.67) | copy-start | bytes 7077892
  222.4 167.1 %reduce-scatter.11.cloned.1.call-start = ((), (), s32[]{:S(2)}) async-start(), calls=%async_computation.5 | async-start | bytes 1327104 | tf_op jit(solution)/shard_map/reduce_scatter | solution.py:530
  227.2 190.0 %reduce-scatter.13.cloned.1.call-start = ((), (), s32[]{:S(2)}) async-start(), calls=%async_computation.6 | async-start | bytes 1327104
  235.9 28.9 %collective-permute-start.14 = (bf16[768,768]{0,1:T(8,128)(2,1)S(1)}, bf16[768,768]{0,1:T(8,128)(2,1)S(1)}, u32[]{:S(2)}, u32[]{:S(2)}) collective-permute-start(bf16[768,768]{0,1:T(8,128)(2,1)S(1)} %pad_maximum_fusion.2), channel_id=1, source_target_pairs={{0,2},{2,0},{1,3},{3,1},{4,6},{6,4},{5,7},{7,5},{8,10},{10,8},{9,1... | collective-permute-start | bytes 3538952 | tf_op jit(solution)/shard_map/ppermute | solution.py:488
  242.6 71.9 %collective-permute-start.15 = (bf16[768,1536]{1,0:T(8,128)(2,1)}, bf16[768,1536]{1,0:T(8,128)(2,1)S(1)}, u32[]{:S(2)}, u32[]{:S(2)}) collective-permute-start(bf16[768,1536]{1,0:T(8,128)(2,1)} %convolution_convert_fusion), channel_id=1, source_target_pairs={{0,2},{2,0},{1,3},{3,1},{4,6},{6,4},{5,7},{7,5},{8,10},{10,8},{9,1... | collective-permute-start | bytes 7077896 | tf_op jit(solution)/shard_map/ppermute | solution.py:488
  266.5 222.0 %reduce-scatter.9.cloned.1.call-start = ((), (), s32[]{:S(2)}) async-start(), calls=%async_computation.4 | async-start | bytes 2654208 | tf_op jit(solution)/shard_map/reduce_scatter | solution.py:531
  266.8 58.5 %collective-permute-start.11 = (bf16[1536,768]{1,0:T(8,128)(2,1)}, bf16[1536,768]{1,0:T(8,128)(2,1)}, u32[]{:S(2)}, u32[]{:S(2)}) collective-permute-start(bf16[1536,768]{1,0:T(8,128)(2,1)} %get-tuple-element.60), channel_id=1, source_target_pairs={{0,1},{1,0},{2,3},{3,2},{4,5},{5,4},{6,7},{7,6},{8,9},{9,8},{10,11... | collective-permute-start | bytes 7077896 | tf_op jit(solution)/shard_map/ppermute | solution.py:488
  324.6 29.0 %collective-permute-start.8 = (bf16[768,768]{1,0:T(8,128)(2,1)S(1)}, bf16[768,768]{1,0:T(8,128)(2,1)S(1)}, u32[]{:S(2)}, u32[]{:S(2)}) collective-permute-start(bf16[768,768]{1,0:T(8,128)(2,1)S(1)} %constant_dynamic-slice_fusion.1), channel_id=1, source_target_pairs={{0,2},{2,0},{1,3},{3,1},{4,6},{6,4},{5,7},{7,5},{8,10},{10,8},{9,1... | collective-permute-start | bytes 3538952 | tf_op jit(solution)/shard_map/ppermute | solution.py:488
  329.8 53.3 %copy-start = (bf16[1536,768]{1,0:T(8,128)(2,1)}, bf16[1536,768]{1,0:T(8,128)(2,1)S(1)}, u32[]{:S(2)}) copy-start(bf16[1536,768]{1,0:T(8,128)(2,1)S(1)} %add_convert_fusion.1.mine) | copy-start | bytes 7077892
  329.9 47.4 %collective-permute-start.12 = (bf16[768,768]{1,0:T(8,128)(2,1)S(1)}, bf16[768,768]{1,0:T(8,128)(2,1)}, u32[]{:S(2)}, u32[]{:S(2)}) collective-permute-start(bf16[768,768]{1,0:T(8,128)(2,1)S(1)} %constant_dynamic-slice_fusion), channel_id=1, source_target_pairs={{0,2},{2,0},{1,3},{3,1},{4,6},{6,4},{5,7},{7,5},{8,10},{10,8},{9,1... | collective-permute-start | bytes 3538952 | tf_op jit(solution)/shard_map/ppermute | solution.py:488
  353.6 24.2 %copy-start.3 = (bf16[768,768]{1,0:T(8,128)(2,1)}, bf16[768,768]{1,0:T(8,128)(2,1)S(1)}, u32[]{:S(2)}) copy-start(bf16[768,768]{1,0:T(8,128)(2,1)S(1)} %collective-permute-done.8.near) | copy-start | bytes 3538948
  353.6 24.2 %collective-permute-start.9 = (bf16[768,768]{1,0:T(8,128)(2,1)S(1)}, bf16[768,768]{1,0:T(8,128)(2,1)}, u32[]{:S(2)}, u32[]{:S(2)}) collective-permute-start(bf16[768,768]{1,0:T(8,128)(2,1)S(1)} %collective-permute-done.8.near), channel_id=1, source_target_pairs={{0,1},{1,0},{2,3},{3,2},{4,5},{5,4},{6,7},{7,6},{8,9},{9,8},{10,11... | collective-permute-start | bytes 3538952 | tf_op jit(solution)/shard_map/ppermute | solution.py:488
  377.3 42.6 %collective-permute-start.13 = (bf16[768,768]{1,0:T(8,128)(2,1)}, bf16[768,768]{1,0:T(8,128)(2,1)}, u32[]{:S(2)}, u32[]{:S(2)}) collective-permute-start(bf16[768,768]{1,0:T(8,128)(2,1)} %collective-permute-done.12.near), channel_id=1, source_target_pairs={{0,1},{1,0},{2,3},{3,2},{4,5},{5,4},{6,7},{7,6},{8,9},{9,8},{10,11... | collective-permute-start | bytes 3538952 | tf_op jit(solution)/shard_map/ppermute | solution.py:488
  (17 other events, 79.9 us)
Sparse Core Ops, SparseCore 0:
  222.5 61.6 reduce-scatter.14
  287.6 63.0 reduce-scatter.10
  354.1 63.0 reduce-scatter.12
  420.5 67.9 reduce-scatter.8

commit v2 on v1

--- a/solution.py
+++ b/solution.py
@@ -166,7 +166,6 @@
 def feed(hb, up, down, a_ref, b_ref, act_ref):
     hidden = down.shape[0]
     step = 256
-    total = None
     for at in range(0, hidden, step):
         cols = slice(at, at + step)
         gate = dot(hb, up[0, :, cols])
@@ -178,9 +177,7 @@
         a_ref[:, cols] = (lift * (cdf + gate * pdf)).astype(BF16)
         b_ref[:, cols] = gelu.astype(BF16)
         act_ref[:, cols] = act
-        term = dot(act, down[cols, :])
-        total = term if total is None else total + term
-    return total
+    return dot(act_ref[...], down[...])
 
 
 def ffn_first_kernel(pa, pb, x_ref, nb, up, down, normed_ref, recip_ref, h_ref, a_ref, b_ref, act_ref, part):
@@ -259,7 +256,7 @@
     )(hb, prev, up, down)
 
 
-def ffn_bwd_kernel(info, pa, pb, normed_ref, cot, nb, up0, up1, down0, down1, a0, a1, b0, b1,
+def ffn_bwd_kernel(info, pa, pb, normed_ref, cot, nb, up0, up1, down0, down1, a_all, b_all,
                    out_ref, d2_ref, d2b_ref, dgu0, dgu1, dh_ref, sums_ref):
     hidden = down0.shape[0]
     h = normed_ref[...] * nb[0:1] + nb[1:2]
@@ -284,20 +281,19 @@
 
     total = None
     step = 256
-    for up, down, a_ref, b_ref, dgu in ((up0, down0, a0, b0, dgu0), (up1, down1, a1, b1, dgu1)):
+    for g, (up, down, dgu) in enumerate(((up0, down0, dgu0), (up1, down1, dgu1))):
         for at in range(0, hidden, step):
             cols = slice(at, at + step)
             dact = dot_nt(d2b, down[cols, :])
-            dg = (dact * a_ref[:, cols].astype(F32)).astype(BF16)
-            du = (dact * b_ref[:, cols].astype(F32)).astype(BF16)
-            dgu[:, cols] = dg
-            dgu[:, slice(hidden + at, hidden + at + step)] = du
-            term = dot_nt(dg, up[0, :, cols]) + dot_nt(du, up[1, :, cols])
+            dgu[:, cols] = (dact * a_all[g, :, cols].astype(F32)).astype(BF16)
+            dgu[:, slice(hidden + at, hidden + at + step)] = (dact * b_all[g, :, cols].astype(F32)).astype(BF16)
+        for k in range(2):
+            term = dot_nt(dgu[:, k * hidden:(k + 1) * hidden], up[k])
             total = term if total is None else total + term
     dh_ref[...] = total.astype(BF16)
 
 
-def ffn_bwd(info, pa, pb, normed, cot, nb, up0, up1, down0, down1, a0, a1, b0, b1, tile=256):
+def ffn_bwd(info, pa, pb, normed, cot, nb, up0, up1, down0, down1, a_all, b_all, tile=256):
     half, d = pa.shape
     hidden = down0.shape[0]
     n = half // tile
@@ -312,7 +308,8 @@
                 pl.BlockSpec((tile, d), lambda i, info: (info[0] * n + i, 0)),
                 whole(nb.shape),
                 whole(up0.shape), whole(up1.shape), whole(down0.shape), whole(down1.shape),
-                row(hidden), row(hidden), row(hidden), row(hidden),
+                pl.BlockSpec((2, tile, hidden), lambda i, *_: (0, i, 0)),
+                pl.BlockSpec((2, tile, hidden), lambda i, *_: (0, i, 0)),
             ],
             out_specs=[row(d), row(d), row(d), row(2 * hidden), row(2 * hidden), row(d), whole((8, d))],
         ),
@@ -331,12 +328,12 @@
             transcendentals=half,
         ),
         name="ffn_bwd",
-    )(info, pa, pb, normed, cot, nb, up0, up1, down0, down1, a0, a1, b0, b1)
-
-
-def attn_bwd_kernel(info, slopes, d2_ref, ha, hb, normed_ref, recip_ref, nb, wqkv0, wqkv1, wout0, wout1,
-                    proj0, proj1, att0, att1, lse0, lse1,
-                    d1_ref, d1b_ref, dproj0, dproj1, part, sums_ref, dist):
+    )(info, pa, pb, normed, cot, nb, up0, up1, down0, down1, a_all, b_all)
+
+
+def attn_bwd_kernel(info, slopes, x_ref, d2_ref, ha, hb, normed_ref, recip_ref, nb, wqkv0, wqkv1, wout0, wout1,
+                    proj_all, att_all, lse_all,
+                    d1_ref, part, grad0, grad1, sums_ref, dist, sum0, sum1):
     step = pl.program_id(0)
     win = d2_ref.shape[0]
     width = wout0.shape[0]
@@ -351,7 +348,7 @@
     d1 = norm_grad(dh, normed, recip_ref[:, 0:1], nb[0:1])
     d1_ref[...] = d1
     d1b = d1.astype(BF16)
-    d1b_ref[...] = d1b
+    x = x_ref[...]
     sums = rows_of_sums([dh * normed, dh, d1])
 
     @pl.when(step == 0)
@@ -367,12 +364,10 @@
     key_on = lax.broadcasted_iota(jnp.int32, (win, 1), 0) < limit
     stat_lane = lax.broadcasted_iota(jnp.int32, (1, 128), 1)
     total = None
-    for g, (wqkv, wout, proj, att_ref, lse, dproj) in enumerate(
-        ((wqkv0, wout0, proj0, att0, lse0, dproj0), (wqkv1, wout1, proj1, att1, lse1, dproj1))
-    ):
-        q, k, v = proj[0], proj[1], proj[2]
+    for g, (wqkv, wout, acc) in enumerate(((wqkv0, wout0, sum0), (wqkv1, wout1, sum1))):
+        q, k, v = proj_all[g, 0], proj_all[g, 1], proj_all[g, 2]
         datt = dot_nt(d1b, wout[...]).astype(BF16)
-        product = datt.astype(F32) * att_ref[...].astype(F32)
+        product = datt.astype(F32) * att_all[g].astype(F32)
         stat = jnp.zeros((win, 128), F32)
         for h in range(heads):
             inner = jnp.sum(jnp.where(lanes[h], product, 0.0), axis=1, keepdims=True)
@@ -387,7 +382,7 @@
             oh = jnp.where(lanes[h], datt, jnp.zeros_like(datt))
             s = dot_nt(k, qh) - slopes[g * heads + h] * dist[...]
             s = jnp.where(key_on, s, NEG)
-            p = jnp.exp(s - lse[0, h:h + 1, :])
+            p = jnp.exp(s - lse_all[g, 0, h:h + 1, :])
             dp = dot_nt(v, oh)
             ds = (p * (dp - inner_rows[h:h + 1, :])).astype(BF16)
             dv = jnp.where(lanes[h], dot(p.astype(BF16), datt), dv)
@@ -396,51 +391,68 @@
         dqb = (dq * SCALE).astype(BF16)
         dkb = (dk * SCALE).astype(BF16)
         dvb = dv.astype(BF16)
-        dproj[0], dproj[1], dproj[2] = dqb, dkb, dvb
+        terms = [dot_tn(x, dqb), dot_tn(x, dkb), dot_tn(x, dvb), dot_tn(d1b, att_all[g])]
+
+        @pl.when(step == 0)
+        def _():
+            for i in range(4):
+                acc[i] = terms[i]
+
+        @pl.when(step > 0)
+        def _():
+            for i in range(4):
+                acc[i] += terms[i]
+
         term = dot_nt(dqb, wqkv[0]) + dot_nt(dkb, wqkv[1]) + dot_nt(dvb, wqkv[2])
         total = term if total is None else total + term
     part[...] = total.astype(BF16)
 
-
-def attn_bwd(info, slopes, d2, ha, hb, normed, recip, nb, wqkv0, wqkv1, wout0, wout1,
-             proj0, proj1, att0, att1, lse0, lse1):
+    @pl.when(step == pl.num_programs(0) - 1)
+    def _():
+        for acc, grad in ((sum0, grad0), (sum1, grad1)):
+            for i in range(4):
+                grad[:, i * width:(i + 1) * width] = acc[i].astype(BF16)
+
+
+def attn_bwd(info, slopes, tokens, d2, ha, hb, normed, recip, nb, wqkv0, wqkv1, wout0, wout1,
+             proj, att, lse):
     half, d = d2.shape
     width = wout0.shape[0]
-    nwin, _, win = lse0.shape
+    _, nwin, _, win = lse.shape
     heads = 2 * width // HEAD_DIM
     row = lambda w: pl.BlockSpec((win, w), lambda i, *_: (i, 0))
-    deep = pl.BlockSpec((3, win, width), lambda i, *_: (0, i, 0))
-    stat = pl.BlockSpec((1, 8, win), lambda i, *_: (i, 0, 0))
     return pl.pallas_call(
         attn_bwd_kernel,
         grid_spec=pltpu.PrefetchScalarGridSpec(
             num_scalar_prefetch=2,
             grid=(nwin,),
             in_specs=[
+                pl.BlockSpec((win, d), lambda i, info, sl: (info[0] * nwin + i, 0)),
                 row(d), row(d), row(d), row(d), row(128), whole(nb.shape),
                 whole(wqkv0.shape), whole(wqkv1.shape), whole(wout0.shape), whole(wout1.shape),
-                deep, deep, row(width), row(width), stat, stat,
+                pl.BlockSpec((2, 3, win, width), lambda i, *_: (0, 0, i, 0)),
+                pl.BlockSpec((2, win, width), lambda i, *_: (0, i, 0)),
+                pl.BlockSpec((2, 1, 8, win), lambda i, *_: (0, i, 0, 0)),
             ],
-            out_specs=[row(d), row(d), deep, deep, row(d), whole((8, d))],
-            scratch_shapes=[pltpu.VMEM((win, win), F32)],
+            out_specs=[row(d), row(d), whole((d, 4 * width)), whole((d, 4 * width)), whole((8, d))],
+            scratch_shapes=[pltpu.VMEM((win, win), F32), pltpu.VMEM((4, d, width), F32), pltpu.VMEM((4, d, width), F32)],
         ),
         out_shape=[
             jax.ShapeDtypeStruct((half, d), F32),
             jax.ShapeDtypeStruct((half, d), BF16),
-            jax.ShapeDtypeStruct((3, half, width), BF16),
-            jax.ShapeDtypeStruct((3, half, width), BF16),
-            jax.ShapeDtypeStruct((half, d), BF16),
+            jax.ShapeDtypeStruct((d, 4 * width), BF16),
+            jax.ShapeDtypeStruct((d, 4 * width), BF16),
             jax.ShapeDtypeStruct((8, d), F32),
         ],
         compiler_params=params(),
         cost_estimate=pl.CostEstimate(
-            flops=2 * half * d * width * 8 + 10 * nwin * heads * win * win * 256,
+            flops=2 * half * d * width * 16 + 10 * nwin * heads * win * win * 256,
             bytes_accessed=half * d * 20 + half * width * 32 + d * width * 16,
             transcendentals=nwin * heads * win * win,
         ),
         name="attn_bwd",
-    )(info, slopes, d2, ha, hb, normed, recip, nb, wqkv0, wqkv1, wout0, wout1,
-      proj0, proj1, att0, att1, lse0, lse1)
+    )(info, slopes, tokens, d2, ha, hb, normed, recip, nb, wqkv0, wqkv1, wout0, wout1,
+      proj, att, lse)
 
 
 def place_kernel(order, mine, near, far, out):
@@ -480,6 +492,335 @@
     )(order, mine, near, far)
 
 
+MESH_ID = pl.DeviceIdType.MESH
+TILE = 256
+
+
+def remote(src, dst, send, recv, axis, peer):
+    return pltpu.make_async_remote_copy(src, dst, send, recv, device_id={axis: peer}, device_id_type=MESH_ID)
+
+
+def forward_kernel(info, slopes, nb, tokens, wqkv, wout, up, down,
+                   proj_out, att_out, lse_out, normed_out, recip_out, h_out, a_out, b_out, act_out, fown_out, frecv_out,
+                   wqkv1_out, wout1_out, up1_out, down1_out,
+                   xbuf, wqv, wov, upv, downv, projb, attb, lseb, pown, precv, normedb, recipb, hbuf, ab, bb, actb,
+                   facc, fown, frecv, dist,
+                   load_sem, ysend, yrecv, xsend, xrecv, psend, prem, fsend, frem, out_sem, pout_sem, tout_sem, fout_sem):
+    x_at, y_at, c_at = (lax.axis_index(n) for n in ("x", "y", "core"))
+    nwin, _, win = lse_out.shape[1:]
+    half, d = xbuf.shape
+    width = wout.shape[0]
+    hidden = down.shape[0]
+    heads = width // HEAD_DIM
+    tiles = half // TILE
+
+    barrier = pltpu.get_barrier_semaphore()
+    for axis, at in (("x", x_at), ("y", y_at), ("core", c_at)):
+        pl.semaphore_signal(barrier, inc=1, device_id={axis: 1 - at}, device_id_type=MESH_ID)
+    pl.semaphore_wait(barrier, 3)
+
+    hd, hw, hf = d // 2, width // 2, hidden // 2
+
+    def pieces(at):
+        rows = pl.ds(at * hd, hd)
+        return (
+            (wqkv.at[0:2, rows], wqv.at[1, 0:2, rows]),
+            (wqkv.at[2:3, rows], wqv.at[1, 2:3, rows]),
+            (wout.at[pl.ds(at * hw, hw)], wov.at[1, pl.ds(at * hw, hw)]),
+            (up.at[at, 0:hd], upv.at[1, at, 0:hd]),
+            (up.at[at, hd:d], upv.at[1, at, hd:d]),
+            (down.at[pl.ds(at * hf, hf)], downv.at[1, pl.ds(at * hf, hf)]),
+        )
+
+    mine = pieces(x_at)
+    theirs = pieces(1 - x_at)
+
+    def over_y(i):
+        return remote(mine[i][0], mine[i][1], ysend.at[i], yrecv.at[i], "y", 1 - y_at)
+
+    def over_x(i):
+        return remote(mine[i][1], mine[i][1], xsend.at[i], xrecv.at[i], "x", 1 - x_at)
+
+    def arriving_x(i):
+        return remote(theirs[i][1], theirs[i][1], xsend.at[i], xrecv.at[i], "x", 1 - x_at)
+
+    def pass_on(i):
+        over_y(i).wait_recv()
+        over_x(i).start()
+
+    loads = [
+        pltpu.make_async_copy(tokens.at[pl.ds(y_at * half, half)], xbuf, load_sem.at[0]),
+        pltpu.make_async_copy(wqkv, wqv.at[0], load_sem.at[1]),
+        pltpu.make_async_copy(wout, wov.at[0], load_sem.at[2]),
+        pltpu.make_async_copy(up, upv.at[0], load_sem.at[3]),
+        pltpu.make_async_copy(down, downv.at[0], load_sem.at[4]),
+    ]
+    for i in range(6):
+        over_y(i).start()
+    for load in loads:
+        load.start()
+    fill_distance(dist)
+    lanes = head_lanes(width)
+    stat_lane = lax.broadcasted_iota(jnp.int32, (1, 128), 1)
+    key_at = lax.broadcasted_iota(jnp.int32, (1, win), 1)
+    for load in loads[:3]:
+        load.wait()
+
+    def part_copy(w):
+        rows = pl.ds(w * win, win)
+        return remote(pown.at[rows], precv.at[rows], psend.at[w], prem.at[w], "core", 1 - c_at)
+
+    def proj_copy(t):
+        g, rows = t // nwin, pl.ds((t % nwin) * win, win)
+        return (
+            pltpu.make_async_copy(projb.at[g, :, rows], proj_out.at[g, :, rows], pout_sem.at[0, t]),
+            pltpu.make_async_copy(attb.at[g, rows], att_out.at[g, rows], pout_sem.at[1, t]),
+        )
+
+    def attention(t, carry):
+        g, w = t // nwin, t % nwin
+        start = w * win
+        x = xbuf[pl.ds(start, win)]
+        q = dot(x, wqv[g, 0]).astype(BF16)
+        k = dot(x, wqv[g, 1]).astype(BF16)
+        v = dot(x, wqv[g, 2]).astype(BF16)
+        projb[g, 0, pl.ds(start, win)] = q
+        projb[g, 1, pl.ds(start, win)] = k
+        projb[g, 2, pl.ds(start, win)] = v
+        key_on = key_at < info[y_at * nwin + w]
+        rows = win // 2
+        for b in range(2):
+            at = slice(b * rows, (b + 1) * rows)
+            qb = q[at] * jnp.asarray(SCALE, BF16)
+            att = jnp.zeros((rows, width), F32)
+            stat = jnp.zeros((rows, 128), F32)
+            for h in range(heads):
+                qh = jnp.where(lanes[h], qb, jnp.zeros_like(qb))
+                s = dot_nt(qh, k) - slopes[g * heads + h] * dist[at]
+                s = jnp.where(key_on, s, NEG)
+                top = jnp.max(s, axis=1, keepdims=True)
+                p = jnp.exp(s - top)
+                total = jnp.sum(p, axis=1, keepdims=True)
+                o = dot(p.astype(BF16), v) * (1.0 / total)
+                att = jnp.where(lanes[h], o, att)
+                stat = jnp.where(stat_lane == h, top + jnp.log(total), stat)
+            attb[g, pl.ds(start + b * rows, rows)] = att.astype(BF16)
+            lseb[g, w, :, at] = stat.T[0:8]
+        for copy in proj_copy(t):
+            copy.start()
+
+        @pl.when(t >= nwin)
+        def _():
+            out = dot(attb[0, pl.ds(start, win)], wov[0]) + dot(attb[1, pl.ds(start, win)], wov[1])
+            pown[pl.ds(start, win)] = out.astype(BF16)
+            part_copy(w).start()
+
+        @pl.when(t == nwin - 2)
+        def _():
+            pass_on(0)
+
+        @pl.when(t == nwin - 1)
+        def _():
+            pass_on(1)
+            pass_on(2)
+            for i in range(3):
+                arriving_x(i).wait_recv()
+
+        @pl.when(t == 2 * nwin - 2)
+        def _():
+            pass_on(3)
+
+        return carry
+
+    lax.fori_loop(0, 2 * nwin, attention, 0)
+    lse_copy = pltpu.make_async_copy(lseb, lse_out, out_sem.at[0])
+    lse_copy.start()
+    loads[3].wait()
+    loads[4].wait()
+    step = 256
+
+    def hidden_units(g, start, hb):
+        for at in range(0, hidden, step):
+            cols = slice(at, at + step)
+            gate = dot(hb, upv[g, 0, :, cols])
+            lift = dot(hb, upv[g, 1, :, cols])
+            cdf = 0.5 * (1.0 + lax.erf(gate * (1.0 / math.sqrt(2.0))))
+            pdf = jnp.exp(-0.5 * gate * gate) * (1.0 / math.sqrt(2.0 * math.pi))
+            gelu = gate * cdf
+            rows = pl.ds(start, TILE)
+            ab[g, rows, cols] = (lift * (cdf + gate * pdf)).astype(BF16)
+            bb[g, rows, cols] = gelu.astype(BF16)
+            actb[g, rows, cols] = (gelu * lift).astype(BF16)
+
+    def tile_copies(t):
+        g, rows = t // tiles, pl.ds((t % tiles) * TILE, TILE)
+        return [
+            pltpu.make_async_copy(b.at[g, rows], o.at[g, rows], tout_sem.at[i, t])
+            for i, (b, o) in enumerate(((ab, a_out), (bb, b_out), (actb, act_out)))
+        ]
+
+    def norm_copies(i):
+        rows = pl.ds(i * TILE, TILE)
+        return [
+            pltpu.make_async_copy(b.at[rows], o.at[rows], fout_sem.at[n, i])
+            for n, (b, o) in enumerate(((normedb, normed_out), (recipb, recip_out), (hbuf, h_out)))
+        ]
+
+    def first(i, carry):
+        start = i * TILE
+
+        @pl.when(i % (win // TILE) == 0)
+        def _():
+            part_copy(i // (win // TILE)).wait_recv()
+
+        rows = pl.ds(start, TILE)
+        value = (pown[rows].astype(F32) + precv[rows].astype(F32)) + nb[2:3] + xbuf[rows].astype(F32)
+        normed, recip = standardize(value)
+        normedb[rows] = normed
+        recipb[rows] = jnp.broadcast_to(recip, (TILE, 128))
+        hb = (normed * nb[0:1] + nb[1:2]).astype(BF16)
+        hbuf[rows] = hb
+        hidden_units(0, start, hb)
+        facc[rows] = dot(actb[0, rows], downv[0])
+        for copy in tile_copies(i) + norm_copies(i):
+            copy.start()
+
+        @pl.when(i == 1)
+        def _():
+            pass_on(4)
+
+        @pl.when(i == tiles - 1)
+        def _():
+            pass_on(5)
+
+        return carry
+
+    lax.fori_loop(0, tiles, first, 0)
+    arriving_x(3).wait_recv()
+    arriving_x(4).wait_recv()
+
+    def second(i, carry):
+        start = i * TILE
+        hidden_units(1, start, hbuf[pl.ds(start, TILE)])
+        for copy in tile_copies(tiles + i):
+            copy.start()
+        return carry
+
+    lax.fori_loop(0, tiles, second, 0)
+    arriving_x(5).wait_recv()
+
+    def final_copy(i):
+        rows = pl.ds(i * TILE, TILE)
+        return (
+            remote(fown.at[rows], frecv.at[rows], fsend.at[i], frem.at[i], "core", 1 - c_at),
+            pltpu.make_async_copy(fown.at[rows], fown_out.at[rows], fout_sem.at[3, i]),
+        )
+
+    def third(i, carry):
+        rows = pl.ds(i * TILE, TILE)
+        fown[rows] = (facc[rows] + dot(actb[1, rows], downv[1])).astype(BF16)
+        for copy in final_copy(i):
+            copy.start()
+        return carry
+
+    weights_out = [
+        pltpu.make_async_copy(wqv.at[1], wqkv1_out, out_sem.at[1]),
+        pltpu.make_async_copy(wov.at[1], wout1_out, out_sem.at[2]),
+        pltpu.make_async_copy(upv.at[1], up1_out, out_sem.at[3]),
+        pltpu.make_async_copy(downv.at[1], down1_out, out_sem.at[4]),
+    ]
+    for copy in weights_out:
+        copy.start()
+    lax.fori_loop(0, tiles, third, 0)
+
+    def finish(i, carry):
+        sent, kept = final_copy(i)
+        sent.wait_recv()
+        back = pltpu.make_async_copy(frecv.at[pl.ds(i * TILE, TILE)], frecv_out.at[pl.ds(i * TILE, TILE)], fout_sem.at[4, i])
+        back.start()
+        sent.wait_send()
+        kept.wait()
+        for copy in norm_copies(i):
+            copy.wait()
+        return carry
+
+    lax.fori_loop(0, tiles, finish, 0)
+
+    def drain(i, carry):
+        pltpu.make_async_copy(
+            frecv.at[pl.ds(i * TILE, TILE)], frecv_out.at[pl.ds(i * TILE, TILE)], fout_sem.at[4, i]
+        ).wait()
+        return carry
+
+    lax.fori_loop(0, tiles, drain, 0)
+
+    def drain_tiles(t, carry):
+        for copy in tile_copies(t):
+            copy.wait()
+        return carry
+
+    lax.fori_loop(0, 2 * tiles, drain_tiles, 0)
+
+    def drain_proj(t, carry):
+        for copy in proj_copy(t):
+            copy.wait()
+        return carry
+
+    lax.fori_loop(0, 2 * nwin, drain_proj, 0)
+
+    def drain_part(w, carry):
+        part_copy(w).wait_send()
+        return carry
+
+    lax.fori_loop(0, nwin, drain_part, 0)
+    lse_copy.wait()
+    for copy in weights_out:
+        copy.wait()
+    for i in range(6):
+        over_y(i).wait_send()
+        over_x(i).wait_send()
+
+
+def forward(lengths, slopes, nb, tokens, wqkv, wout, up, down):
+    d = tokens.shape[1]
+    nwin = lengths.shape[0] // 2
+    half = tokens.shape[0] // 2
+    win = half // nwin
+    width, hidden = wout.shape[0], down.shape[0]
+    tiles = half // TILE
+    heads = width // HEAD_DIM
+    smem = pl.BlockSpec(memory_space=pltpu.SMEM)
+    vmem = pl.BlockSpec(memory_space=pltpu.VMEM)
+    hbm = pl.BlockSpec(memory_space=pl.ANY)
+    acts = [((2, half, hidden), BF16)] * 3
+    outs = [
+        ((2, 3, half, width), BF16), ((2, half, width), BF16), ((2, nwin, 8, win), F32),
+        ((half, d), F32), ((half, 128), F32), ((half, d), BF16), *acts,
+        ((half, d), BF16), ((half, d), BF16),
+        (wqkv.shape, BF16), (wout.shape, BF16), (up.shape, BF16), (down.shape, BF16),
+    ]
+    bufs = [
+        ((half, d), BF16), ((2,) + wqkv.shape, BF16), ((2,) + wout.shape, BF16), ((2,) + up.shape, BF16),
+        ((2,) + down.shape, BF16), ((2, 3, half, width), BF16), ((2, half, width), BF16), ((2, nwin, 8, win), F32),
+        ((half, d), BF16), ((half, d), BF16), ((half, d), F32), ((half, 128), F32), ((half, d), BF16), *acts,
+        ((half, d), F32), ((half, d), BF16), ((half, d), BF16), ((win, win), F32),
+    ]
+    sems = [(5,), (6,), (6,), (6,), (6,), (nwin,), (nwin,), (tiles,), (tiles,), (5,), (2, 2 * nwin), (3, 2 * tiles), (5, tiles)]
+    return pl.pallas_call(
+        forward_kernel,
+        in_specs=[smem, smem, vmem] + [hbm] * 5,
+        out_specs=[hbm] * len(outs),
+        out_shape=[jax.ShapeDtypeStruct(*o) for o in outs],
+        scratch_shapes=[pltpu.VMEM(*b) for b in bufs] + [pltpu.SemaphoreType.DMA(n) for n in sems],
+        compiler_params=pltpu.CompilerParams(vmem_limit_bytes=62 * 1024 * 1024, collective_id=0, has_side_effects=True),
+        cost_estimate=pl.CostEstimate(
+            flops=2 * half * d * width * 16 + 12 * half * d * hidden + 8 * nwin * heads * win * win * 256,
+            bytes_accessed=half * d * 30 + half * hidden * 12, transcendentals=half * hidden * 4,
+        ),
+        name="forward",
+    )(lengths, slopes, nb, tokens, wqkv, wout, up, down)
+
+
 SWAP = [(0, 1), (1, 0)]
 WIDE = ("wo", "x")
 
@@ -488,64 +829,80 @@
     return lax.ppermute(value, axis, SWAP)
 
 
+def after(value, *others):
+    return lax.optimization_barrier((value, *others))[0]
+
+
 def shards(tokens, wqkv, wout, nb, up, down, lengths, cot):
     x_at, y_at, c_at = (lax.axis_index(name) for name in ("x", "y", "core"))
+    d = tokens.shape[1]
     group_heads = wqkv.shape[2] // HEAD_DIM
     own = 2 * y_at + c_at
     heads = jnp.concatenate([own * group_heads + jnp.arange(group_heads), (own ^ 2) * group_heads + jnp.arange(group_heads)])
     slopes = 2.0 ** (-8.0 * (heads + 1).astype(F32) / HEADS)
     info = jnp.concatenate([y_at[None].astype(jnp.int32), lengths])
 
-    wqkv1 = swap(wqkv, "y")
-    wout1 = swap(wout, "y")
-    half_up = swap(lax.dynamic_index_in_dim(up, x_at, 0, keepdims=False), "y")
-    other_up = swap(half_up, "x")
-    up1 = jnp.stack([jnp.where(x_at == 0, half_up, other_up), jnp.where(x_at == 0, other_up, half_up)])
-    rows = down.shape[0] // 2
-    half_down = swap(lax.dynamic_slice_in_dim(down, x_at * rows, rows, 0), "y")
-    other_down = swap(half_down, "x")
-    down1 = jnp.concatenate(
-        [jnp.where(x_at == 0, half_down, other_down), jnp.where(x_at == 0, other_down, half_down)], axis=0
-    )
-
-    proj0, att0, lse0, part0 = attn_fwd(info, slopes[:group_heads], tokens, wqkv, wout, None)
-    proj1, att1, lse1, part = attn_fwd(info, slopes[group_heads:], tokens, wqkv1, wout1, part0)
-    part_other = swap(part, "core")
-    normed, recip, hb, a0, b0, act0, fpart0 = ffn_first(info, part, part_other, tokens, nb, up, down)
-    a1, b1, act1, fpart = ffn_second(hb, fpart0, up1, down1)
-    fpart_other = swap(fpart, "core")
+    (proj, att, lse, normed, recip, hb, a_all, b_all, act, fpart, fpart_other,
+     wqkv1, wout1, up1, down1) = forward(lengths, slopes, nb, tokens, wqkv, wout, up, down)
+    act0, act1 = act[0], act[1]
     out, d2, d2b, dgu0, dgu1, dh, sums2 = ffn_bwd(
-        info, fpart, fpart_other, normed, cot, nb, up, up1, down, down1, a0, a1, b0, b1
+        info, fpart, fpart_other, normed, cot, nb, up, up1, down, down1, a_all, b_all
     )
     dh_other = swap(dh, "core")
 
     def grad(a, b):
-        return lax.dot_general(a, b, (((0,), (0,)), ((), ())), preferred_element_type=F32)
-
-    down_peer = swap(grad(d2b, act1).astype(BF16), "y")
-    up_peer = swap(grad(hb, dgu1).astype(BF16), "y")
-    down_all = (grad(d2b, act0) + down_peer.astype(F32)).astype(BF16)
-    up_all = (grad(hb, dgu0) + up_peer.astype(F32)).astype(BF16)
-    scatter = functools.partial(lax.psum_scatter, axis_name=WIDE, scatter_dimension=0, tiled=True)
-    down_share = scatter(down_all).astype(F32).T
-    up_share = scatter(up_all).astype(F32)
+        return lax.dot_general(a, b, (((0,), (0,)), ((), ())), preferred_element_type=F32).astype(BF16)
+
+    wo = lax.axis_size("wo")
+
+    def part_of(value, at):
+        split = value.reshape(wo, 2, -1, value.shape[1])
+        return lax.dynamic_index_in_dim(split, at, 1, keepdims=False).reshape(-1, value.shape[1])
+
+    def add(a, b):
+        return a.astype(F32) + b.astype(F32)
+
+    down_peer = grad(d2b, act1)
+    down_peer_in = swap(down_peer, "y")
+    up_peer = grad(hb, dgu1)
+    up_own = grad(hb, dgu0)
+    up_in = swap(jnp.concatenate([part_of(up_own, 1 - x_at), part_of(up_peer, 1 - x_at)], axis=0), "x")
+    down_own = grad(d2b, act0)
+
+    quarter = out.shape[0] // 2
+    order = jnp.stack([2 * y_at, 2 * y_at + 1, 2 * (1 - y_at) + c_at, 2 * (1 - y_at) + 1 - c_at]).astype(jnp.int32)
+
+    def mine(value):
+        return lax.dynamic_slice_in_dim(value, c_at * quarter, quarter, 0)
+
+    d2 = after(d2, down_own)
+    d1, ipart, agrad0, agrad1, sums1 = attn_bwd(
+        info, slopes, tokens, d2, dh, dh_other, normed, recip, nb, wqkv, wqkv1, wout, wout1,
+        proj, att, lse,
+    )
+    ipart_other = swap(ipart, "core")
+    near_out = swap(mine(out), "y")
+
+    attn_in = swap(jnp.concatenate([part_of(agrad0, 1 - x_at), part_of(agrad1, 1 - x_at)], axis=0), "x")
+
+    total = (d1 + add(ipart, ipart_other)).astype(BF16)
+    near_in = swap(mine(total), "y")
+
+    down_all = add(down_own, down_peer_in).astype(BF16)
+    down_in = swap(part_of(down_all, 1 - x_at), "x")
+    down_half = add(part_of(down_all, x_at), down_in).astype(BF16)
+    n = d // 2
+    up_peer_half = add(part_of(up_peer, x_at), up_in[n:]).astype(BF16)
+    up_half = add(add(part_of(up_own, x_at), up_in[:n]), swap(up_peer_half, "y")).astype(BF16)
+    attn_peer_half = add(part_of(agrad1, x_at), attn_in[n:]).astype(BF16)
+    attn_half = add(add(part_of(agrad0, x_at), attn_in[:n]), swap(attn_peer_half, "y")).astype(BF16)
+
+    scatter = functools.partial(lax.psum_scatter, axis_name="wo", scatter_dimension=0, tiled=True)
+    ffn_share = scatter(jnp.concatenate([down_half, up_half], axis=1)).astype(F32)
     hidden = down.shape[0]
-    up_share = jnp.stack([up_share[:, :hidden], up_share[:, hidden:]])
-
-    d1, d1b, dproj0, dproj1, ipart, sums1 = attn_bwd(
-        info, slopes, d2, dh, dh_other, normed, recip, nb, wqkv, wqkv1, wout, wout1,
-        proj0, proj1, att0, att1, lse0, lse1,
-    )
-    half = d1.shape[0]
-    mine = lax.dynamic_slice_in_dim(tokens, y_at * half, half, 0)
-
-    def attn_grads(dproj, att):
-        pieces = [grad(mine, dproj[i]) for i in range(3)] + [grad(d1b, att)]
-        return jnp.concatenate(pieces, axis=1)
-
-    attn_peer = swap(attn_grads(dproj1, att1).astype(BF16), "y")
-    attn_all = (attn_grads(dproj0, att0) + attn_peer.astype(F32)).astype(BF16)
-    attn_share = scatter(attn_all).astype(F32)
+    down_share = ffn_share[:, :hidden].T
+    up_share = jnp.stack([ffn_share[:, hidden:2 * hidden], ffn_share[:, 2 * hidden:]])
+    attn_share = scatter(attn_half).astype(F32)
     width = wqkv.shape[2]
     qkv_share = jnp.stack([attn_share[:, i * width:(i + 1) * width] for i in range(3)])
     out_share = attn_share[:, 3 * width:].T
@@ -553,18 +910,8 @@
     small = jnp.concatenate([sums1[:3], sums2[:3]], axis=0)
     small_share = lax.psum_scatter(lax.psum(small, "y"), WIDE, scatter_dimension=1, tiled=True)
 
-    quarter = half // 2
-    order = jnp.stack([2 * y_at, 2 * y_at + 1, 2 * (1 - y_at) + c_at, 2 * (1 - y_at) + 1 - c_at]).astype(jnp.int32)
-
-    def share(value, dtype):
-        near = swap(lax.dynamic_slice_in_dim(value, c_at * quarter, quarter, 0), "y")
-        far = swap(near, "core")
-        return place(order, value, near, far, dtype)
-
-    block_out = share(out, BF16)
-    ipart_other = swap(ipart, "core")
-    total = (d1 + (ipart.astype(F32) + ipart_other.astype(F32))).astype(BF16)
-    input_grad = share(total, F32)
+    block_out = place(order, out, near_out, swap(near_out, "core"), BF16)
+    input_grad = place(order, total, near_in, swap(near_in, "core"), F32)
     return (block_out, input_grad, qkv_share, out_share, up_share, down_share, small_share)
 
 

time: 501 us -> 376 us (0.75)
  waiting for transfers between devices: 256 us -> 132 us
  Pallas kernels: 136 us -> 160 us
  matrix products: 34.7 us -> 17.7 us
  other arithmetic: 13.3 us -> 22.4 us
  local copies, waits for them, and re-layouts: 20.6 us -> 13.5 us
  starting transfers between devices: 16.8 us -> 9.94 us
    ppermute x17 -> x12, waiting for transfers between devices: 167 us -> 92.4 us  [swap(): return lax.ppermute(value, axis, SWAP)]
    pallas_call x4 -> x1, Pallas kernels: 53.1 us -> 80.3 us  [forward(): pl.pallas_call(forward_kernel, in_specs=[smem, smem, vmem] + [hbm] * 5, o...]
    unnamed x6 -> x4, waiting for transfers between devices: 26.1 us -> 0.05 us
    reduce_scatter x2, waiting for transfers between devices: 62.1 us -> 39.9 us  [the longest x1 36.6 us: shards(): scatter(jnp.concatenate([down_half, up_half], axis=1)).astype(F32)]
    dot_general x12 -> x4, matrix products: 34.7 us -> 17.7 us  [grad(): lax.dot_general(a, b, (((0,), (0,)), ((), ())), preferred_element_type=F32)]
    pallas_call x1, Pallas kernels: 41.3 us -> 27.1 us  [ffn_bwd(): pl.pallas_call(ffn_bwd_kernel, grid_spec=pltpu.PrefetchScalarGridSpec(num...]
    pallas_call x1, Pallas kernels: 30.2 us -> 41 us  [attn_bwd(): pl.pallas_call(attn_bwd_kernel, grid_spec=pltpu.PrefetchScalarGridSpec(nu...]
    convert_element_type x4 -> x8, other arithmetic: 5.74 us -> 14.6 us  [the longest x1 4.5 us: shards(): total = (d1 + add(ipart, ipart_other)).astype(BF16)]
  transfers between devices with their start and end apart: 21 -> 15, of which waited for: 11 -> 7; matrix products, arithmetic and copies ran while one was open for 12% -> 12% of each run, Pallas kernels for 14% -> 12%
where the time goes in v2:
time: 376 us
  Pallas kernels  160 us (43%)
  waiting for transfers between devices  132 us (35%)
  other arithmetic  22.4 us (6%)
  matrix products  17.7 us (5%)
  between operations  14 us (4%)
  local copies, waits for them, and re-layouts  13.5 us (4%)
  starting transfers between devices  9.94 us (3%)
  blocking collectives  5.52 us (1%)
    ppermute x12, waiting for transfers between devices, swap(): return lax.ppermute(value, axis, SWAP)  92.4 us
    pallas_call x1, Pallas kernels, forward(): pl.pallas_call(forward_kernel, in_specs=[smem, smem, vmem] + [hbm] * 5, o...  80.3 us
    pallas_call x1, Pallas kernels, attn_bwd(): pl.pallas_call(attn_bwd_kernel, grid_spec=pltpu.PrefetchScalarGridSpec(nu...  41 us
    reduce_scatter x1, waiting for transfers between devices, shards(): scatter(jnp.concatenate([down_half, up_half], axis=1)).astype(F32)  36.6 us
    pallas_call x1, Pallas kernels, ffn_bwd(): pl.pallas_call(ffn_bwd_kernel, grid_spec=pltpu.PrefetchScalarGridSpec(num...  27.1 us
    dot_general x4, matrix products, grad(): lax.dot_general(a, b, (((0,), (0,)), ((), ())), preferred_element_type=F32)  17.7 us
    pallas_call x2, Pallas kernels, place(): pl.pallas_call(place_kernel, grid_spec=pltpu.PrefetchScalarGridSpec(num_s...  11.8 us
    ppermute x12, starting transfers between devices, swap(): return lax.ppermute(value, axis, SWAP)  9.82 us
  transfers between devices with their start and end apart: 15, of which 7 were waited for; matrix products, arithmetic and copies ran while one was open for 12% of the time, Pallas kernels for 12%

profile of v2, /device:TPU:0, one launch (start us, length us, event | category | flops | bytes accessed | tf_op | source)
XLA Modules:
  0.0 375.7 jit_solution(17534420500411332479)
XLA Ops:
  7.2 2.4 copy.29.wqkv.wqkv0
  11.5 80.3 %forward.1 = (bf16[2,3,1536,192]{3,2,1,0:T(8,128)(2,1)}, bf16[2,1536,192]{2,1,0:T(8,128)(2,1)}, f32[2,3,8,512]{3,2,1,0:T(8,128)}, f32[1536,768]{1,0:T(8,128)}, f...) custom-call(s32[6]{0:T(128)} %info.1, ...), custom_call_target="tpu_custom_call" | custom-call | flops 22951231488 | bytes 49545216 | tf_op jit(solution)/shard_map/forward/pallas_call | solution.py:809
  91.8 27.1 %ffn_bwd.1 = (bf16[1536,768]{1,0:T(8,128)(2,1)}, f32[1536,768]{1,0:T(8,128)}, bf16[1536,768]{1,0:T(8,128)(2,1)}, bf16[1536,1536]{1,0:T(8,128)(2,1)}, bf16[1536,1...) custom-call(s32[7]{0:T(128)} %pad_add_fusion.1.info, bf16[1536,768]{1,0:T(8,128)(2,1)} %get-tuple-element.35.pa, ...), custom_call_target="tpu_custom_call" | custom-call | flops 10871635968 | bytes 49545216 | tf_op jit(solution)/shard_map/ffn_bwd/pallas_call | solution.py:301
  118.9 4.9 %fusion.12 = bf16[768,768]{1,0:T(8,128)(2,1)} fusion(bf16[1536,768]{1,0:T(8,128)(2,1)} %get-tuple-element.44, bf16[2,1536,768]{2,1,0:T(8,128)(2,1)S(1)} %copy-done.7), kind=kOutput, calls=%fused_computation.18 | convolution fusion | flops 1812529152 | bytes 5898240 | tf_op jit(solution)/shard_map/dot_general | solution.py:854
  125.0 5.4 %convolution_convert_fusion = bf16[768,1536]{1,0:T(8,128)(2,1)} fusion(bf16[1536,768]{1,0:T(8,128)(2,1)S(1)} %copy-done.10, bf16[1536,1536]{1,0:T(8,128)(2,1)S(1)} %copy-done.8), kind=kOutput, calls=%fused_computation.1 | convolution fusion | flops 3625058304 | bytes 9437184 | tf_op jit(solution)/shard_map/dot_general | solution.py:854
  130.4 4.1 %convolution_convert_fusion.1 = bf16[768,1536]{1,0:T(8,128)(2,1)S(1)} fusion(bf16[1536,768]{1,0:T(8,128)(2,1)S(1)} %copy-done.10, bf16[1536,1536]{1,0:T(8,128)(2,1)S(1)} %bitcast.86), kind=kOutput, calls=%fused_computation.2 | convolution fusion | flops 3625058304 | bytes 9437184 | tf_op jit(solution)/shard_map/dot_general | solution.py:854
  134.6 1.9 constant_dynamic-slice_fusion
  138.4 2.2 collective-permute-start.10
  140.5 12.4 %collective-permute-done.8 = bf16[768,768]{1,0:T(8,128)(2,1)} collective-permute-done((bf16[768,768]{1,0:T(8,128)(2,1)}, bf16[768,768]{1,0:T(8,128)(2,1)}, u32[]{:S(2)}, u32[]{:S(2)}) %collective-permute-start.8) | collective-permute-done | bytes 1179680 | tf_op jit(solution)/shard_map/ppermute | solution.py:829
  153.0 3.3 add_convert_fusion.1
  156.3 41.0 %attn_bwd.1 = (f32[1536,768]{1,0:T(8,128)}, bf16[1536,768]{1,0:T(8,128)(2,1)}, bf16[768,768]{1,0:T(8,128)(2,1)}, bf16[768,768]{1,0:T(8,128)(2,1)}, f32[8,768]{1,0:T(8,128)}) custom-call(s32[7]{0:T(128)} %pad_add_fusion.1.info, f32[6]{0:T(128)} %fusion.21.slopes, bf16[3072,768]{1,0:T(8,128)(2,1)} %x_ref.1, f32[1536,768]{1,0:T(8,128)} %get-tuple-element.46.d2_ref, ...), custom_call_target="tpu_custom_call" | custom-call | flops 19327352832 | bytes 35389440 | tf_op jit(solution)/shard_map/attn_bwd/pallas_call | solution.py:424
  199.9 2.5 collective-permute-start.6
  203.8 24.8 %collective-permute-done.6 = bf16[768,768]{1,0:T(8,128)(2,1)S(1)} collective-permute-done((bf16[768,768]{1,0:T(8,128)(2,1)S(1)}, bf16[768,768]{1,0:T(8,128)(2,1)S(1)}, u32[]{:S(2)}, u32[]{:S(2)}) %collective-permute-start.6) | collective-permute-done | bytes 1179680 | tf_op jit(solution)/shard_map/ppermute | solution.py:829
  230.9 1.7 collective-permute-start.9
  235.0 9.9 %collective-permute-done.7 = bf16[384,768]{1,0:T(8,128)(2,1)} collective-permute-done((bf16[384,768]{1,0:T(8,128)(2,1)}, bf16[384,768]{1,0:T(8,128)(2,1)}, u32[]{:S(2)}, u32[]{:S(2)}) %collective-permute-start.7) | collective-permute-done | bytes 589856 | tf_op jit(solution)/shard_map/ppermute | solution.py:829
  245.0 2.5 fusion.18
  253.9 4.5 %add_convert_fusion.mine = bf16[1536,768]{1,0:T(8,128)(2,1)S(1)} fusion(f32[1536,768]{1,0:T(8,128)} %get-tuple-element.54, bf16[1536,768]{1,0:T(8,128)(2,1)} %collective-permute-done.3, bf16[1536,768]{1,0:T(8,128)(2,1)} %get-tuple-element.55), kind=kLoop, calls=%fused_computation | loop fusion | flops 5898240 | bytes 11796480 | tf_op jit(solution)/shard_map/convert_element_type | solution.py:888
  259.8 22.2 %collective-permute-done.near = bf16[768,768]{1,0:T(8,128)(2,1)S(1)} collective-permute-done((bf16[768,768]{1,0:T(8,128)(2,1)S(1)}, bf16[768,768]{1,0:T(8,128)(2,1)S(1)}, u32[]{:S(2)}, u32[]{:S(2)}) %collective-permute-start) | collective-permute-done | bytes 1179680 | tf_op jit(solution)/shard_map/ppermute | solution.py:829
  282.0 23.1 %collective-permute-done.4.near = bf16[768,768]{1,0:T(8,128)(2,1)} collective-permute-done((bf16[768,768]{1,0:T(8,128)(2,1)S(1)}, bf16[768,768]{1,0:T(8,128)(2,1)}, u32[]{:S(2)}, u32[]{:S(2)}) %collective-permute-start.4) | collective-permute-done | bytes 1179680 | tf_op jit(solution)/shard_map/ppermute | solution.py:829
  305.8 5.3 %place.2 = bf16[3072,768]{1,0:T(8,128)(2,1)} custom-call(s32[4]{0:T(128)} %pad_add_fusion.order, bf16[1536,768]{1,0:T(8,128)(2,1)} %get-tuple-element.42.mine, bf16[768,768]{1,0:T(8,128)(2,1)} %copy-done.2, bf16[768,768]{1,0:T(8,128)(2,1)} %collective-permute-done.1.far), custom_call_target="tpu_custom_call" | custom-call | bytes 14155776 | tf_op jit(solution)/shard_map/place/pallas_call | solution.py:476
  311.9 5.5 %psum.8 = f32[6,96]{1,0:T(8,128)} all-reduce(f32[6,96]{1,0:T(8,128)S(1)} %copy.37), channel_id=1, replica_groups=mesh['wo'=4,'x'=2,'y'=2,'core'=2] {'y'}, use_global_device_ids=true, to_apply=%region_2.3 | all-reduce | flops 576 | bytes 4608 | tf_op jit(solution)/shard_map/psum | solution.py:911
  317.4 3.3 reduce-scatter.6.cloned.1.call-done
  323.3 36.6 %reduce-scatter.8.cloned.1.call-done = bf16[96,2304]{1,0:T(8,128)(2,1)} async-done(((bf16[384,2304]{1,0:T(8,128)(2,1)}), bf16[96,2304]{1,0:T(8,128)(2,1)}) %reduce-scatter.8.cloned.1.call-update) | async-done | bytes 442384 | tf_op jit(solution)/shard_map/reduce_scatter | solution.py:901
  362.6 6.6 %place.3 = f32[3072,768]{1,0:T(8,128)} custom-call(s32[4]{0:T(128)} %pad_add_fusion.order, bf16[1536,768]{1,0:T(8,128)(2,1)} %copy-done, bf16[768,768]{1,0:T(8,128)(2,1)} %collective-permute-done.4.near, bf16[768,768]{1,0:T(8,128)(2,1)} %collective-permute-done.5.far), custom_call_target="tpu_custom_call" | custom-call | bytes 14155776 | tf_op jit(solution)/shard_map/place/pallas_call | solution.py:476
  (84 shorter events, 28.2 us)
Async XLA Ops:
  7.2 303.9 %reduce-scatter.10.cloned.1.call-start = ((), (), s32[]{:S(2)}) async-start(), calls=%async_computation.5 | async-start | bytes 442368
  91.8 27.1 %copy-start.7 = (bf16[2,1536,768]{2,1,0:T(8,128)(2,1)S(1)}, bf16[2,1536,768]{2,1,0:T(8,128)(2,1)}, u32[]{:S(2)}) copy-start(bf16[2,1536,768]{2,1,0:T(8,128)(2,1)} %get-tuple-element.45) | copy-start | bytes 14155780
  118.9 11.5 %slice-start.2 = ((s8[4718592]{0:T(1024)(128)(4,1)}), s8[4194304]{0:T(1024)(128)(4,1)S(1)}, s32[]{:S(2)}) async-start(s8[4718592]{0:T(1024)(128)(4,1)} %bitcast.85), calls=%async_computation.8 | async-start | bytes 8388608
  123.8 29.1 %collective-permute-start.8 = (bf16[768,768]{1,0:T(8,128)(2,1)}, bf16[768,768]{1,0:T(8,128)(2,1)}, u32[]{:S(2)}, u32[]{:S(2)}) collective-permute-start(bf16[768,768]{1,0:T(8,128)(2,1)} %fusion.12), channel_id=1, source_target_pairs={{0,2},{2,0},{1,3},{3,1},{4,6},{6,4},{5,7},{7,5},{8,10},{10,8},{9,1... | collective-permute-start | bytes 3538952 | tf_op jit(solution)/shard_map/ppermute | solution.py:829
  124.4 31.9 %collective-permute-start.2 = (bf16[1536,768]{1,0:T(8,128)(2,1)}, bf16[1536,768]{1,0:T(8,128)(2,1)}, u32[]{:S(2)}, u32[]{:S(2)}) collective-permute-start(bf16[1536,768]{1,0:T(8,128)(2,1)} %get-tuple-element.47.ha), channel_id=1, source_target_pairs={{0,1},{1,0},{2,3},{3,2},{4,5},{5,4},{6,7},{7,6},{8,9},{9,8},{10,11... | collective-permute-start | bytes 7077896 | tf_op jit(solution)/shard_map/ppermute | solution.py:829
  134.6 18.4 %slice-start = ((s8[4718592]{0:T(1024)(128)(4,1)}), s8[4194304]{0:T(1024)(128)(4,1)S(1)}, s32[]{:S(2)}) async-start(s8[4718592]{0:T(1024)(128)(4,1)} %bitcast.83), calls=%async_computation.6 | async-start | bytes 8388608
  136.5 16.4 %slice-start.1 = ((s8[4718592]{0:T(1024)(128)(4,1)}), s8[524288]{0:T(1024)(128)(4,1)S(1)}, s32[]{:S(2)}) async-start(s8[4718592]{0:T(1024)(128)(4,1)} %bitcast.83), calls=%async_computation.7 | async-start | bytes 1048576
  136.7 16.2 %copy-start.9 = (bf16[1536,768]{1,0:T(8,128)(2,1)S(1)}, bf16[1536,768]{1,0:T(8,128)(2,1)}, u32[]{:S(2)}) copy-start(bf16[1536,768]{1,0:T(8,128)(2,1)} %get-tuple-element.44) | copy-start | bytes 7077892
  138.4 64.1 %collective-permute-start.10 = (bf16[768,1536]{1,0:T(8,128)(2,1)}, bf16[768,1536]{1,0:T(8,128)(2,1)S(1)}, u32[]{:S(2)}, u32[]{:S(2)}) collective-permute-start(bf16[768,1536]{1,0:T(8,128)(2,1)} %pad_maximum_fusion), channel_id=1, source_target_pairs={{0,4},{4,0},{1,5},{5,1},{2,6},{6,2},{3,7},{7,3},{8,12},{12,8},{9,1... | collective-permute-start | bytes 7077896 | tf_op jit(solution)/shard_map/ppermute | solution.py:829
  199.9 28.7 %collective-permute-start.6 = (bf16[768,768]{1,0:T(8,128)(2,1)S(1)}, bf16[768,768]{1,0:T(8,128)(2,1)S(1)}, u32[]{:S(2)}, u32[]{:S(2)}) collective-permute-start(bf16[768,768]{1,0:T(8,128)(2,1)S(1)} %pad_maximum_fusion.2), channel_id=1, source_target_pairs={{0,4},{4,0},{1,5},{5,1},{2,6},{6,2},{3,7},{7,3},{8,12},{12,8},{9,1... | collective-permute-start | bytes 3538952 | tf_op jit(solution)/shard_map/ppermute | solution.py:829
  203.8 28.9 %copy-start.5 = (f32[8,768]{1,0:T(8,128)S(1)}, f32[8,768]{1,0:T(8,128)}, u32[]{:S(2)}) copy-start(f32[8,768]{1,0:T(8,128)} %get-tuple-element.62) | copy-start | bytes 73732
  203.8 28.9 %copy-start.6 = (f32[8,768]{1,0:T(8,128)S(1)}, f32[8,768]{1,0:T(8,128)}, u32[]{:S(2)}) copy-start(f32[8,768]{1,0:T(8,128)} %get-tuple-element.61) | copy-start | bytes 73732
  203.8 45.1 %collective-permute-start.11 = (bf16[384,1536]{1,0:T(8,128)(2,1)}, bf16[384,1536]{1,0:T(8,128)(2,1)}, u32[]{:S(2)}, u32[]{:S(2)}) collective-permute-start(bf16[384,1536]{1,0:T(8,128)(2,1)} %fusion), channel_id=1, source_target_pairs={{0,2},{2,0},{1,3},{3,1},{4,6},{6,4},{5,7},{7,5},{8,10},{10,8},{9,1... | collective-permute-start | bytes 3538952 | tf_op jit(solution)/shard_map/ppermute | solution.py:829
  229.7 15.2 %collective-permute-start.7 = (bf16[384,768]{1,0:T(8,128)(2,1)}, bf16[384,768]{1,0:T(8,128)(2,1)}, u32[]{:S(2)}, u32[]{:S(2)}) collective-permute-start(bf16[384,768]{1,0:T(8,128)(2,1)} %fusion.16), channel_id=1, source_target_pairs={{0,2},{2,0},{1,3},{3,1},{4,6},{6,4},{5,7},{7,5},{8,10},{10,8},{9,1... | collective-permute-start | bytes 1769480 | tf_op jit(solution)/shard_map/ppermute | solution.py:829
  230.9 16.6 %collective-permute-start.9 = (bf16[384,768]{1,0:T(8,128)(2,1)}, bf16[384,768]{1,0:T(8,128)(2,1)}, u32[]{:S(2)}, u32[]{:S(2)}) collective-permute-start(bf16[384,768]{1,0:T(8,128)(2,1)} %bitcast.19), channel_id=1, source_target_pairs={{0,4},{4,0},{1,5},{5,1},{2,6},{6,2},{3,7},{7,3},{8,12},{12,8},{9,1... | collective-permute-start | bytes 1769480 | tf_op jit(solution)/shard_map/ppermute | solution.py:829
  232.6 21.3 %collective-permute-start.3 = (bf16[1536,768]{1,0:T(8,128)(2,1)}, bf16[1536,768]{1,0:T(8,128)(2,1)}, u32[]{:S(2)}, u32[]{:S(2)}) collective-permute-start(bf16[1536,768]{1,0:T(8,128)(2,1)} %get-tuple-element.55), channel_id=1, source_target_pairs={{0,1},{1,0},{2,3},{3,2},{4,5},{5,4},{6,7},{7,6},{8,9},{9,8},{10,11... | collective-permute-start | bytes 7077896 | tf_op jit(solution)/shard_map/ppermute | solution.py:829
  235.0 85.7 %reduce-scatter.6.cloned.1.call-start = ((), (), s32[]{:S(2)}) async-start(), calls=%async_computation.3 | async-start | bytes 737280 | tf_op jit(solution)/shard_map/reduce_scatter | solution.py:905
  247.5 112.4 %reduce-scatter.8.cloned.1.call-start = ((), (), s32[]{:S(2)}) async-start(), calls=%async_computation.4 | async-start | bytes 2211840 | tf_op jit(solution)/shard_map/reduce_scatter | solution.py:901
  253.0 29.0 %collective-permute-start = (bf16[768,768]{1,0:T(8,128)(2,1)S(1)}, bf16[768,768]{1,0:T(8,128)(2,1)S(1)}, u32[]{:S(2)}, u32[]{:S(2)}) collective-permute-start(bf16[768,768]{1,0:T(8,128)(2,1)S(1)} %constant_dynamic-slice_fusion.11), channel_id=1, source_target_pairs={{0,2},{2,0},{1,3},{3,1},{4,6},{6,4},{5,7},{7,5},{8,10},{10,8},{9,1... | collective-permute-start | bytes 3538952 | tf_op jit(solution)/shard_map/ppermute | solution.py:829
  258.5 52.6 %copy-start = (bf16[1536,768]{1,0:T(8,128)(2,1)}, bf16[1536,768]{1,0:T(8,128)(2,1)S(1)}, u32[]{:S(2)}) copy-start(bf16[1536,768]{1,0:T(8,128)(2,1)S(1)} %add_convert_fusion.mine) | copy-start | bytes 7077892
  258.6 46.6 %collective-permute-start.4 = (bf16[768,768]{1,0:T(8,128)(2,1)S(1)}, bf16[768,768]{1,0:T(8,128)(2,1)}, u32[]{:S(2)}, u32[]{:S(2)}) collective-permute-start(bf16[768,768]{1,0:T(8,128)(2,1)S(1)} %constant_dynamic-slice_fusion.10), channel_id=1, source_target_pairs={{0,2},{2,0},{1,3},{3,1},{4,6},{6,4},{5,7},{7,5},{8,10},{10,8},{9,1... | collective-permute-start | bytes 3538952 | tf_op jit(solution)/shard_map/ppermute | solution.py:829
  282.0 23.8 %copy-start.2 = (bf16[768,768]{1,0:T(8,128)(2,1)}, bf16[768,768]{1,0:T(8,128)(2,1)S(1)}, u32[]{:S(2)}) copy-start(bf16[768,768]{1,0:T(8,128)(2,1)S(1)} %collective-permute-done.near) | copy-start | bytes 3538948
  282.0 23.8 %collective-permute-start.1 = (bf16[768,768]{1,0:T(8,128)(2,1)S(1)}, bf16[768,768]{1,0:T(8,128)(2,1)}, u32[]{:S(2)}, u32[]{:S(2)}) collective-permute-start(bf16[768,768]{1,0:T(8,128)(2,1)S(1)} %collective-permute-done.near), channel_id=1, source_target_pairs={{0,1},{1,0},{2,3},{3,2},{4,5},{5,4},{6,7},{7,6},{8,9},{9,8},{10,11... | collective-permute-start | bytes 3538952 | tf_op jit(solution)/shard_map/ppermute | solution.py:829
  305.1 57.5 %collective-permute-start.5 = (bf16[768,768]{1,0:T(8,128)(2,1)}, bf16[768,768]{1,0:T(8,128)(2,1)}, u32[]{:S(2)}, u32[]{:S(2)}) collective-permute-start(bf16[768,768]{1,0:T(8,128)(2,1)} %collective-permute-done.4.near), channel_id=1, source_target_pairs={{0,1},{1,0},{2,3},{3,2},{4,5},{5,4},{6,7},{7,6},{8,9},{9,8},{10,11... | collective-permute-start | bytes 3538952 | tf_op jit(solution)/shard_map/ppermute | solution.py:829
  (6 other events, 23.9 us)
Sparse Core Ops, SparseCore 0:
  235.1 62.3 reduce-scatter.9
  299.8 20.9 reduce-scatter.5
  323.1 36.7 reduce-scatter.7

commit v3 on v2

--- a/solution.py
+++ b/solution.py
@@ -50,101 +50,6 @@
     return pltpu.CompilerParams(vmem_limit_bytes=VMEM_LIMIT, dimension_semantics=("arbitrary",))
 
 
-def attn_fwd_kernel(last, info, slopes, x_ref, wqkv, wout, *rest):
-    if last:
-        prev, proj, att_ref, lse_ref, part, dist = rest
-    else:
-        proj, att_ref, lse_ref, part, dist = rest
-    step = pl.program_id(0)
-    win = x_ref.shape[0]
-    width = wqkv.shape[2]
-    heads = width // HEAD_DIM
-
-    @pl.when(step == 0)
-    def _():
-        fill_distance(dist)
-
-    x = x_ref[...]
-    q = dot(x, wqkv[0]).astype(BF16)
-    k = dot(x, wqkv[1]).astype(BF16)
-    v = dot(x, wqkv[2]).astype(BF16)
-    proj[0], proj[1], proj[2] = q, k, v
-    limit = info[1 + info[0] * pl.num_programs(0) + step]
-    lanes = head_lanes(width)
-    key_on = lax.broadcasted_iota(jnp.int32, (1, win), 1) < limit
-    rows = win // 2
-    stat_lane = lax.broadcasted_iota(jnp.int32, (1, 128), 1)
-    for b in range(win // rows):
-        at = slice(b * rows, (b + 1) * rows)
-        qb = q[at] * jnp.asarray(SCALE, BF16)
-        att = jnp.zeros((rows, width), F32)
-        stat = jnp.zeros((rows, 128), F32)
-        for h in range(heads):
-            qh = jnp.where(lanes[h], qb, jnp.zeros_like(qb))
-            s = dot_nt(qh, k) - slopes[h] * dist[at]
-            s = jnp.where(key_on, s, NEG)
-            top = jnp.max(s, axis=1, keepdims=True)
-            p = jnp.exp(s - top)
-            total = jnp.sum(p, axis=1, keepdims=True)
-            o = dot(p.astype(BF16), v) * (1.0 / total)
-            att = jnp.where(lanes[h], o, att)
-            stat = jnp.where(stat_lane == h, top + jnp.log(total), stat)
-        attb = att.astype(BF16)
-        att_ref[at] = attb
-        lse_ref[0, :, at] = stat.T[0:8]
-        out = dot(attb, wout[...])
-        if last:
-            out = out + prev[at].astype(F32)
-        part[at] = out.astype(BF16)
-
-
-def attn_fwd(info, slopes, tokens, wqkv, wout, prev):
-    _, d, width = wqkv.shape
-    nwin = (info.shape[0] - 1) // 2
-    win = tokens.shape[0] // (2 * nwin)
-    half = nwin * win
-    last = prev is not None
-    heads = width // HEAD_DIM
-    row = lambda w: pl.BlockSpec((win, w), lambda i, *_: (i, 0))
-    specs = [
-        pl.BlockSpec((win, d), lambda i, info, sl: (info[0] * nwin + i, 0)),
-        whole(wqkv.shape),
-        whole(wout.shape),
-    ]
-    args = [tokens, wqkv, wout]
-    if last:
-        specs.append(row(d))
-        args.append(prev)
-    return pl.pallas_call(
-        functools.partial(attn_fwd_kernel, last),
-        grid_spec=pltpu.PrefetchScalarGridSpec(
-            num_scalar_prefetch=2,
-            grid=(nwin,),
-            in_specs=specs,
-            out_specs=[
-                pl.BlockSpec((3, win, width), lambda i, *_: (0, i, 0)),
-                row(width),
-                pl.BlockSpec((1, 8, win), lambda i, *_: (i, 0, 0)),
-                row(d),
-            ],
-            scratch_shapes=[pltpu.VMEM((win, win), F32)],
-        ),
-        out_shape=[
-            jax.ShapeDtypeStruct((3, half, width), BF16),
-            jax.ShapeDtypeStruct((half, width), BF16),
-            jax.ShapeDtypeStruct((nwin, 8, win), F32),
-            jax.ShapeDtypeStruct((half, d), BF16),
-        ],
-        compiler_params=params(),
-        cost_estimate=pl.CostEstimate(
-            flops=2 * half * d * width * 4 + 4 * nwin * heads * win * win * 256,
-            bytes_accessed=2 * (half * d * 2 + half * width * 4 + d * width * 4),
-            transcendentals=nwin * heads * win * win,
-        ),
-        name="attn_fwd_last" if last else "attn_fwd_first",
-    )(info, slopes, *args)
-
-
 def standardize(value):
     center = value - jnp.mean(value, axis=1, keepdims=True)
     recip = lax.rsqrt(jnp.mean(center * center, axis=1, keepdims=True) + EPS)
@@ -163,101 +68,8 @@
     return jnp.concatenate(sums + [jnp.zeros((8 - len(sums), width), F32)], axis=0)
 
 
-def feed(hb, up, down, a_ref, b_ref, act_ref):
-    hidden = down.shape[0]
-    step = 256
-    for at in range(0, hidden, step):
-        cols = slice(at, at + step)
-        gate = dot(hb, up[0, :, cols])
-        lift = dot(hb, up[1, :, cols])
-        cdf = 0.5 * (1.0 + lax.erf(gate * (1.0 / math.sqrt(2.0))))
-        pdf = jnp.exp(-0.5 * gate * gate) * (1.0 / math.sqrt(2.0 * math.pi))
-        gelu = gate * cdf
-        act = (gelu * lift).astype(BF16)
-        a_ref[:, cols] = (lift * (cdf + gate * pdf)).astype(BF16)
-        b_ref[:, cols] = gelu.astype(BF16)
-        act_ref[:, cols] = act
-    return dot(act_ref[...], down[...])
-
-
-def ffn_first_kernel(pa, pb, x_ref, nb, up, down, normed_ref, recip_ref, h_ref, a_ref, b_ref, act_ref, part):
-    first = pa[...].astype(F32) + pb[...].astype(F32) + nb[2:3] + x_ref[...].astype(F32)
-    normed, recip = standardize(first)
-    normed_ref[...] = normed
-    recip_ref[...] = jnp.broadcast_to(recip, recip_ref.shape)
-    hb = (normed * nb[0:1] + nb[1:2]).astype(BF16)
-    h_ref[...] = hb
-    part[...] = feed(hb, up, down, a_ref, b_ref, act_ref).astype(BF16)
-
-
-def ffn_second_kernel(hb, prev, up, down, a_ref, b_ref, act_ref, part):
-    total = feed(hb[...], up, down, a_ref, b_ref, act_ref)
-    part[...] = (total + prev[...].astype(F32)).astype(BF16)
-
-
-def ffn_first(half_block, pa, pb, tokens, nb, up, down, tile=256):
-    half, d = pa.shape
-    hidden = down.shape[0]
-    n = half // tile
-    row = lambda w: pl.BlockSpec((tile, w), lambda i, *_: (i, 0))
-
-    def kernel(info, *refs):
-        ffn_first_kernel(*refs)
-
-    return pl.pallas_call(
-        kernel,
-        grid_spec=pltpu.PrefetchScalarGridSpec(
-            num_scalar_prefetch=1,
-            grid=(n,),
-            in_specs=[
-                row(d),
-                row(d),
-                pl.BlockSpec((tile, d), lambda i, info: (info[0] * n + i, 0)),
-                whole(nb.shape),
-                whole(up.shape),
-                whole(down.shape),
-            ],
-            out_specs=[row(d), row(128), row(d), row(hidden), row(hidden), row(hidden), row(d)],
-        ),
-        out_shape=[
-            jax.ShapeDtypeStruct((half, d), F32),
-            jax.ShapeDtypeStruct((half, 128), F32),
-            jax.ShapeDtypeStruct((half, d), BF16),
-            jax.ShapeDtypeStruct((half, hidden), BF16),
-            jax.ShapeDtypeStruct((half, hidden), BF16),
-            jax.ShapeDtypeStruct((half, hidden), BF16),
-            jax.ShapeDtypeStruct((half, d), BF16),
-        ],
-        compiler_params=params(),
-        cost_estimate=pl.CostEstimate(
-            flops=6 * half * d * hidden, bytes_accessed=half * d * 14 + half * hidden * 6 + 6 * d * hidden,
-            transcendentals=half * hidden * 2,
-        ),
-        name="ffn_first",
-    )(half_block, pa, pb, tokens, nb, up, down)
-
-
-def ffn_second(hb, prev, up, down, tile=256):
-    half, d = hb.shape
-    hidden = down.shape[0]
-    row = lambda w: pl.BlockSpec((tile, w), lambda i: (i, 0))
-    return pl.pallas_call(
-        ffn_second_kernel,
-        grid=(half // tile,),
-        in_specs=[row(d), row(d), whole(up.shape), whole(down.shape)],
-        out_specs=[row(hidden), row(hidden), row(hidden), row(d)],
-        out_shape=[jax.ShapeDtypeStruct((half, hidden), BF16)] * 3 + [jax.ShapeDtypeStruct((half, d), BF16)],
-        compiler_params=params(),
-        cost_estimate=pl.CostEstimate(
-            flops=6 * half * d * hidden, bytes_accessed=half * d * 6 + half * hidden * 6 + 6 * d * hidden,
-            transcendentals=half * hidden * 2,
-        ),
-        name="ffn_second",
-    )(hb, prev, up, down)
-
-
 def ffn_bwd_kernel(info, pa, pb, normed_ref, cot, nb, up0, up1, down0, down1, a_all, b_all,
-                   out_ref, d2_ref, d2b_ref, dgu0, dgu1, dh_ref, sums_ref):
+                   out_ref, d2_ref, d2t_ref, dgu, dh_ref, sums_ref):
     hidden = down0.shape[0]
     h = normed_ref[...] * nb[0:1] + nb[1:2]
     second = pa[...].astype(F32) + pb[...].astype(F32) + nb[5:6] + h
@@ -268,7 +80,7 @@
     d2 = norm_grad(c, normed, recip, gain)
     d2_ref[...] = d2
     d2b = d2.astype(BF16)
-    d2b_ref[...] = d2b
+    d2t_ref[...] = d2b.T
     sums = rows_of_sums([c * normed, c, d2])
 
     @pl.when(pl.program_id(0) == 0)
@@ -281,14 +93,14 @@
 
     total = None
     step = 256
-    for g, (up, down, dgu) in enumerate(((up0, down0, dgu0), (up1, down1, dgu1))):
+    for g, (up, down) in enumerate(((up0, down0), (up1, down1))):
         for at in range(0, hidden, step):
             cols = slice(at, at + step)
             dact = dot_nt(d2b, down[cols, :])
-            dgu[:, cols] = (dact * a_all[g, :, cols].astype(F32)).astype(BF16)
-            dgu[:, slice(hidden + at, hidden + at + step)] = (dact * b_all[g, :, cols].astype(F32)).astype(BF16)
+            dgu[g, :, cols] = (dact * a_all[g, :, cols].astype(F32)).astype(BF16)
+            dgu[g, :, slice(hidden + at, hidden + at + step)] = (dact * b_all[g, :, cols].astype(F32)).astype(BF16)
         for k in range(2):
-            term = dot_nt(dgu[:, k * hidden:(k + 1) * hidden], up[k])
+            term = dot_nt(dgu[g, :, k * hidden:(k + 1) * hidden], up[k])
             total = term if total is None else total + term
     dh_ref[...] = total.astype(BF16)
 
@@ -311,14 +123,17 @@
                 pl.BlockSpec((2, tile, hidden), lambda i, *_: (0, i, 0)),
                 pl.BlockSpec((2, tile, hidden), lambda i, *_: (0, i, 0)),
             ],
-            out_specs=[row(d), row(d), row(d), row(2 * hidden), row(2 * hidden), row(d), whole((8, d))],
+            out_specs=[
+                pl.BlockSpec((tile, d), lambda i, info: (info[0] * n + i, 0)), row(d),
+                pl.BlockSpec((d, tile), lambda i, *_: (0, i)),
+                pl.BlockSpec((2, tile, 2 * hidden), lambda i, *_: (0, i, 0)), row(d), whole((8, d)),
+            ],
         ),
         out_shape=[
-            jax.ShapeDtypeStruct((half, d), BF16),
+            jax.ShapeDtypeStruct((2 * half, d), BF16),
             jax.ShapeDtypeStruct((half, d), F32),
-            jax.ShapeDtypeStruct((half, d), BF16),
-            jax.ShapeDtypeStruct((half, 2 * hidden), BF16),
-            jax.ShapeDtypeStruct((half, 2 * hidden), BF16),
+            jax.ShapeDtypeStruct((d, half), BF16),
+            jax.ShapeDtypeStruct((2, half, 2 * hidden), BF16),
             jax.ShapeDtypeStruct((half, d), BF16),
             jax.ShapeDtypeStruct((8, d), F32),
         ],
@@ -501,9 +316,9 @@
 
 
 def forward_kernel(info, slopes, nb, tokens, wqkv, wout, up, down,
-                   proj_out, att_out, lse_out, normed_out, recip_out, h_out, a_out, b_out, act_out, fown_out, frecv_out,
+                   proj_out, att_out, lse_out, normed_out, recip_out, ht_out, a_out, b_out, act_out, fown_out, frecv_out,
                    wqkv1_out, wout1_out, up1_out, down1_out,
-                   xbuf, wqv, wov, upv, downv, projb, attb, lseb, pown, precv, normedb, recipb, hbuf, ab, bb, actb,
+                   xbuf, wqv, wov, upv, downv, projb, attb, lseb, pown, precv, normedb, recipb, hbuf, htb, ab, bb, actb,
                    facc, fown, frecv, dist,
                    load_sem, ysend, yrecv, xsend, xrecv, psend, prem, fsend, frem, out_sem, pout_sem, tout_sem, fout_sem):
     x_at, y_at, c_at = (lax.axis_index(n) for n in ("x", "y", "core"))
@@ -660,11 +475,11 @@
         ]
 
     def norm_copies(i):
-        rows = pl.ds(i * TILE, TILE)
+        rows = pl.ds(pl.multiple_of(i * TILE, TILE), TILE)
         return [
             pltpu.make_async_copy(b.at[rows], o.at[rows], fout_sem.at[n, i])
-            for n, (b, o) in enumerate(((normedb, normed_out), (recipb, recip_out), (hbuf, h_out)))
-        ]
+            for n, (b, o) in enumerate(((normedb, normed_out), (recipb, recip_out)))
+        ] + [pltpu.make_async_copy(htb.at[:, rows], ht_out.at[:, rows], fout_sem.at[2, i])]
 
     def first(i, carry):
         start = i * TILE
@@ -680,6 +495,7 @@
         recipb[rows] = jnp.broadcast_to(recip, (TILE, 128))
         hb = (normed * nb[0:1] + nb[1:2]).astype(BF16)
         hbuf[rows] = hb
+        htb[:, pl.ds(pl.multiple_of(start, TILE), TILE)] = hb.T
         hidden_units(0, start, hb)
         facc[rows] = dot(actb[0, rows], downv[0])
         for copy in tile_copies(i) + norm_copies(i):
@@ -795,14 +611,14 @@
     acts = [((2, half, hidden), BF16)] * 3
     outs = [
         ((2, 3, half, width), BF16), ((2, half, width), BF16), ((2, nwin, 8, win), F32),
-        ((half, d), F32), ((half, 128), F32), ((half, d), BF16), *acts,
+        ((half, d), F32), ((half, 128), F32), ((d, half), BF16), *acts,
         ((half, d), BF16), ((half, d), BF16),
         (wqkv.shape, BF16), (wout.shape, BF16), (up.shape, BF16), (down.shape, BF16),
     ]
     bufs = [
         ((half, d), BF16), ((2,) + wqkv.shape, BF16), ((2,) + wout.shape, BF16), ((2,) + up.shape, BF16),
         ((2,) + down.shape, BF16), ((2, 3, half, width), BF16), ((2, half, width), BF16), ((2, nwin, 8, win), F32),
-        ((half, d), BF16), ((half, d), BF16), ((half, d), F32), ((half, 128), F32), ((half, d), BF16), *acts,
+        ((half, d), BF16), ((half, d), BF16), ((half, d), F32), ((half, 128), F32), ((half, d), BF16), ((d, half), BF16), *acts,
         ((half, d), F32), ((half, d), BF16), ((half, d), BF16), ((win, win), F32),
     ]
     sems = [(5,), (6,), (6,), (6,), (6,), (nwin,), (nwin,), (tiles,), (tiles,), (5,), (2, 2 * nwin), (3, 2 * tiles), (5, tiles)]
@@ -821,6 +637,451 @@
     )(lengths, slopes, nb, tokens, wqkv, wout, up, down)
 
 
+BLOCK = 256
+FLIGHT = 4
+
+
+def backward_kernel(lengths, slopes, nb, sums2, tokens, d2_in, dh_in, normed_in, recip_in, wqkv, wqkv1, wout, wout1,
+                    proj_in, att_in, lse_in, dgu_in, act_in, ht_in, d2t_in, half_in,
+                    share, total_sums, block_out, input_grad,
+                    gbuf, r1, r2, zr, dhr, dhw, normw, d2w, recw, xw, projw, attw, lsev, wqv, wov, ipown, iprecv, totb,
+                    sumb, sumr, sumz, sum1,
+                    g1s, g1r, g2s, g2r, zs, zrs, pre_sem, win_sem, w_sem, dh_s, dh_r, ip_s, ip_r,
+                    tot_sem, iy_s, iy_r, ic_s, ic_r, bo_s, bo_r, sm_s, sm_r, smz_s, smz_r, ring_sem, t_sem):
+    at = {n: lax.axis_index(n) for n in ("wo", "x", "y", "core")}
+    wo_at, x_at, y_at, c_at = at["wo"], at["x"], at["y"], at["core"]
+    n_wo = gbuf.shape[3]
+    blocks = gbuf.shape[0]
+    own_rows = gbuf.shape[4]
+    half, d = normed_in.shape
+    _, nwin, _, win = lse_in.shape
+    width = wout.shape[0]
+    hidden = act_in.shape[2]
+    heads = width // HEAD_DIM
+    ffn_blocks = 3 * hidden // BLOCK
+
+    barrier = pltpu.get_barrier_semaphore()
+    for axis in ("x", "y", "core"):
+        pl.semaphore_signal(barrier, inc=1, device_id={axis: 1 - at[axis]}, device_id_type=MESH_ID)
+    for k in range(n_wo - 1):
+        pl.semaphore_signal(barrier, inc=1, device_id={"wo": (wo_at + k + 1) % n_wo}, device_id_type=MESH_ID)
+    pl.semaphore_wait(barrier, n_wo + 2)
+
+    def copy_one(b, is_y):
+        send = 1 if is_y else 1 - x_at
+        axis = "y" if is_y else "x"
+        return remote(gbuf.at[b, send], r1.at[b], g1s.at[b], g1r.at[b], axis, 1 - at[axis])
+
+    def copy_two(b, is_y):
+        keep = 0 if is_y else x_at
+        send = 1 - x_at if is_y else 1
+        axis = "x" if is_y else "y"
+        return remote(gbuf.at[b, keep, send], r2.at[b], g2s.at[b], g2r.at[b], axis, 1 - at[axis])
+
+    def copy_z(b, is_y, k):
+        keep = 0 if is_y else x_at
+        keep2 = x_at if is_y else 0
+        to = (wo_at + k + 1) % n_wo
+        return remote(gbuf.at[b, keep, keep2, to], zr.at[b, k], zs.at[b, k], zrs.at[b, k], "wo", to)
+
+    def by_kind(b, f):
+        @pl.when(b % 4 == 1)
+        def _():
+            f(True)
+
+        @pl.when(b % 4 != 1)
+        def _():
+            f(False)
+
+    def stage_one(b):
+        copy_one(b, False).wait_recv()
+
+        def go(is_y):
+            keep = 0 if is_y else x_at
+            gbuf[b, keep] = (gbuf[b, keep].astype(F32) + r1[b].astype(F32)).astype(BF16)
+            copy_two(b, is_y).start()
+
+        by_kind(b, go)
+
+        @pl.when((b + FLIGHT < blocks) & ((b + FLIGHT < ffn_blocks) | (b >= 2 * nwin)))
+        def _():
+            by_kind(b + FLIGHT, lambda is_y: copy_one(b + FLIGHT, is_y).start())
+
+    def stage_two(b):
+        copy_two(b, False).wait_recv()
+
+        def go(is_y):
+            keep = 0 if is_y else x_at
+            keep2 = x_at if is_y else 0
+            gbuf[b, keep, keep2] = (gbuf[b, keep, keep2].astype(F32) + r2[b].astype(F32)).astype(BF16)
+            for k in range(n_wo - 1):
+                copy_z(b, is_y, k).start()
+
+        by_kind(b, go)
+
+    def stage_three(b):
+        for k in range(n_wo - 1):
+            copy_z(b, False, k).wait_recv()
+
+        def go(is_y):
+            keep = 0 if is_y else x_at
+            keep2 = x_at if is_y else 0
+            total = gbuf[b, keep, keep2, wo_at].astype(F32)
+            for k in range(n_wo - 1):
+                total = total + zr[b, k].astype(F32)
+            share[b] = total
+
+        by_kind(b, go)
+
+    def advance(j):
+        @pl.when(j < blocks)
+        def _():
+            stage_one(j)
+
+        @pl.when((j >= 1) & (j < blocks + 1))
+        def _():
+            stage_two(j - 1)
+
+        @pl.when((j >= 2) & (j < blocks + 2))
+        def _():
+            stage_three(j - 2)
+
+    def put(b, g, value):
+        for j in range(2 * n_wo):
+            rows = value[j * own_rows:(j + 1) * own_rows].astype(BF16)
+            px, w = j % 2, j // 2
+
+            @pl.when(b % 4 == 1)
+            def _():
+                gbuf[b, g, px, w] = rows
+
+            @pl.when(b % 4 != 1)
+            def _():
+                gbuf[b, px, g, w] = rows
+
+    def pre_loads(w):
+        rows = pl.ds(w * win, win)
+        return [
+            pltpu.make_async_copy(src, dst, pre_sem.at[i])
+            for i, (src, dst) in enumerate((
+                (normed_in.at[rows], normw), (d2_in.at[rows], d2w), (recip_in.at[rows], recw), (dh_in.at[rows], dhw),
+                (tokens.at[pl.ds(y_at * half + w * win, win)], xw),
+            ))
+        ]
+
+    def win_loads(w):
+        rows, slot = pl.ds(w * win, win), w % 2
+        return [
+            pltpu.make_async_copy(proj_in.at[:, :, rows], projw.at[slot], win_sem.at[0, slot]),
+            pltpu.make_async_copy(att_in.at[:, rows], attw.at[slot], win_sem.at[1, slot]),
+        ]
+
+    dh_copy = remote(dh_in, dhr, dh_s.at[0], dh_r.at[0], "core", 1 - c_at)
+    quarter = half // 2
+    near = pl.ds(y_at * half + c_at * quarter, quarter)
+    near_in = pl.ds((1 - y_at) * half + c_at * quarter, quarter)
+    out_y = remote(block_out.at[near], block_out.at[near], bo_s.at[0], bo_r.at[0], "y", 1 - y_at)
+    out_c = remote(block_out.at[near_in], block_out.at[near_in], bo_s.at[1], bo_r.at[1], "core", 1 - c_at)
+
+    loads = [
+        pltpu.make_async_copy(src, dst, w_sem.at[i])
+        for i, (src, dst) in enumerate((
+            (wqkv, wqv.at[0]), (wqkv1, wqv.at[1]), (wout, wov.at[0]), (wout1, wov.at[1]), (lse_in, lsev),
+        ))
+    ]
+
+    def ffn_grads(ring, lhs_d, lhs_h):
+        lhs = [pltpu.make_async_copy(d2t_in, lhs_d, t_sem.at[0]), pltpu.make_async_copy(ht_in, lhs_h, t_sem.at[1])]
+        down_blocks = hidden // BLOCK
+        up_blocks = 2 * hidden // BLOCK
+
+        def fetch(src, b, g):
+            return pltpu.make_async_copy(src.at[g, :, pl.ds(pl.multiple_of(b * BLOCK, BLOCK), BLOCK)],
+                                         ring.at[b % 2, g], ring_sem.at[b % 2, g])
+
+        def run(src, left, count, first):
+            for g in range(2):
+                fetch(src, 0, g).start()
+
+            def one(b, carry):
+                @pl.when(b + 1 < count)
+                def _():
+                    for g in range(2):
+                        fetch(src, b + 1, g).start()
+
+                for g in range(2):
+                    fetch(src, b, g).wait()
+                    put(b + first, g, dot(left[...], ring[b % 2, g]))
+
+                @pl.when(b + first < FLIGHT)
+                def _():
+                    by_kind(b + first, lambda is_y: copy_one(b + first, is_y).start())
+
+                return carry
+
+            lax.fori_loop(0, count, one, 0)
+
+        lhs[0].start()
+        dh_copy.start()
+        out_y.start()
+        lhs[1].start()
+        for copy in loads + pre_loads(0) + win_loads(0):
+            copy.start()
+        lhs[0].wait()
+        run(act_in, lhs_d, down_blocks, 0)
+        lhs[1].wait()
+        run(dgu_in, lhs_h, up_blocks, down_blocks)
+
+    pl.run_scoped(ffn_grads, pltpu.VMEM((2, 2, half, BLOCK), BF16), pltpu.VMEM((d, half), BF16), pltpu.VMEM((d, half), BF16))
+
+    for load in loads:
+        load.wait()
+    dh_copy.wait_recv()
+    lanes = head_lanes(width)
+    stat_lane = lax.broadcasted_iota(jnp.int32, (1, 128), 1)
+
+    def part_copy(w):
+        return remote(ipown.at[w], iprecv.at[w], ip_s.at[w], ip_r.at[w], "core", 1 - c_at)
+
+    side = win // 2
+
+    def own_copy(w):
+        return pltpu.make_async_copy(totb.at[w], input_grad.at[pl.ds(y_at * half + w * win, win)], tot_sem.at[w])
+
+    def in_y(w):
+        return remote(totb.at[w, pl.ds(c_at * side, side)], input_grad.at[pl.ds(y_at * half + w * win + c_at * side, side)],
+                      iy_s.at[w], iy_r.at[w], "y", 1 - y_at)
+
+    def in_c(w):
+        rows = pl.ds((1 - y_at) * half + w * win + c_at * side, side)
+        return remote(input_grad.at[rows], input_grad.at[rows], ic_s.at[w], ic_r.at[w], "core", 1 - c_at)
+
+    def attention(acc, xt, d1t, d1b, d1w, iptot, dist, stage):
+        fill_distance(dist)
+        acc[...] = jnp.zeros_like(acc)
+        sum1[...] = jnp.zeros_like(sum1)
+
+        def send_total(w):
+            part_copy(w).wait_recv()
+            value = d1w[w % 2] + (ipown[w].astype(F32) + iprecv[w].astype(F32))
+            totb[w] = value.astype(BF16)
+            own_copy(w).start()
+            in_y(w).start()
+
+        def step(t, carry):
+            w, g = t // 2, t % 2
+            slot = w % 2
+
+            @pl.when(g == 0)
+            def _():
+                for copy in pre_loads(w) + win_loads(w):
+                    copy.wait()
+                normed = normw[...]
+                dh = d2w[...] + (dhw[...].astype(F32) + dhr[pl.ds(w * win, win)].astype(F32))
+                d1 = norm_grad(dh, normed, recw[:, 0:1], nb[0:1])
+                d1w[slot] = d1
+                low = d1.astype(BF16)
+                d1b[...] = low
+                d1t[...] = low.T
+                xt[...] = xw[...].T
+                sum1[...] += rows_of_sums([dh * normed, dh, d1])
+
+                @pl.when(w + 1 < nwin)
+                def _():
+                    for copy in pre_loads(w + 1) + win_loads(w + 1):
+                        copy.start()
+
+            q, k, v = projw[slot, g, 0], projw[slot, g, 1], projw[slot, g, 2]
+            att = attw[slot, g]
+            datt = dot_nt(d1b[...], wov[g]).astype(BF16)
+            product = datt.astype(F32) * att.astype(F32)
+            stat = jnp.zeros((win, 128), F32)
+            for h in range(heads):
+                inner = jnp.sum(jnp.where(lanes[h], product, 0.0), axis=1, keepdims=True)
+                stat = jnp.where(stat_lane == h, inner, stat)
+            inner_rows = stat.T[0:8]
+            qs = q * jnp.asarray(SCALE, BF16)
+            dq = jnp.zeros((win, width), F32)
+            dks, dvs = [], []
+            half_keys = win // 2
+            limit = lengths[y_at * nwin + w]
+            for kb in range(2):
+                keys = slice(kb * half_keys, (kb + 1) * half_keys)
+                kk, vk = k[keys], v[keys]
+                key_on = lax.broadcasted_iota(jnp.int32, (half_keys, 1), 0) + kb * half_keys < limit
+                dk = jnp.zeros((half_keys, width), F32)
+                dv = jnp.zeros((half_keys, width), F32)
+                for h in range(heads):
+                    qh = jnp.where(lanes[h], qs, jnp.zeros_like(qs))
+                    oh = jnp.where(lanes[h], datt, jnp.zeros_like(datt))
+                    s = dot_nt(kk, qh) - slopes[g * heads + h] * dist[keys]
+                    s = jnp.where(key_on, s, NEG)
+                    p = jnp.exp(s - lsev[g, w, h:h + 1, :])
+                    dp = dot_nt(vk, oh)
+                    ds = (p * (dp - inner_rows[h:h + 1, :])).astype(BF16)
+                    dv = jnp.where(lanes[h], dot(p.astype(BF16), datt), dv)
+                    dk = jnp.where(lanes[h], dot(ds, q), dk)
+                    dq = dq + jnp.where(lanes[h], dot_tn(ds, kk), 0.0)
+                dks.append((dk * SCALE).astype(BF16))
+                dvs.append(dv.astype(BF16))
+            dqb = (dq * SCALE).astype(BF16)
+            dkb = jnp.concatenate(dks, axis=0)
+            dvb = jnp.concatenate(dvs, axis=0)
+            acc[g, 0] += dot(xt[...], dqb)
+            acc[g, 1] += dot(xt[...], dkb)
+            acc[g, 2] += dot(xt[...], dvb)
+            acc[g, 3] += dot(d1t[...], att)
+            term = dot_nt(dqb, wqv[g, 0]) + dot_nt(dkb, wqv[g, 1]) + dot_nt(dvb, wqv[g, 2])
+
+            @pl.when(g == 0)
+            def _():
+                iptot[...] = term
+
+            @pl.when(g == 1)
+            def _():
+                ipown[w] = (iptot[...] + term).astype(BF16)
+                part_copy(w).start()
+
+            @pl.when((g == 0) & (w > 0))
+            def _():
+                send_total(w - 1)
+
+            advance(t)
+
+            @pl.when(t == 3)
+            def _():
+                out_y.wait_recv()
+                out_c.start()
+
+            return carry
+
+        lax.fori_loop(0, 2 * nwin, step, 0)
+
+        first = blocks - 4 * width // BLOCK
+        for g in range(2):
+            for i in range(4):
+                stage[:, i * width:(i + 1) * width] = acc[g, i].astype(BF16)
+            for i in range(4 * width // BLOCK):
+                put(first + i, g, stage[:, i * BLOCK:(i + 1) * BLOCK])
+        for i in range(first, min(2 * nwin + FLIGHT, blocks)):
+            copy_one(i, i % 4 == 1).start()
+        send_total(nwin - 1)
+
+    pl.run_scoped(
+        attention,
+        pltpu.VMEM((2, 4, d, width), F32), pltpu.VMEM((d, win), BF16), pltpu.VMEM((d, win), BF16), pltpu.VMEM((win, d), BF16),
+        pltpu.VMEM((2, win, d), F32), pltpu.VMEM((win, d), F32), pltpu.VMEM((win, win), F32), pltpu.VMEM((d, 4 * width), BF16),
+    )
+
+    sumb[0] = jnp.concatenate([sum1[0:3], sums2[0:3], jnp.zeros((2, d), F32)], axis=0)
+
+    def sum_copy(i, axis):
+        return remote(sumb.at[i], sumr.at[i], sm_s.at[i], sm_r.at[i], axis, 1 - at[axis])
+
+    def sum_z(k):
+        to = (wo_at + k + 1) % n_wo
+        return remote(sumb.at[2], sumz.at[k], smz_s.at[k], smz_r.at[k], "wo", to)
+
+    sum_copy(0, "y").start()
+
+    def tail(i, carry):
+        j = 2 * nwin + i
+        advance(j)
+
+        @pl.when(i < nwin)
+        def _():
+            in_y(i).wait_recv()
+            in_c(i).start()
+
+        @pl.when(i == 0)
+        def _():
+            sum_copy(0, "y").wait_recv()
+            sumb[1] = sumb[0] + sumr[0]
+            sum_copy(1, "x").start()
+
+        @pl.when(i == 1)
+        def _():
+            sum_copy(1, "x").wait_recv()
+            sumb[2] = sumb[1] + sumr[1]
+            for k in range(n_wo - 1):
+                sum_z(k).start()
+
+        return carry
+
+    lax.fori_loop(0, blocks + 2 - 2 * nwin, tail, 0)
+    total = sumb[2]
+    for k in range(n_wo - 1):
+        sum_z(k).wait_recv()
+        total = total + sumz[k]
+    total_sums[...] = total
+
+    out_c.wait_recv()
+    out_y.wait_send()
+    out_c.wait_send()
+    dh_copy.wait_send()
+    for i, axis in ((0, "y"), (1, "x")):
+        sum_copy(i, axis).wait_send()
+    for k in range(n_wo - 1):
+        sum_z(k).wait_send()
+
+    def drain_window(w, carry):
+        part_copy(w).wait_send()
+        own_copy(w).wait()
+        in_y(w).wait_send()
+        in_c(w).wait_send()
+        in_c(w).wait_recv()
+        return carry
+
+    lax.fori_loop(0, nwin, drain_window, 0)
+
+    def drain_block(b, carry):
+        copy_one(b, False).wait_send()
+        copy_two(b, False).wait_send()
+        for k in range(n_wo - 1):
+            copy_z(b, False, k).wait_send()
+        return carry
+
+    lax.fori_loop(0, blocks, drain_block, 0)
+
+
+def backward(n_wo, lengths, slopes, nb, sums2, tokens, d2, dh, normed, recip, wqkv, wqkv1, wout, wout1,
+             proj, att, lse, dgu, act, ht, d2t, half_out):
+    half, d = normed.shape
+    _, nwin, _, win = lse.shape
+    width, hidden = wout.shape[0], act.shape[2]
+    rows = d // (2 * n_wo)
+    blocks = (3 * hidden + 4 * width) // BLOCK
+    heads = width // HEAD_DIM
+    smem = pl.BlockSpec(memory_space=pltpu.SMEM)
+    vmem = pl.BlockSpec(memory_space=pltpu.VMEM)
+    hbm = pl.BlockSpec(memory_space=pl.ANY)
+    outs = [((blocks, rows, BLOCK), F32), ((8, d), F32), (tokens.shape, BF16), (tokens.shape, BF16)]
+    bufs = [
+        ((blocks, 2, 2, n_wo, rows, BLOCK), BF16), ((blocks, 2, n_wo, rows, BLOCK), BF16), ((blocks, n_wo, rows, BLOCK), BF16),
+        ((blocks, n_wo - 1, rows, BLOCK), BF16), ((half, d), BF16), ((win, d), BF16), ((win, d), F32), ((win, d), F32),
+        ((win, 128), F32), ((win, d), BF16), ((2, 2, 3, win, width), BF16), ((2, 2, win, width), BF16), (lse.shape, F32),
+        ((2,) + wqkv.shape, BF16), ((2,) + wout.shape, BF16), ((nwin, win, d), BF16), ((nwin, win, d), BF16),
+        ((nwin, win, d), BF16), ((3, 8, d), F32), ((2, 8, d), F32), ((n_wo - 1, 8, d), F32), ((8, d), F32),
+    ]
+    sems = [(blocks,)] * 4 + [(blocks, n_wo - 1)] * 2 + [(5,), (2, 2), (5,), (1,), (1,)] + [(nwin,)] * 7
+    sems += [(2,), (2,), (2,), (2,), (n_wo - 1,), (n_wo - 1,), (2, 2), (2,)]
+    return pl.pallas_call(
+        backward_kernel,
+        in_specs=[smem, smem, vmem, vmem] + [hbm] * 17,
+        out_specs=[vmem, vmem, hbm, hbm],
+        input_output_aliases={20: 2},
+        out_shape=[jax.ShapeDtypeStruct(*o) for o in outs],
+        scratch_shapes=[pltpu.VMEM(*b) for b in bufs] + [pltpu.SemaphoreType.DMA(n) for n in sems],
+        compiler_params=pltpu.CompilerParams(vmem_limit_bytes=63 * 1024 * 1024, collective_id=1, has_side_effects=True),
+        cost_estimate=pl.CostEstimate(
+            flops=2 * half * d * width * 16 + 12 * half * d * hidden + 20 * nwin * heads * win * win * 256,
+            bytes_accessed=half * d * 60 + half * hidden * 12, transcendentals=2 * nwin * heads * win * win,
+        ),
+        name="backward",
+    )(lengths, slopes, nb, sums2, tokens, d2, dh, normed, recip, wqkv, wqkv1, wout, wout1,
+      proj, att, lse, dgu, act, ht, d2t, half_out)
+
+
 SWAP = [(0, 1), (1, 0)]
 WIDE = ("wo", "x")
 
@@ -831,6 +1092,15 @@
 
 def after(value, *others):
     return lax.optimization_barrier((value, *others))[0]
+
+
+def weight_shares(columns, hidden, width):
+    down_share = columns[:, :hidden].T
+    up_share = jnp.stack([columns[:, hidden:2 * hidden], columns[:, 2 * hidden:3 * hidden]])
+    start = 3 * hidden
+    qkv_share = jnp.stack([columns[:, start + i * width:start + (i + 1) * width] for i in range(3)])
+    out_share = columns[:, start + 3 * width:].T
+    return qkv_share, out_share, up_share, down_share
 
 
 def shards(tokens, wqkv, wout, nb, up, down, lengths, cot):
@@ -842,18 +1112,27 @@
     slopes = 2.0 ** (-8.0 * (heads + 1).astype(F32) / HEADS)
     info = jnp.concatenate([y_at[None].astype(jnp.int32), lengths])
 
-    (proj, att, lse, normed, recip, hb, a_all, b_all, act, fpart, fpart_other,
+    (proj, att, lse, normed, recip, ht, a_all, b_all, act, fpart, fpart_other,
      wqkv1, wout1, up1, down1) = forward(lengths, slopes, nb, tokens, wqkv, wout, up, down)
-    act0, act1 = act[0], act[1]
-    out, d2, d2b, dgu0, dgu1, dh, sums2 = ffn_bwd(
+    out, d2, d2t, dgu, dh, sums2 = ffn_bwd(
         info, fpart, fpart_other, normed, cot, nb, up, up1, down, down1, a_all, b_all
     )
+    wo = lax.axis_size("wo")
+    width, hidden = wqkv.shape[2], down.shape[0]
+    if (d // (2 * wo)) % 16 == 0:
+        share, sums, block_out, input_low = backward(
+            wo, lengths, slopes, nb, sums2, tokens, d2, dh, normed, recip, wqkv, wqkv1, wout, wout1,
+            proj, att, lse, dgu, act, ht, d2t, out,
+        )
+        columns = jnp.concatenate(list(share), axis=1)
+        small_share = lax.dynamic_slice_in_dim(sums[:6], (lax.axis_index("wo") * 2 + x_at) * (d // (2 * wo)), d // (2 * wo), 1)
+        return (block_out, input_low.astype(F32), *weight_shares(columns, hidden, width), small_share)
+
+    out = lax.dynamic_slice_in_dim(out, y_at * (out.shape[0] // 2), out.shape[0] // 2, 0)
     dh_other = swap(dh, "core")
 
     def grad(a, b):
-        return lax.dot_general(a, b, (((0,), (0,)), ((), ())), preferred_element_type=F32).astype(BF16)
-
-    wo = lax.axis_size("wo")
+        return lax.dot_general(a, b, (((1,), (0,)), ((), ())), preferred_element_type=F32).astype(BF16)
 
     def part_of(value, at):
         split = value.reshape(wo, 2, -1, value.shape[1])
@@ -862,12 +1141,12 @@
     def add(a, b):
         return a.astype(F32) + b.astype(F32)
 
-    down_peer = grad(d2b, act1)
+    down_peer = grad(d2t, act[1])
     down_peer_in = swap(down_peer, "y")
-    up_peer = grad(hb, dgu1)
-    up_own = grad(hb, dgu0)
+    up_peer = grad(ht, dgu[1])
+    up_own = grad(ht, dgu[0])
     up_in = swap(jnp.concatenate([part_of(up_own, 1 - x_at), part_of(up_peer, 1 - x_at)], axis=0), "x")
-    down_own = grad(d2b, act0)
+    down_own = grad(d2t, act[0])
 
     quarter = out.shape[0] // 2
     order = jnp.stack([2 * y_at, 2 * y_at + 1, 2 * (1 - y_at) + c_at, 2 * (1 - y_at) + 1 - c_at]).astype(jnp.int32)
@@ -898,21 +1177,13 @@
     attn_half = add(add(part_of(agrad0, x_at), attn_in[:n]), swap(attn_peer_half, "y")).astype(BF16)
 
     scatter = functools.partial(lax.psum_scatter, axis_name="wo", scatter_dimension=0, tiled=True)
-    ffn_share = scatter(jnp.concatenate([down_half, up_half], axis=1)).astype(F32)
-    hidden = down.shape[0]
-    down_share = ffn_share[:, :hidden].T
-    up_share = jnp.stack([ffn_share[:, hidden:2 * hidden], ffn_share[:, 2 * hidden:]])
-    attn_share = scatter(attn_half).astype(F32)
-    width = wqkv.shape[2]
-    qkv_share = jnp.stack([attn_share[:, i * width:(i + 1) * width] for i in range(3)])
-    out_share = attn_share[:, 3 * width:].T
-
+    columns = jnp.concatenate([scatter(jnp.concatenate([down_half, up_half], axis=1)), scatter(attn_half)], axis=1).astype(F32)
     small = jnp.concatenate([sums1[:3], sums2[:3]], axis=0)
     small_share = lax.psum_scatter(lax.psum(small, "y"), WIDE, scatter_dimension=1, tiled=True)
 
     block_out = place(order, out, near_out, swap(near_out, "core"), BF16)
     input_grad = place(order, total, near_in, swap(near_in, "core"), F32)
-    return (block_out, input_grad, qkv_share, out_share, up_share, down_share, small_share)
+    return (block_out, input_grad, *weight_shares(columns, hidden, width), small_share)
 
 
 def solution(mesh):

time: 376 us -> 279 us (0.74)
  waiting for transfers between devices: 132 us -> 0 us
  Pallas kernels: 160 us -> 257 us
  matrix products: 17.7 us -> 0 us
  between operations: 14 us -> 0.69 us
  other arithmetic: 22.4 us -> 11.6 us
  starting transfers between devices: 9.94 us -> 0 us
  blocking collectives: 5.52 us -> 0 us
  local copies, waits for them, and re-layouts: 13.5 us -> 8.04 us
    pallas_call x3 -> x1, Pallas kernels: 52.8 us -> 150 us  [backward(): pl.pallas_call(backward_kernel, in_specs=[smem, smem, vmem, vmem] + [hbm]...]
    ppermute x12 -> x0, waiting for transfers between devices: 92.4 us -> none  [swap(): return lax.ppermute(value, axis, SWAP)]
    reduce_scatter x2 -> x0, waiting for transfers between devices: 39.9 us -> none  [the longest x1 36.6 us: shards(): scatter(jnp.concatenate([down_half, up_half], axis=1)).astype(F32)]
    dot_general x4 -> x0, matrix products: 17.7 us -> none  [grad(): lax.dot_general(a, b, (((0,), (0,)), ((), ())), preferred_element_type=F32)]
    ppermute x12 -> x0, starting transfers between devices: 9.82 us -> none  [swap(): return lax.ppermute(value, axis, SWAP)]
    convert_element_type x8 -> x1, other arithmetic: 14.6 us -> 7.28 us  [shards(): input_low.astype(F32)]
    psum x1 -> x0, blocking collectives: 5.52 us -> none  [shards(): lax.psum(small, 'y')]
    dynamic_slice x7 -> x1, local copies, waits for them, and re-layouts: 5.78 us -> 1.37 us  [shards(): lax.dynamic_slice_in_dim(sums[:6], (lax.axis_index('wo') * 2 + x_at) * (d...]
  transfers between devices with their start and end apart: 15 -> 0, of which waited for: 7 -> 0; matrix products, arithmetic and copies ran while one was open for 12% -> 0% of each run, Pallas kernels for 12% -> 0%
where the time goes in v3:
time: 279 us; the launch traced here: 277 us
  Pallas kernels  257 us (92%)
  other arithmetic  11.6 us (4%)
  local copies, waits for them, and re-layouts  8.04 us (3%)
    pallas_call x1, Pallas kernels, backward(): pl.pallas_call(backward_kernel, in_specs=[smem, smem, vmem, vmem] + [hbm]...  150 us
    pallas_call x1, Pallas kernels, forward(): pl.pallas_call(forward_kernel, in_specs=[smem, smem, vmem] + [hbm] * 5, o...  80.3 us
    pallas_call x1, Pallas kernels, ffn_bwd(): pl.pallas_call(ffn_bwd_kernel, grid_spec=pltpu.PrefetchScalarGridSpec(num...  27.2 us
    convert_element_type x1, other arithmetic, shards(): input_low.astype(F32)  7.28 us

profile of v3, /device:TPU:0, one launch (start us, length us, event | category | flops | bytes accessed | tf_op | source)
XLA Modules:
  0.0 277.4 jit_solution(3529161821407007480)
XLA Ops:
  0.6 1.2 pad_add_fusion.info
  1.9 0.6 fusion.4.slopes
  2.5 2.3 copy.16.wqkv
  4.8 80.3 %forward.1 = (bf16[2,3,1536,192]{3,2,1,0:T(8,128)(2,1)}, bf16[2,1536,192]{2,1,0:T(8,128)(2,1)}, f32[2,3,8,512]{3,2,1,0:T(8,128)}, f32[1536,768]{1,0:T(8,128)}, f...) custom-call(s32[6]{0:T(128)} %lengths.1, ...), custom_call_target="tpu_custom_call" | custom-call | flops 22951231488 | bytes 49545216 | tf_op jit(solution)/shard_map/forward/pallas_call | solution.py:625
  85.1 27.2 %ffn_bwd.1 = (bf16[3072,768]{1,0:T(8,128)(2,1)}, f32[1536,768]{1,0:T(8,128)}, bf16[768,1536]{1,0:T(8,128)(2,1)}, bf16[2,1536,1536]{2,1,0:T(8,128)(2,1)}, bf16[1536,768]{1,0:T(8,128)(2,1)}, /*index=5*/f32[8,768]{1,0:T(8,128)}) custom-call(s32[7]{0:T(128)} %pad_add_fusion.info, bf16[1536,768]{1,0:T(8,128)(2,1)} %get-tuple-element.32.pa, ...), custom_call_target="tpu_custom_call" | custom-call | flops 10871635968 | bytes 49545216 | tf_op jit(solution)/shard_map/ffn_bwd/pallas_call | solution.py:113
  112.4 149.5 %backward.1 = (f32[12,96,256]{2,1,0:T(8,128)}, f32[8,768]{1,0:T(8,128)}, bf16[3072,768]{1,0:T(8,128)(2,1)}, bf16[3072,768]{1,0:T(8,128)(2,1)}) custom-call(s32[6]{0:T(128)} %lengths.1, f32[6]{0:T(128)} %fusion.4.slopes, f32[6,768]{1,0:T(8,128)} %nb.5, f32[8,768]{1,0:T(8,128)} %get-tuple-element.39.sums2, ...), custom_call_target="tpu_custom_call", output_to_operand_aliasing={{2}: (20, {})} | custom-call | flops 30198988800 | bytes 84934656 | tf_op jit(solution)/shard_map/backward/pallas_call | solution.py:1068
  261.9 1.4 constant_dynamic-slice_fusion
  263.3 1.4 slice_bitcast_fusion.4
  264.7 0.7 maximum_bitcast_fusion.2
  265.5 0.9 pad_maximum_fusion
  266.3 0.1 slice_bitcast_fusion
  266.4 0.7 copy.18
  267.2 0.0 slice-start
  267.2 0.7 pad_maximum_fusion.1
  267.9 0.0 slice-start.1
  267.9 7.3 %convert_element_type.7 = f32[3072,768]{1,0:T(8,128)} convert(bf16[3072,768]{1,0:T(8,128)(2,1)} %get-tuple-element.54) | non-fusion elementwise | flops 2359296 | bytes 14155776 | tf_op jit(solution)/shard_map/convert_element_type | solution.py:1129
  275.2 0.0 slice-done
  275.2 0.0 slice-done.1
  275.2 2.2 copy.21
  (4 shorter events, 0.0 us)
Async XLA Ops:
  267.2 8.0 %slice-start = ((s8[4718592]{0:T(1024)(128)(4,1)}), s8[4194304]{0:T(1024)(128)(4,1)S(1)}, s32[]{:S(2)}) async-start(s8[4718592]{0:T(1024)(128)(4,1)} %bitcast.40), calls=%async_computation | async-start | bytes 8388608
  267.9 7.3 %slice-start.1 = ((s8[4718592]{0:T(1024)(128)(4,1)}), s8[524288]{0:T(1024)(128)(4,1)S(1)}, s32[]{:S(2)}) async-start(s8[4718592]{0:T(1024)(128)(4,1)} %bitcast.40), calls=%async_computation.1 | async-start | bytes 1048576

commit v4 on v3

--- a/solution.py
+++ b/solution.py
@@ -15,6 +15,7 @@
 BF16 = jnp.bfloat16
 SCALE = 1.0 / math.sqrt(HEAD_DIM)
 NEG = -1e30
+MESH_ID = pl.DeviceIdType.MESH
 VMEM_LIMIT = 56 * 1024 * 1024
 
 
@@ -50,6 +51,10 @@
     return pltpu.CompilerParams(vmem_limit_bytes=VMEM_LIMIT, dimension_semantics=("arbitrary",))
 
 
+def remote(src, dst, send, recv, axis, peer):
+    return pltpu.make_async_remote_copy(src, dst, send, recv, device_id={axis: peer}, device_id_type=MESH_ID)
+
+
 def standardize(value):
     center = value - jnp.mean(value, axis=1, keepdims=True)
     recip = lax.rsqrt(jnp.mean(center * center, axis=1, keepdims=True) + EPS)
@@ -68,14 +73,38 @@
     return jnp.concatenate(sums + [jnp.zeros((8 - len(sums), width), F32)], axis=0)
 
 
-def ffn_bwd_kernel(info, pa, pb, normed_ref, cot, nb, up0, up1, down0, down1, a_all, b_all,
-                   out_ref, d2_ref, d2t_ref, dgu, dh_ref, sums_ref):
+def ffn_bwd_kernel(pa, pb, normed_ref, cot, nb, up0, up1, down0, down1, a_all, b_all,
+                   block_out, d2_ref, d2t_ref, dgu, dh_ref, sums_ref, outb, own_sem, ysend, yrecv):
     hidden = down0.shape[0]
+    i = pl.program_id(0)
+    n, tile, _ = outb.shape
+    y_at, c_at = lax.axis_index("y"), lax.axis_index("core")
+
+    @pl.when(i == 0)
+    def _():
+        barrier = pltpu.get_barrier_semaphore()
+        pl.semaphore_signal(barrier, inc=1, device_id={"y": 1 - y_at}, device_id_type=MESH_ID)
+        pl.semaphore_wait(barrier, 1)
+
+    def own_copy(t):
+        return pltpu.make_async_copy(outb.at[t], block_out.at[pl.ds((y_at * n + t) * tile, tile)], own_sem.at[t])
+
+    def side_copy(t):
+        side = tile // 2
+        return remote(outb.at[t, pl.ds(c_at * side, side)], block_out.at[pl.ds((y_at * n + t) * tile + c_at * side, side)],
+                      ysend.at[t], yrecv.at[t], "y", 1 - y_at)
+
     h = normed_ref[...] * nb[0:1] + nb[1:2]
     second = pa[...].astype(F32) + pb[...].astype(F32) + nb[5:6] + h
     normed, recip = standardize(second)
     gain = nb[3:4]
-    out_ref[...] = (normed * gain + nb[4:5]).astype(BF16)
+    outb[i] = (normed * gain + nb[4:5]).astype(BF16)
+    own_copy(i).start()
+
+    @pl.when(i < n - 1)
+    def _():
+        side_copy(i).start()
+
     c = cot[...].astype(F32)
     d2 = norm_grad(c, normed, recip, gain)
     d2_ref[...] = d2
@@ -92,7 +121,7 @@
         sums_ref[...] += sums
 
     total = None
-    step = 256
+    step = 768
     for g, (up, down) in enumerate(((up0, down0), (up1, down1))):
         for at in range(0, hidden, step):
             cols = slice(at, at + step)
@@ -104,31 +133,39 @@
             total = term if total is None else total + term
     dh_ref[...] = total.astype(BF16)
 
-
-def ffn_bwd(info, pa, pb, normed, cot, nb, up0, up1, down0, down1, a_all, b_all, tile=256):
+    @pl.when(i == n - 1)
+    def _():
+        for t in range(n):
+            own_copy(t).wait()
+        for t in range(n - 1):
+            side_copy(t).wait()
+
+
+def ffn_bwd(tile, pa, pb, normed, cot, nb, up0, up1, down0, down1, a_all, b_all):
     half, d = pa.shape
     hidden = down0.shape[0]
     n = half // tile
     row = lambda w: pl.BlockSpec((tile, w), lambda i, *_: (i, 0))
     return pl.pallas_call(
         ffn_bwd_kernel,
-        grid_spec=pltpu.PrefetchScalarGridSpec(
-            num_scalar_prefetch=1,
-            grid=(n,),
-            in_specs=[
-                row(d), row(d), row(d),
-                pl.BlockSpec((tile, d), lambda i, info: (info[0] * n + i, 0)),
-                whole(nb.shape),
-                whole(up0.shape), whole(up1.shape), whole(down0.shape), whole(down1.shape),
-                pl.BlockSpec((2, tile, hidden), lambda i, *_: (0, i, 0)),
-                pl.BlockSpec((2, tile, hidden), lambda i, *_: (0, i, 0)),
-            ],
-            out_specs=[
-                pl.BlockSpec((tile, d), lambda i, info: (info[0] * n + i, 0)), row(d),
-                pl.BlockSpec((d, tile), lambda i, *_: (0, i)),
-                pl.BlockSpec((2, tile, 2 * hidden), lambda i, *_: (0, i, 0)), row(d), whole((8, d)),
-            ],
-        ),
+        grid=(n,),
+        in_specs=[
+            row(d), row(d), row(d),
+            pl.BlockSpec((tile, d), lambda i: (lax.axis_index("y") * n + i, 0)),
+            whole(nb.shape),
+            whole(up0.shape), whole(up1.shape), whole(down0.shape), whole(down1.shape),
+            pl.BlockSpec((2, tile, hidden), lambda i: (0, i, 0)),
+            pl.BlockSpec((2, tile, hidden), lambda i: (0, i, 0)),
+        ],
+        out_specs=[
+            pl.BlockSpec(memory_space=pl.ANY), row(d),
+            pl.BlockSpec((d, tile), lambda i: (0, i)),
+            pl.BlockSpec((2, tile, 2 * hidden), lambda i: (0, i, 0)), row(d), whole((8, d)),
+        ],
+        scratch_shapes=[
+            pltpu.VMEM((n, tile, d), BF16), pltpu.SemaphoreType.DMA((n,)), pltpu.SemaphoreType.DMA((n - 1,)),
+            pltpu.SemaphoreType.DMA((n - 1,)),
+        ],
         out_shape=[
             jax.ShapeDtypeStruct((2 * half, d), BF16),
             jax.ShapeDtypeStruct((half, d), F32),
@@ -137,13 +174,15 @@
             jax.ShapeDtypeStruct((half, d), BF16),
             jax.ShapeDtypeStruct((8, d), F32),
         ],
-        compiler_params=params(),
+        compiler_params=pltpu.CompilerParams(
+            vmem_limit_bytes=VMEM_LIMIT, dimension_semantics=("arbitrary",), collective_id=2, has_side_effects=True
+        ),
         cost_estimate=pl.CostEstimate(
             flops=12 * half * d * hidden, bytes_accessed=half * d * 20 + half * hidden * 16 + 12 * d * hidden,
             transcendentals=half,
         ),
         name="ffn_bwd",
-    )(info, pa, pb, normed, cot, nb, up0, up1, down0, down1, a_all, b_all)
+    )(pa, pb, normed, cot, nb, up0, up1, down0, down1, a_all, b_all)
 
 
 def attn_bwd_kernel(info, slopes, x_ref, d2_ref, ha, hb, normed_ref, recip_ref, nb, wqkv0, wqkv1, wout0, wout1,
@@ -218,7 +257,7 @@
             for i in range(4):
                 acc[i] += terms[i]
 
-        term = dot_nt(dqb, wqkv[0]) + dot_nt(dkb, wqkv[1]) + dot_nt(dvb, wqkv[2])
+        term = dot(dqb, wqkv[0]) + dot(dkb, wqkv[1]) + dot(dvb, wqkv[2])
         total = term if total is None else total + term
     part[...] = total.astype(BF16)
 
@@ -307,61 +346,73 @@
     )(order, mine, near, far)
 
 
-MESH_ID = pl.DeviceIdType.MESH
 TILE = 256
-
-
-def remote(src, dst, send, recv, axis, peer):
-    return pltpu.make_async_remote_copy(src, dst, send, recv, device_id={axis: peer}, device_id_type=MESH_ID)
 
 
 def forward_kernel(info, slopes, nb, tokens, wqkv, wout, up, down,
                    proj_out, att_out, lse_out, normed_out, recip_out, ht_out, a_out, b_out, act_out, fown_out, frecv_out,
                    wqkv1_out, wout1_out, up1_out, down1_out,
                    xbuf, wqv, wov, upv, downv, projb, attb, lseb, pown, precv, normedb, recipb, hbuf, htb, ab, bb, actb,
-                   facc, fown, frecv, dist,
-                   load_sem, ysend, yrecv, xsend, xrecv, psend, prem, fsend, frem, out_sem, pout_sem, tout_sem, fout_sem):
-    x_at, y_at, c_at = (lax.axis_index(n) for n in ("x", "y", "core"))
+                   facc, fown, dist,
+                   load_sem, ysend, yrecv, xsend, xrecv, zsend, zrecv, psend, prem, fsend, frem, out_sem, pout_sem, tout_sem, fout_sem):
+    wo_at, x_at, y_at, c_at = (lax.axis_index(n) for n in ("wo", "x", "y", "core"))
     nwin, _, win = lse_out.shape[1:]
     half, d = xbuf.shape
     width = wout.shape[0]
     hidden = down.shape[0]
     heads = width // HEAD_DIM
     tiles = half // TILE
+    z_at = wo_at % 2
+    z_peer = wo_at + 1 - 2 * z_at
 
     barrier = pltpu.get_barrier_semaphore()
-    for axis, at in (("x", x_at), ("y", y_at), ("core", c_at)):
-        pl.semaphore_signal(barrier, inc=1, device_id={axis: 1 - at}, device_id_type=MESH_ID)
-    pl.semaphore_wait(barrier, 3)
-
-    hd, hw, hf = d // 2, width // 2, hidden // 2
-
-    def pieces(at):
-        rows = pl.ds(at * hd, hd)
-        return (
-            (wqkv.at[0:2, rows], wqv.at[1, 0:2, rows]),
-            (wqkv.at[2:3, rows], wqv.at[1, 2:3, rows]),
-            (wout.at[pl.ds(at * hw, hw)], wov.at[1, pl.ds(at * hw, hw)]),
-            (up.at[at, 0:hd], upv.at[1, at, 0:hd]),
-            (up.at[at, hd:d], upv.at[1, at, hd:d]),
-            (down.at[pl.ds(at * hf, hf)], downv.at[1, pl.ds(at * hf, hf)]),
-        )
-
-    mine = pieces(x_at)
-    theirs = pieces(1 - x_at)
+    for axis, to in (("x", 1 - x_at), ("y", 1 - y_at), ("core", 1 - c_at), ("wo", z_peer)):
+        pl.semaphore_signal(barrier, inc=1, device_id={axis: to}, device_id_type=MESH_ID)
+    pl.semaphore_wait(barrier, 4)
+
+    def quarter(i, q):
+        if i == 0:
+            return wqkv.at[:, pl.ds(q * (width // 4), width // 4)], wqv.at[1, :, pl.ds(q * (width // 4), width // 4)]
+        if i == 1:
+            return wout.at[pl.ds(q * (width // 4), width // 4)], wov.at[1, pl.ds(q * (width // 4), width // 4)]
+        if i == 2:
+            return up.at[:, pl.ds(q * (d // 4), d // 4)], upv.at[1, :, pl.ds(q * (d // 4), d // 4)]
+        return down.at[pl.ds(q * (hidden // 4), hidden // 4)], downv.at[1, pl.ds(q * (hidden // 4), hidden // 4)]
+
+    def eighth(i, q, e):
+        if i == 0:
+            return wqv.at[1, :, pl.ds(q * (width // 4), width // 4), e * (d // 2):(e + 1) * (d // 2)]
+        if i == 1:
+            return wov.at[1, pl.ds(q * (width // 4), width // 4), e * (d // 2):(e + 1) * (d // 2)]
+        if i == 2:
+            return upv.at[1, :, pl.ds(q * (d // 4) + e * (d // 8), d // 8)]
+        return downv.at[1, pl.ds(q * (hidden // 4) + e * (hidden // 8), hidden // 8)]
+
+    here = 2 * x_at + z_at
+    across_x = 2 * (1 - x_at) + z_at
+    across_z = 2 * x_at + 1 - z_at
 
     def over_y(i):
-        return remote(mine[i][0], mine[i][1], ysend.at[i], yrecv.at[i], "y", 1 - y_at)
-
-    def over_x(i):
-        return remote(mine[i][1], mine[i][1], xsend.at[i], xrecv.at[i], "x", 1 - x_at)
-
-    def arriving_x(i):
-        return remote(theirs[i][1], theirs[i][1], xsend.at[i], xrecv.at[i], "x", 1 - x_at)
-
-    def pass_on(i):
-        over_y(i).wait_recv()
-        over_x(i).start()
+        src, dst = quarter(i, here)
+        return remote(src, dst, ysend.at[i], yrecv.at[i], "y", 1 - y_at)
+
+    def level_one(i):
+        _, ref = quarter(i, here)
+        return (remote(ref, ref, xsend.at[0, i], xrecv.at[0, i], "x", 1 - x_at),
+                remote(ref, ref, zsend.at[0, i], zrecv.at[0, i], "wo", z_peer))
+
+    def level_two(i):
+        from_z, from_x = eighth(i, across_z, 0), eighth(i, across_x, 1)
+        return (remote(from_z, from_z, xsend.at[1, i], xrecv.at[1, i], "x", 1 - x_at),
+                remote(from_x, from_x, zsend.at[1, i], zrecv.at[1, i], "wo", z_peer))
+
+    def launch(copies):
+        for copy in copies:
+            copy.start()
+
+    def arrive(copies):
+        for copy in copies:
+            copy.wait_recv()
 
     loads = [
         pltpu.make_async_copy(tokens.at[pl.ds(y_at * half, half)], xbuf, load_sem.at[0]),
@@ -370,8 +421,8 @@
         pltpu.make_async_copy(up, upv.at[0], load_sem.at[3]),
         pltpu.make_async_copy(down, downv.at[0], load_sem.at[4]),
     ]
-    for i in range(6):
-        over_y(i).start()
+    over_y(0).start()
+    over_y(1).start()
     for load in loads:
         load.start()
     fill_distance(dist)
@@ -396,9 +447,9 @@
         g, w = t // nwin, t % nwin
         start = w * win
         x = xbuf[pl.ds(start, win)]
-        q = dot(x, wqv[g, 0]).astype(BF16)
-        k = dot(x, wqv[g, 1]).astype(BF16)
-        v = dot(x, wqv[g, 2]).astype(BF16)
+        q = dot_nt(x, wqv[g, 0]).astype(BF16)
+        k = dot_nt(x, wqv[g, 1]).astype(BF16)
+        v = dot_nt(x, wqv[g, 2]).astype(BF16)
         projb[g, 0, pl.ds(start, win)] = q
         projb[g, 1, pl.ds(start, win)] = k
         projb[g, 2, pl.ds(start, win)] = v
@@ -430,20 +481,26 @@
             pown[pl.ds(start, win)] = out.astype(BF16)
             part_copy(w).start()
 
-        @pl.when(t == nwin - 2)
-        def _():
-            pass_on(0)
+        @pl.when(t == 0)
+        def _():
+            for i in range(2):
+                over_y(i).wait_recv()
+                launch(level_one(i))
+            over_y(2).start()
 
         @pl.when(t == nwin - 1)
         def _():
-            pass_on(1)
-            pass_on(2)
-            for i in range(3):
-                arriving_x(i).wait_recv()
-
-        @pl.when(t == 2 * nwin - 2)
-        def _():
-            pass_on(3)
+            over_y(3).start()
+            for i in range(2):
+                arrive(level_one(i))
+                launch(level_two(i))
+            for i in range(2):
+                arrive(level_two(i))
+
+        @pl.when(t == nwin)
+        def _():
+            over_y(2).wait_recv()
+            launch(level_one(2))
 
         return carry
 
@@ -501,34 +558,38 @@
         for copy in tile_copies(i) + norm_copies(i):
             copy.start()
 
-        @pl.when(i == 1)
-        def _():
-            pass_on(4)
-
-        @pl.when(i == tiles - 1)
-        def _():
-            pass_on(5)
+        @pl.when(i == tiles // 2 - 1)
+        def _():
+            arrive(level_one(2))
+            launch(level_two(2))
+            over_y(3).wait_recv()
 
         return carry
 
     lax.fori_loop(0, tiles, first, 0)
-    arriving_x(3).wait_recv()
-    arriving_x(4).wait_recv()
+    launch(level_one(3))
+    arrive(level_two(2))
 
     def second(i, carry):
         start = i * TILE
         hidden_units(1, start, hbuf[pl.ds(start, TILE)])
         for copy in tile_copies(tiles + i):
             copy.start()
+
+        @pl.when(i == tiles - 2)
+        def _():
+            arrive(level_one(3))
+            launch(level_two(3))
+
         return carry
 
     lax.fori_loop(0, tiles, second, 0)
-    arriving_x(5).wait_recv()
+    arrive(level_two(3))
 
     def final_copy(i):
         rows = pl.ds(i * TILE, TILE)
         return (
-            remote(fown.at[rows], frecv.at[rows], fsend.at[i], frem.at[i], "core", 1 - c_at),
+            remote(fown.at[rows], frecv_out.at[rows], fsend.at[i], frem.at[i], "core", 1 - c_at),
             pltpu.make_async_copy(fown.at[rows], fown_out.at[rows], fout_sem.at[3, i]),
         )
 
@@ -552,8 +613,6 @@
     def finish(i, carry):
         sent, kept = final_copy(i)
         sent.wait_recv()
-        back = pltpu.make_async_copy(frecv.at[pl.ds(i * TILE, TILE)], frecv_out.at[pl.ds(i * TILE, TILE)], fout_sem.at[4, i])
-        back.start()
         sent.wait_send()
         kept.wait()
         for copy in norm_copies(i):
@@ -562,14 +621,6 @@
 
     lax.fori_loop(0, tiles, finish, 0)
 
-    def drain(i, carry):
-        pltpu.make_async_copy(
-            frecv.at[pl.ds(i * TILE, TILE)], frecv_out.at[pl.ds(i * TILE, TILE)], fout_sem.at[4, i]
-        ).wait()
-        return carry
-
-    lax.fori_loop(0, tiles, drain, 0)
-
     def drain_tiles(t, carry):
         for copy in tile_copies(t):
             copy.wait()
@@ -592,9 +643,10 @@
     lse_copy.wait()
     for copy in weights_out:
         copy.wait()
-    for i in range(6):
+    for i in range(4):
         over_y(i).wait_send()
-        over_x(i).wait_send()
+        for copy in level_one(i) + level_two(i):
+            copy.wait_send()
 
 
 def forward(lengths, slopes, nb, tokens, wqkv, wout, up, down):
@@ -619,9 +671,9 @@
         ((half, d), BF16), ((2,) + wqkv.shape, BF16), ((2,) + wout.shape, BF16), ((2,) + up.shape, BF16),
         ((2,) + down.shape, BF16), ((2, 3, half, width), BF16), ((2, half, width), BF16), ((2, nwin, 8, win), F32),
         ((half, d), BF16), ((half, d), BF16), ((half, d), F32), ((half, 128), F32), ((half, d), BF16), ((d, half), BF16), *acts,
-        ((half, d), F32), ((half, d), BF16), ((half, d), BF16), ((win, win), F32),
+        ((half, d), F32), ((half, d), BF16), ((win, win), F32),
     ]
-    sems = [(5,), (6,), (6,), (6,), (6,), (nwin,), (nwin,), (tiles,), (tiles,), (5,), (2, 2 * nwin), (3, 2 * tiles), (5, tiles)]
+    sems = [(5,), (4,), (4,), (2, 4), (2, 4), (2, 4), (2, 4), (nwin,), (nwin,), (tiles,), (tiles,), (5,), (2, 2 * nwin), (3, 2 * tiles), (5, tiles)]
     return pl.pallas_call(
         forward_kernel,
         in_specs=[smem, smem, vmem] + [hbm] * 5,
@@ -637,8 +689,10 @@
     )(lengths, slopes, nb, tokens, wqkv, wout, up, down)
 
 
-BLOCK = 256
-FLIGHT = 4
+BLOCK = 128
+PAIR = 2 * BLOCK
+FLIGHT = 6
+TAIL_FLIGHT = 3
 
 
 def backward_kernel(lengths, slopes, nb, sums2, tokens, d2_in, dh_in, normed_in, recip_in, wqkv, wqkv1, wout, wout1,
@@ -685,11 +739,11 @@
         return remote(gbuf.at[b, keep, keep2, to], zr.at[b, k], zs.at[b, k], zrs.at[b, k], "wo", to)
 
     def by_kind(b, f):
-        @pl.when(b % 4 == 1)
+        @pl.when(b % 3 == 1)
         def _():
             f(True)
 
-        @pl.when(b % 4 != 1)
+        @pl.when(b % 3 != 1)
         def _():
             f(False)
 
@@ -703,9 +757,13 @@
 
         by_kind(b, go)
 
-        @pl.when((b + FLIGHT < blocks) & ((b + FLIGHT < ffn_blocks) | (b >= 2 * nwin)))
+        @pl.when(b + FLIGHT < ffn_blocks)
         def _():
             by_kind(b + FLIGHT, lambda is_y: copy_one(b + FLIGHT, is_y).start())
+
+        @pl.when((b >= ffn_blocks) & (b + TAIL_FLIGHT < blocks))
+        def _():
+            by_kind(b + TAIL_FLIGHT, lambda is_y: copy_one(b + TAIL_FLIGHT, is_y).start())
 
     def stage_two(b):
         copy_two(b, False).wait_recv()
@@ -733,31 +791,25 @@
 
         by_kind(b, go)
 
-    def advance(j):
-        @pl.when(j < blocks)
-        def _():
+    def advance(k):
+        for j in (2 * k, 2 * k + 1):
             stage_one(j)
 
-        @pl.when((j >= 1) & (j < blocks + 1))
-        def _():
-            stage_two(j - 1)
-
-        @pl.when((j >= 2) & (j < blocks + 2))
-        def _():
-            stage_three(j - 2)
+            @pl.when(k >= 1)
+            def _():
+                stage_two(j - 2)
+
+            @pl.when(k >= 2)
+            def _():
+                stage_three(j - 4)
 
     def put(b, g, value):
+        r = b % 3
+        is_y = r * (2 - r)
         for j in range(2 * n_wo):
-            rows = value[j * own_rows:(j + 1) * own_rows].astype(BF16)
             px, w = j % 2, j // 2
-
-            @pl.when(b % 4 == 1)
-            def _():
-                gbuf[b, g, px, w] = rows
-
-            @pl.when(b % 4 != 1)
-            def _():
-                gbuf[b, px, g, w] = rows
+            outer = g * is_y + px * (1 - is_y)
+            gbuf[b, outer, g + px - outer, w] = value[j * own_rows:(j + 1) * own_rows].astype(BF16)
 
     def pre_loads(w):
         rows = pl.ds(w * win, win)
@@ -777,11 +829,13 @@
         ]
 
     dh_copy = remote(dh_in, dhr, dh_s.at[0], dh_r.at[0], "core", 1 - c_at)
-    quarter = half // 2
-    near = pl.ds(y_at * half + c_at * quarter, quarter)
-    near_in = pl.ds((1 - y_at) * half + c_at * quarter, quarter)
-    out_y = remote(block_out.at[near], block_out.at[near], bo_s.at[0], bo_r.at[0], "y", 1 - y_at)
-    out_c = remote(block_out.at[near_in], block_out.at[near_in], bo_s.at[1], bo_r.at[1], "core", 1 - c_at)
+    side = win // 2
+    last_rows = pl.ds(y_at * half + (nwin - 1) * win + c_at * side, side)
+    out_y = remote(block_out.at[last_rows], block_out.at[last_rows], bo_s.at[nwin], bo_r.at[nwin], "y", 1 - y_at)
+
+    def out_c(w):
+        rows = pl.ds((1 - y_at) * half + w * win + c_at * side, side)
+        return remote(block_out.at[rows], block_out.at[rows], bo_s.at[w], bo_r.at[w], "core", 1 - c_at)
 
     loads = [
         pltpu.make_async_copy(src, dst, w_sem.at[i])
@@ -792,12 +846,12 @@
 
     def ffn_grads(ring, lhs_d, lhs_h):
         lhs = [pltpu.make_async_copy(d2t_in, lhs_d, t_sem.at[0]), pltpu.make_async_copy(ht_in, lhs_h, t_sem.at[1])]
-        down_blocks = hidden // BLOCK
-        up_blocks = 2 * hidden // BLOCK
+        down_pairs = hidden // PAIR
+        up_pairs = 2 * hidden // PAIR
 
         def fetch(src, b, g):
-            return pltpu.make_async_copy(src.at[g, :, pl.ds(pl.multiple_of(b * BLOCK, BLOCK), BLOCK)],
-                                         ring.at[b % 2, g], ring_sem.at[b % 2, g])
+            return pltpu.make_async_copy(src.at[g, :, pl.ds(pl.multiple_of(b * PAIR, PAIR), PAIR)],
+                                         ring.at[b % 2, :, g * PAIR:(g + 1) * PAIR], ring_sem.at[b % 2, g])
 
         def run(src, left, count, first):
             for g in range(2):
@@ -811,11 +865,20 @@
 
                 for g in range(2):
                     fetch(src, b, g).wait()
-                    put(b + first, g, dot(left[...], ring[b % 2, g]))
-
-                @pl.when(b + first < FLIGHT)
+                value = dot(left[...], ring[b % 2]).astype(BF16)
+                k = b + first
+                for side in range(2):
+                    for g in range(2):
+                        at = g * PAIR + side * BLOCK
+                        put(2 * k + side, g, value[:, at:at + BLOCK])
+
+                    @pl.when(2 * k + side < FLIGHT)
+                    def _():
+                        by_kind(2 * k + side, lambda is_y: copy_one(2 * k + side, is_y).start())
+
+                @pl.when((k >= 4) & (k % 2 == 0))
                 def _():
-                    by_kind(b + first, lambda is_y: copy_one(b + first, is_y).start())
+                    advance((k - 4) // 2)
 
                 return carry
 
@@ -824,15 +887,17 @@
         lhs[0].start()
         dh_copy.start()
         out_y.start()
+        for w in range(nwin - 1):
+            out_c(w).start()
         lhs[1].start()
         for copy in loads + pre_loads(0) + win_loads(0):
             copy.start()
         lhs[0].wait()
-        run(act_in, lhs_d, down_blocks, 0)
+        run(act_in, lhs_d, down_pairs, 0)
         lhs[1].wait()
-        run(dgu_in, lhs_h, up_blocks, down_blocks)
-
-    pl.run_scoped(ffn_grads, pltpu.VMEM((2, 2, half, BLOCK), BF16), pltpu.VMEM((d, half), BF16), pltpu.VMEM((d, half), BF16))
+        run(dgu_in, lhs_h, up_pairs, down_pairs)
+
+    pl.run_scoped(ffn_grads, pltpu.VMEM((2, half, 2 * PAIR), BF16), pltpu.VMEM((d, half), BF16), pltpu.VMEM((d, half), BF16))
 
     for load in loads:
         load.wait()
@@ -842,8 +907,6 @@
 
     def part_copy(w):
         return remote(ipown.at[w], iprecv.at[w], ip_s.at[w], ip_r.at[w], "core", 1 - c_at)
-
-    side = win // 2
 
     def own_copy(w):
         return pltpu.make_async_copy(totb.at[w], input_grad.at[pl.ds(y_at * half + w * win, win)], tot_sem.at[w])
@@ -931,7 +994,7 @@
             acc[g, 1] += dot(xt[...], dkb)
             acc[g, 2] += dot(xt[...], dvb)
             acc[g, 3] += dot(d1t[...], att)
-            term = dot_nt(dqb, wqv[g, 0]) + dot_nt(dkb, wqv[g, 1]) + dot_nt(dvb, wqv[g, 2])
+            term = dot(dqb, wqv[g, 0]) + dot(dkb, wqv[g, 1]) + dot(dvb, wqv[g, 2])
 
             @pl.when(g == 0)
             def _():
@@ -946,12 +1009,29 @@
             def _():
                 send_total(w - 1)
 
-            advance(t)
+            @pl.when(t == 0)
+            def _():
+                advance(3)
+
+            @pl.when(t == 1)
+            def _():
+                advance(4)
+
+            @pl.when((t > 0) & (t < 2 * nwin - 1))
+            def _():
+                advance(t + 4)
+
+            @pl.when(t == 2 * nwin - 1)
+            def _():
+                for b in (ffn_blocks - 2, ffn_blocks - 1):
+                    stage_two(b)
+                    stage_three(b - 2)
+
 
             @pl.when(t == 3)
             def _():
                 out_y.wait_recv()
-                out_c.start()
+                out_c(nwin - 1).start()
 
             return carry
 
@@ -963,8 +1043,15 @@
                 stage[:, i * width:(i + 1) * width] = acc[g, i].astype(BF16)
             for i in range(4 * width // BLOCK):
                 put(first + i, g, stage[:, i * BLOCK:(i + 1) * BLOCK])
-        for i in range(first, min(2 * nwin + FLIGHT, blocks)):
-            copy_one(i, i % 4 == 1).start()
+        for i in range(first, first + TAIL_FLIGHT):
+            copy_one(i, i % 3 == 1).start()
+        for b in (ffn_blocks - 2, ffn_blocks - 1):
+            stage_three(b)
+        for w in range(nwin - 1):
+            in_y(w).wait_recv()
+            in_c(w).start()
+        stage_one(first)
+        stage_one(first + 1)
         send_total(nwin - 1)
 
     pl.run_scoped(
@@ -985,13 +1072,19 @@
     sum_copy(0, "y").start()
 
     def tail(i, carry):
-        j = 2 * nwin + i
-        advance(j)
-
-        @pl.when(i < nwin)
-        def _():
-            in_y(i).wait_recv()
-            in_c(i).start()
+        j = ffn_blocks + 1 + i
+
+        @pl.when((i > 0) & (j < blocks))
+        def _():
+            stage_one(j)
+
+        @pl.when(j <= blocks)
+        def _():
+            stage_two(j - 1)
+
+        @pl.when(i > 0)
+        def _():
+            stage_three(j - 2)
 
         @pl.when(i == 0)
         def _():
@@ -1008,16 +1101,18 @@
 
         return carry
 
-    lax.fori_loop(0, blocks + 2 - 2 * nwin, tail, 0)
+    lax.fori_loop(0, blocks + 1 - ffn_blocks, tail, 0)
+    in_y(nwin - 1).wait_recv()
+    in_c(nwin - 1).start()
     total = sumb[2]
     for k in range(n_wo - 1):
         sum_z(k).wait_recv()
         total = total + sumz[k]
     total_sums[...] = total
 
-    out_c.wait_recv()
     out_y.wait_send()
-    out_c.wait_send()
+    for w in range(nwin):
+        out_c(w).wait()
     dh_copy.wait_send()
     for i, axis in ((0, "y"), (1, "x")):
         sum_copy(i, axis).wait_send()
@@ -1064,7 +1159,7 @@
         ((nwin, win, d), BF16), ((3, 8, d), F32), ((2, 8, d), F32), ((n_wo - 1, 8, d), F32), ((8, d), F32),
     ]
     sems = [(blocks,)] * 4 + [(blocks, n_wo - 1)] * 2 + [(5,), (2, 2), (5,), (1,), (1,)] + [(nwin,)] * 7
-    sems += [(2,), (2,), (2,), (2,), (n_wo - 1,), (n_wo - 1,), (2, 2), (2,)]
+    sems += [(nwin + 1,), (nwin + 1,), (2,), (2,), (n_wo - 1,), (n_wo - 1,), (2, 2), (2,)]
     return pl.pallas_call(
         backward_kernel,
         in_specs=[smem, smem, vmem, vmem] + [hbm] * 17,
@@ -1106,7 +1201,8 @@
 def shards(tokens, wqkv, wout, nb, up, down, lengths, cot):
     x_at, y_at, c_at = (lax.axis_index(name) for name in ("x", "y", "core"))
     d = tokens.shape[1]
-    group_heads = wqkv.shape[2] // HEAD_DIM
+    group_heads = wout.shape[0] // HEAD_DIM
+    wqkv = jnp.swapaxes(wqkv, 1, 2)
     own = 2 * y_at + c_at
     heads = jnp.concatenate([own * group_heads + jnp.arange(group_heads), (own ^ 2) * group_heads + jnp.arange(group_heads)])
     slopes = 2.0 ** (-8.0 * (heads + 1).astype(F32) / HEADS)
@@ -1115,16 +1211,16 @@
     (proj, att, lse, normed, recip, ht, a_all, b_all, act, fpart, fpart_other,
      wqkv1, wout1, up1, down1) = forward(lengths, slopes, nb, tokens, wqkv, wout, up, down)
     out, d2, d2t, dgu, dh, sums2 = ffn_bwd(
-        info, fpart, fpart_other, normed, cot, nb, up, up1, down, down1, a_all, b_all
+        lse.shape[3], fpart, fpart_other, normed, cot, nb, up, up1, down, down1, a_all, b_all
     )
     wo = lax.axis_size("wo")
-    width, hidden = wqkv.shape[2], down.shape[0]
+    width, hidden = wout.shape[0], down.shape[0]
     if (d // (2 * wo)) % 16 == 0:
         share, sums, block_out, input_low = backward(
             wo, lengths, slopes, nb, sums2, tokens, d2, dh, normed, recip, wqkv, wqkv1, wout, wout1,
             proj, att, lse, dgu, act, ht, d2t, out,
         )
-        columns = jnp.concatenate(list(share), axis=1)
+        columns = share.transpose(1, 0, 2).reshape(share.shape[1], -1)
         small_share = lax.dynamic_slice_in_dim(sums[:6], (lax.axis_index("wo") * 2 + x_at) * (d // (2 * wo)), d // (2 * wo), 1)
         return (block_out, input_low.astype(F32), *weight_shares(columns, hidden, width), small_share)
 

time: 279 us -> 248 us (0.89)
  Pallas kernels: 257 us -> 231 us
    pallas_call x1, Pallas kernels: 80.3 us -> 63.9 us  [forward(): pl.pallas_call(forward_kernel, in_specs=[smem, smem, vmem] + [hbm] * 5, o...]
    pallas_call x1, Pallas kernels: 150 us -> 138 us  [backward(): pl.pallas_call(backward_kernel, in_specs=[smem, smem, vmem, vmem] + [hbm]...]
where the time goes in v4:
time: 248 us
  Pallas kernels  231 us (93%)
  other arithmetic  9.62 us (4%)
  local copies, waits for them, and re-layouts  6.56 us (3%)
    pallas_call x1, Pallas kernels, backward(): pl.pallas_call(backward_kernel, in_specs=[smem, smem, vmem, vmem] + [hbm]...  138 us
    pallas_call x1, Pallas kernels, forward(): pl.pallas_call(forward_kernel, in_specs=[smem, smem, vmem] + [hbm] * 5, o...  63.9 us
    pallas_call x1, Pallas kernels, ffn_bwd(): pl.pallas_call(ffn_bwd_kernel, grid=(n,), in_specs=[row(d), row(d), row(d...  29.7 us
    convert_element_type x1, other arithmetic, shards(): input_low.astype(F32)  7.44 us

profile of v4, /device:TPU:0, one launch (start us, length us, event | category | flops | bytes accessed | tf_op | source)
XLA Modules:
  0.0 248.1 jit_solution(1051247029819997024)
XLA Ops:
  0.7 0.6 fusion.2.slopes
  1.2 63.9 %forward.1 = (bf16[2,3,1536,192]{3,2,1,0:T(8,128)(2,1)}, bf16[2,1536,192]{2,1,0:T(8,128)(2,1)}, f32[2,3,8,512]{3,2,1,0:T(8,128)}, f32[1536,768]{1,0:T(8,128)}, f...) custom-call(s32[6]{0:T(128)} %lengths.1, ...), custom_call_target="tpu_custom_call" | custom-call | flops 22951231488 | bytes 49545216 | tf_op jit(solution)/shard_map/forward/pallas_call | solution.py:677
  65.1 29.7 %ffn_bwd.1 = (bf16[3072,768]{1,0:T(8,128)(2,1)}, f32[1536,768]{1,0:T(8,128)}, bf16[768,1536]{1,0:T(8,128)(2,1)}, bf16[2,1536,1536]{2,1,0:T(8,128)(2,1)}, bf16[1536,768]{1,0:T(8,128)(2,1)}, /*index=5*/f32[8,768]{1,0:T(8,128)}) custom-call(bf16[1536,768]{1,0:T(8,128)(2,1)} %get-tuple-element.32.pa, bf16[1536,768]{1,0:T(8,128)(2,1)} %get-tuple-element.33.pb, ...), custom_call_target="tpu_custom_call" | custom-call | flops 10871635968 | bytes 49545216 | tf_op jit(solution)/shard_map/ffn_bwd/pallas_call | solution.py:149
  94.8 137.7 %backward.1 = (f32[24,96,128]{2,1,0:T(8,128)}, f32[8,768]{1,0:T(8,128)}, bf16[3072,768]{1,0:T(8,128)(2,1)}, bf16[3072,768]{1,0:T(8,128)(2,1)}) custom-call(s32[6]{0:T(128)} %lengths.1, f32[6]{0:T(128)} %fusion.2.slopes, f32[6,768]{1,0:T(8,128)} %nb.5, f32[8,768]{1,0:T(8,128)} %get-tuple-element.39.sums2, ...), custom_call_target="tpu_custom_call", output_to_operand_aliasing={{2}: (20, {})} | custom-call | flops 30198988800 | bytes 84934656 | tf_op jit(solution)/shard_map/backward/pallas_call | solution.py:1163
  232.5 1.4 constant_dynamic-slice_fusion
  233.8 1.4 copy_bitcast_fusion
  235.2 0.1 slice_bitcast_fusion.3
  235.3 0.8 slice_bitcast_fusion
  236.1 0.7 copy.18
  236.9 0.7 pad_maximum_fusion.1
  237.6 0.0 slice-start
  237.6 0.9 pad_maximum_fusion
  238.4 0.0 slice-start.1
  238.4 7.4 %convert_element_type.7 = f32[3072,768]{1,0:T(8,128)} convert(bf16[3072,768]{1,0:T(8,128)(2,1)} %get-tuple-element.54) | non-fusion elementwise | flops 2359296 | bytes 14155776 | tf_op jit(solution)/shard_map/convert_element_type | solution.py:1225
  245.9 0.0 slice-done
  245.9 0.0 slice-done.1
  245.9 2.2 copy.23
  (2 shorter events, 0.0 us)
Async XLA Ops:
  237.6 8.3 %slice-start = ((s8[4718592]{0:T(1024)(128)(4,1)}), s8[4194304]{0:T(1024)(128)(4,1)S(1)}, s32[]{:S(2)}) async-start(s8[4718592]{0:T(1024)(128)(4,1)} %bitcast.22), calls=%async_computation | async-start | bytes 8388608
  238.4 7.4 %slice-start.1 = ((s8[4718592]{0:T(1024)(128)(4,1)}), s8[524288]{0:T(1024)(128)(4,1)S(1)}, s32[]{:S(2)}) async-start(s8[4718592]{0:T(1024)(128)(4,1)} %bitcast.22), calls=%async_computation.1 | async-start | bytes 1048576

commit v5 on v4

--- a/solution.py
+++ b/solution.py
@@ -563,11 +563,11 @@
             arrive(level_one(2))
             launch(level_two(2))
             over_y(3).wait_recv()
+            launch(level_one(3))
 
         return carry
 
     lax.fori_loop(0, tiles, first, 0)
-    launch(level_one(3))
     arrive(level_two(2))
 
     def second(i, carry):
@@ -691,7 +691,7 @@
 
 BLOCK = 128
 PAIR = 2 * BLOCK
-FLIGHT = 6
+FLIGHT = 4
 TAIL_FLIGHT = 3
 
 
@@ -795,13 +795,13 @@
         for j in (2 * k, 2 * k + 1):
             stage_one(j)
 
-            @pl.when(k >= 1)
-            def _():
-                stage_two(j - 2)
-
             @pl.when(k >= 2)
             def _():
-                stage_three(j - 4)
+                stage_two(j - 4)
+
+            @pl.when(k >= 4)
+            def _():
+                stage_three(j - 8)
 
     def put(b, g, value):
         r = b % 3
@@ -1023,9 +1023,9 @@
 
             @pl.when(t == 2 * nwin - 1)
             def _():
-                for b in (ffn_blocks - 2, ffn_blocks - 1):
+                for b in (ffn_blocks - 4, ffn_blocks - 3):
                     stage_two(b)
-                    stage_three(b - 2)
+                    stage_three(b - 4)
 
 
             @pl.when(t == 3)
@@ -1046,7 +1046,13 @@
         for i in range(first, first + TAIL_FLIGHT):
             copy_one(i, i % 3 == 1).start()
         for b in (ffn_blocks - 2, ffn_blocks - 1):
+            stage_two(b)
+
+        def rest(b, carry):
             stage_three(b)
+            return carry
+
+        lax.fori_loop(ffn_blocks - 6, ffn_blocks, rest, 0)
         for w in range(nwin - 1):
             in_y(w).wait_recv()
             in_c(w).start()

time: 248 us -> 244 us (0.984)
  Pallas kernels: 231 us -> 227 us
    pallas_call x1, Pallas kernels: 138 us -> 133 us  [backward(): pl.pallas_call(backward_kernel, in_specs=[smem, smem, vmem, vmem] + [hbm]...]
where the time goes in v5:
time: 244 us
  Pallas kernels  227 us (93%)
  other arithmetic  9.62 us (4%)
  local copies, waits for them, and re-layouts  6.56 us (3%)
    pallas_call x1, Pallas kernels, backward(): pl.pallas_call(backward_kernel, in_specs=[smem, smem, vmem, vmem] + [hbm]...  133 us
    pallas_call x1, Pallas kernels, forward(): pl.pallas_call(forward_kernel, in_specs=[smem, smem, vmem] + [hbm] * 5, o...  63.9 us
    pallas_call x1, Pallas kernels, ffn_bwd(): pl.pallas_call(ffn_bwd_kernel, grid=(n,), in_specs=[row(d), row(d), row(d...  30 us
    convert_element_type x1, other arithmetic, shards(): input_low.astype(F32)  7.44 us

profile of v5, /device:TPU:0, one launch (start us, length us, event | category | flops | bytes accessed | tf_op | source)
XLA Modules:
  0.0 243.9 jit_solution(5092565022710299363)
XLA Ops:
  0.7 0.6 fusion.2.slopes
  1.2 63.9 %forward.1 = (bf16[2,3,1536,192]{3,2,1,0:T(8,128)(2,1)}, bf16[2,1536,192]{2,1,0:T(8,128)(2,1)}, f32[2,3,8,512]{3,2,1,0:T(8,128)}, f32[1536,768]{1,0:T(8,128)}, f...) custom-call(s32[6]{0:T(128)} %lengths.1, ...), custom_call_target="tpu_custom_call" | custom-call | flops 22951231488 | bytes 49545216 | tf_op jit(solution)/shard_map/forward/pallas_call | solution.py:677
  65.1 30.0 %ffn_bwd.1 = (bf16[3072,768]{1,0:T(8,128)(2,1)}, f32[1536,768]{1,0:T(8,128)}, bf16[768,1536]{1,0:T(8,128)(2,1)}, bf16[2,1536,1536]{2,1,0:T(8,128)(2,1)}, bf16[1536,768]{1,0:T(8,128)(2,1)}, /*index=5*/f32[8,768]{1,0:T(8,128)}) custom-call(bf16[1536,768]{1,0:T(8,128)(2,1)} %get-tuple-element.32.pa, bf16[1536,768]{1,0:T(8,128)(2,1)} %get-tuple-element.33.pb, ...), custom_call_target="tpu_custom_call" | custom-call | flops 10871635968 | bytes 49545216 | tf_op jit(solution)/shard_map/ffn_bwd/pallas_call | solution.py:149
  95.1 133.2 %backward.1 = (f32[24,96,128]{2,1,0:T(8,128)}, f32[8,768]{1,0:T(8,128)}, bf16[3072,768]{1,0:T(8,128)(2,1)}, bf16[3072,768]{1,0:T(8,128)(2,1)}) custom-call(s32[6]{0:T(128)} %lengths.1, f32[6]{0:T(128)} %fusion.2.slopes, f32[6,768]{1,0:T(8,128)} %nb.5, f32[8,768]{1,0:T(8,128)} %get-tuple-element.39.sums2, ...), custom_call_target="tpu_custom_call", output_to_operand_aliasing={{2}: (20, {})} | custom-call | flops 30198988800 | bytes 84934656 | tf_op jit(solution)/shard_map/backward/pallas_call | solution.py:1169
  228.3 1.4 constant_dynamic-slice_fusion
  229.7 1.4 copy_bitcast_fusion
  231.1 0.1 slice_bitcast_fusion.3
  231.2 0.8 slice_bitcast_fusion
  232.0 0.7 copy.18
  232.7 0.7 pad_maximum_fusion.1
  233.5 0.0 slice-start
  233.5 0.9 pad_maximum_fusion
  234.3 0.0 slice-start.1
  234.3 7.4 %convert_element_type.7 = f32[3072,768]{1,0:T(8,128)} convert(bf16[3072,768]{1,0:T(8,128)(2,1)} %get-tuple-element.54) | non-fusion elementwise | flops 2359296 | bytes 14155776 | tf_op jit(solution)/shard_map/convert_element_type | solution.py:1231
  241.7 0.0 slice-done
  241.7 0.0 slice-done.1
  241.8 2.2 copy.23
  (2 shorter events, 0.0 us)
Async XLA Ops:
  233.5 8.3 %slice-start = ((s8[4718592]{0:T(1024)(128)(4,1)}), s8[4194304]{0:T(1024)(128)(4,1)S(1)}, s32[]{:S(2)}) async-start(s8[4718592]{0:T(1024)(128)(4,1)} %bitcast.22), calls=%async_computation | async-start | bytes 8388608
  234.3 7.4 %slice-start.1 = ((s8[4718592]{0:T(1024)(128)(4,1)}), s8[524288]{0:T(1024)(128)(4,1)S(1)}, s32[]{:S(2)}) async-start(s8[4718592]{0:T(1024)(128)(4,1)} %bitcast.22), calls=%async_computation.1 | async-start | bytes 1048576

commit v6 on v5

--- a/solution.py
+++ b/solution.py
@@ -74,16 +74,22 @@
 
 
 def ffn_bwd_kernel(pa, pb, normed_ref, cot, nb, up0, up1, down0, down1, a_all, b_all,
-                   block_out, d2_ref, d2t_ref, dgu, dh_ref, sums_ref, outb, own_sem, ysend, yrecv):
+                   block_out, d2_ref, d2t_ref, dgu, dh_ref, sums_ref, outb, upv, downv, own_sem, ysend, yrecv, w_sem):
     hidden = down0.shape[0]
     i = pl.program_id(0)
     n, tile, _ = outb.shape
     y_at, c_at = lax.axis_index("y"), lax.axis_index("core")
+    loads = [
+        pltpu.make_async_copy(src, dst, w_sem.at[j])
+        for j, (src, dst) in enumerate(((down0, downv.at[0]), (up0, upv.at[0]), (down1, downv.at[1]), (up1, upv.at[1])))
+    ]
 
     @pl.when(i == 0)
     def _():
         barrier = pltpu.get_barrier_semaphore()
         pl.semaphore_signal(barrier, inc=1, device_id={"y": 1 - y_at}, device_id_type=MESH_ID)
+        for copy in loads:
+            copy.start()
         pl.semaphore_wait(barrier, 1)
 
     def own_copy(t):
@@ -94,7 +100,7 @@
         return remote(outb.at[t, pl.ds(c_at * side, side)], block_out.at[pl.ds((y_at * n + t) * tile + c_at * side, side)],
                       ysend.at[t], yrecv.at[t], "y", 1 - y_at)
 
-    h = normed_ref[...] * nb[0:1] + nb[1:2]
+    h = normed_ref[...].astype(F32) * nb[0:1] + nb[1:2]
     second = pa[...].astype(F32) + pb[...].astype(F32) + nb[5:6] + h
     normed, recip = standardize(second)
     gain = nb[3:4]
@@ -107,8 +113,8 @@
 
     c = cot[...].astype(F32)
     d2 = norm_grad(c, normed, recip, gain)
-    d2_ref[...] = d2
     d2b = d2.astype(BF16)
+    d2_ref[...] = d2b
     d2t_ref[...] = d2b.T
     sums = rows_of_sums([c * normed, c, d2])
 
@@ -122,14 +128,19 @@
 
     total = None
     step = 768
-    for g, (up, down) in enumerate(((up0, down0), (up1, down1))):
+    for g in range(2):
+        @pl.when(i == 0)
+        def _():
+            loads[2 * g].wait()
+            loads[2 * g + 1].wait()
+
         for at in range(0, hidden, step):
             cols = slice(at, at + step)
-            dact = dot_nt(d2b, down[cols, :])
+            dact = dot_nt(d2b, downv[g, cols, :])
             dgu[g, :, cols] = (dact * a_all[g, :, cols].astype(F32)).astype(BF16)
             dgu[g, :, slice(hidden + at, hidden + at + step)] = (dact * b_all[g, :, cols].astype(F32)).astype(BF16)
         for k in range(2):
-            term = dot_nt(dgu[g, :, k * hidden:(k + 1) * hidden], up[k])
+            term = dot_nt(dgu[g, :, k * hidden:(k + 1) * hidden], upv[g, k])
             total = term if total is None else total + term
     dh_ref[...] = total.astype(BF16)
 
@@ -153,7 +164,7 @@
             row(d), row(d), row(d),
             pl.BlockSpec((tile, d), lambda i: (lax.axis_index("y") * n + i, 0)),
             whole(nb.shape),
-            whole(up0.shape), whole(up1.shape), whole(down0.shape), whole(down1.shape),
+            *[pl.BlockSpec(memory_space=pl.ANY)] * 4,
             pl.BlockSpec((2, tile, hidden), lambda i: (0, i, 0)),
             pl.BlockSpec((2, tile, hidden), lambda i: (0, i, 0)),
         ],
@@ -163,12 +174,12 @@
             pl.BlockSpec((2, tile, 2 * hidden), lambda i: (0, i, 0)), row(d), whole((8, d)),
         ],
         scratch_shapes=[
-            pltpu.VMEM((n, tile, d), BF16), pltpu.SemaphoreType.DMA((n,)), pltpu.SemaphoreType.DMA((n - 1,)),
-            pltpu.SemaphoreType.DMA((n - 1,)),
+            pltpu.VMEM((n, tile, d), BF16), pltpu.VMEM((2,) + up0.shape, BF16), pltpu.VMEM((2,) + down0.shape, BF16),
+            *[pltpu.SemaphoreType.DMA((m,)) for m in (n, n - 1, n - 1, 4)],
         ],
         out_shape=[
             jax.ShapeDtypeStruct((2 * half, d), BF16),
-            jax.ShapeDtypeStruct((half, d), F32),
+            jax.ShapeDtypeStruct((half, d), BF16),
             jax.ShapeDtypeStruct((d, half), BF16),
             jax.ShapeDtypeStruct((2, half, 2 * hidden), BF16),
             jax.ShapeDtypeStruct((half, d), BF16),
@@ -197,8 +208,8 @@
     def _():
         fill_distance(dist)
 
-    normed = normed_ref[...]
-    dh = d2_ref[...] + (ha[...].astype(F32) + hb[...].astype(F32))
+    normed = normed_ref[...].astype(F32)
+    dh = d2_ref[...].astype(F32) + (ha[...].astype(F32) + hb[...].astype(F32))
     d1 = norm_grad(dh, normed, recip_ref[:, 0:1], nb[0:1])
     d1_ref[...] = d1
     d1b = d1.astype(BF16)
@@ -548,7 +559,7 @@
         rows = pl.ds(start, TILE)
         value = (pown[rows].astype(F32) + precv[rows].astype(F32)) + nb[2:3] + xbuf[rows].astype(F32)
         normed, recip = standardize(value)
-        normedb[rows] = normed
+        normedb[rows] = normed.astype(BF16)
         recipb[rows] = jnp.broadcast_to(recip, (TILE, 128))
         hb = (normed * nb[0:1] + nb[1:2]).astype(BF16)
         hbuf[rows] = hb
@@ -663,14 +674,14 @@
     acts = [((2, half, hidden), BF16)] * 3
     outs = [
         ((2, 3, half, width), BF16), ((2, half, width), BF16), ((2, nwin, 8, win), F32),
-        ((half, d), F32), ((half, 128), F32), ((d, half), BF16), *acts,
+        ((half, d), BF16), ((half, 128), F32), ((d, half), BF16), *acts,
         ((half, d), BF16), ((half, d), BF16),
         (wqkv.shape, BF16), (wout.shape, BF16), (up.shape, BF16), (down.shape, BF16),
     ]
     bufs = [
         ((half, d), BF16), ((2,) + wqkv.shape, BF16), ((2,) + wout.shape, BF16), ((2,) + up.shape, BF16),
         ((2,) + down.shape, BF16), ((2, 3, half, width), BF16), ((2, half, width), BF16), ((2, nwin, 8, win), F32),
-        ((half, d), BF16), ((half, d), BF16), ((half, d), F32), ((half, 128), F32), ((half, d), BF16), ((d, half), BF16), *acts,
+        ((half, d), BF16), ((half, d), BF16), ((half, d), BF16), ((half, 128), F32), ((half, d), BF16), ((d, half), BF16), *acts,
         ((half, d), F32), ((half, d), BF16), ((win, win), F32),
     ]
     sems = [(5,), (4,), (4,), (2, 4), (2, 4), (2, 4), (2, 4), (nwin,), (nwin,), (tiles,), (tiles,), (5,), (2, 2 * nwin), (3, 2 * tiles), (5, tiles)]
@@ -939,8 +950,8 @@
             def _():
                 for copy in pre_loads(w) + win_loads(w):
                     copy.wait()
-                normed = normw[...]
-                dh = d2w[...] + (dhw[...].astype(F32) + dhr[pl.ds(w * win, win)].astype(F32))
+                normed = normw[...].astype(F32)
+                dh = d2w[...].astype(F32) + (dhw[...].astype(F32) + dhr[pl.ds(w * win, win)].astype(F32))
                 d1 = norm_grad(dh, normed, recw[:, 0:1], nb[0:1])
                 d1w[slot] = d1
                 low = d1.astype(BF16)
@@ -1114,7 +1125,11 @@
     for k in range(n_wo - 1):
         sum_z(k).wait_recv()
         total = total + sumz[k]
-    total_sums[...] = total
+    for j in range(2 * n_wo):
+        @pl.when(2 * wo_at + x_at == j)
+        def _():
+            total_sums[...] = total[0:6, j * own_rows:(j + 1) * own_rows]
+
 
     out_y.wait_send()
     for w in range(nwin):
@@ -1156,10 +1171,10 @@
     smem = pl.BlockSpec(memory_space=pltpu.SMEM)
     vmem = pl.BlockSpec(memory_space=pltpu.VMEM)
     hbm = pl.BlockSpec(memory_space=pl.ANY)
-    outs = [((blocks, rows, BLOCK), F32), ((8, d), F32), (tokens.shape, BF16), (tokens.shape, BF16)]
+    outs = [((blocks, rows, BLOCK), F32), ((6, rows), F32), (tokens.shape, BF16), (tokens.shape, BF16)]
     bufs = [
         ((blocks, 2, 2, n_wo, rows, BLOCK), BF16), ((blocks, 2, n_wo, rows, BLOCK), BF16), ((blocks, n_wo, rows, BLOCK), BF16),
-        ((blocks, n_wo - 1, rows, BLOCK), BF16), ((half, d), BF16), ((win, d), BF16), ((win, d), F32), ((win, d), F32),
+        ((blocks, n_wo - 1, rows, BLOCK), BF16), ((half, d), BF16), ((win, d), BF16), ((win, d), BF16), ((win, d), BF16),
         ((win, 128), F32), ((win, d), BF16), ((2, 2, 3, win, width), BF16), ((2, 2, win, width), BF16), (lse.shape, F32),
         ((2,) + wqkv.shape, BF16), ((2,) + wout.shape, BF16), ((nwin, win, d), BF16), ((nwin, win, d), BF16),
         ((nwin, win, d), BF16), ((3, 8, d), F32), ((2, 8, d), F32), ((n_wo - 1, 8, d), F32), ((8, d), F32),
@@ -1227,8 +1242,7 @@
             proj, att, lse, dgu, act, ht, d2t, out,
         )
         columns = share.transpose(1, 0, 2).reshape(share.shape[1], -1)
-        small_share = lax.dynamic_slice_in_dim(sums[:6], (lax.axis_index("wo") * 2 + x_at) * (d // (2 * wo)), d // (2 * wo), 1)
-        return (block_out, input_low.astype(F32), *weight_shares(columns, hidden, width), small_share)
+        return (block_out, input_low.astype(F32), *weight_shares(columns, hidden, width), sums)
 
     out = lax.dynamic_slice_in_dim(out, y_at * (out.shape[0] // 2), out.shape[0] // 2, 0)
     dh_other = swap(dh, "core")

time: 244 us -> 244 us (level)
  no operation moved by 1% of the time
where the time goes in v6:
time: 244 us; the launch traced here: 243 us
  Pallas kernels  227 us (93%)
  other arithmetic  9.62 us (4%)
  local copies, waits for them, and re-layouts  5.79 us (2%)
    pallas_call x1, Pallas kernels, backward(): pl.pallas_call(backward_kernel, in_specs=[smem, smem, vmem, vmem] + [hbm]...  134 us
    pallas_call x1, Pallas kernels, forward(): pl.pallas_call(forward_kernel, in_specs=[smem, smem, vmem] + [hbm] * 5, o...  63.9 us
    pallas_call x1, Pallas kernels, ffn_bwd(): pl.pallas_call(ffn_bwd_kernel, grid=(n,), in_specs=[row(d), row(d), row(d...  29.3 us
    convert_element_type x1, other arithmetic, shards(): input_low.astype(F32)  7.44 us

profile of v6, /device:TPU:0, one launch (start us, length us, event | category | flops | bytes accessed | tf_op | source)
XLA Modules:
  0.0 243.4 jit_solution(17776407811102978894)
XLA Ops:
  0.7 0.6 fusion.2.slopes
  1.2 63.9 %forward.1 = (bf16[2,3,1536,192]{3,2,1,0:T(8,128)(2,1)}, bf16[2,1536,192]{2,1,0:T(8,128)(2,1)}, f32[2,3,8,512]{3,2,1,0:T(8,128)}, bf16[1536,768]{1,0:T(8,128)(2,...) custom-call(s32[6]{0:T(128)} %lengths.1, ...), custom_call_target="tpu_custom_call" | custom-call | flops 22951231488 | bytes 49545216 | tf_op jit(solution)/shard_map/forward/pallas_call | solution.py:688
  65.1 29.3 %ffn_bwd.1 = (bf16[3072,768]{1,0:T(8,128)(2,1)}, bf16[1536,768]{1,0:T(8,128)(2,1)}, bf16[768,1536]{1,0:T(8,128)(2,1)}, bf16[2,1536,1536]{2,1,0:T(8,128)(2,1)}, b...) custom-call(bf16[1536,768]{1,0:T(8,128)(2,1)} %get-tuple-element.32.pa, bf16[1536,768]{1,0:T(8,128)(2,1)} %get-tuple-element.33.pb, ...), custom_call_target="tpu_custom_call" | custom-call | flops 10871635968 | bytes 49545216 | tf_op jit(solution)/shard_map/ffn_bwd/pallas_call | solution.py:160
  94.5 134.1 %backward.1 = (f32[24,96,128]{2,1,0:T(8,128)}, f32[6,96]{1,0:T(8,128)}, bf16[3072,768]{1,0:T(8,128)(2,1)}, bf16[3072,768]{1,0:T(8,128)(2,1)}) custom-call(s32[6]{0:T(128)} %lengths.1, f32[6]{0:T(128)} %fusion.2.slopes, f32[6,768]{1,0:T(8,128)} %nb.5, f32[8,768]{1,0:T(8,128)} %get-tuple-element.39.sums2, ...), custom_call_target="tpu_custom_call", output_to_operand_aliasing={{2}: (20, {})} | custom-call | flops 30198988800 | bytes 84934656 | tf_op jit(solution)/shard_map/backward/pallas_call | solution.py:1184
  228.6 1.4 copy_bitcast_fusion
  229.9 0.1 slice_bitcast_fusion.3
  230.1 0.8 slice_bitcast_fusion
  230.8 0.7 copy.18
  231.6 0.7 pad_maximum_fusion.1
  232.3 0.0 slice-start
  232.3 0.9 pad_maximum_fusion
  233.2 0.0 slice-start.1
  233.2 7.4 %convert_element_type.7 = f32[3072,768]{1,0:T(8,128)} convert(bf16[3072,768]{1,0:T(8,128)(2,1)} %get-tuple-element.54) | non-fusion elementwise | flops 2359296 | bytes 14155776 | tf_op jit(solution)/shard_map/convert_element_type | solution.py:1245
  240.6 0.0 slice-done
  240.6 0.0 slice-done.1
  240.6 0.0 copy-start
  240.6 2.2 copy.24
  242.8 0.0 copy-done
  242.8 0.6 copy.25
  (2 shorter events, 0.0 us)
Async XLA Ops:
  232.3 8.3 %slice-start = ((s8[4718592]{0:T(1024)(128)(4,1)}), s8[4194304]{0:T(1024)(128)(4,1)S(1)}, s32[]{:S(2)}) async-start(s8[4718592]{0:T(1024)(128)(4,1)} %bitcast.21), calls=%async_computation | async-start | bytes 8388608
  233.2 7.4 %slice-start.1 = ((s8[4718592]{0:T(1024)(128)(4,1)}), s8[524288]{0:T(1024)(128)(4,1)S(1)}, s32[]{:S(2)}) async-start(s8[4718592]{0:T(1024)(128)(4,1)} %bitcast.21), calls=%async_computation.1 | async-start | bytes 1048576
  240.6 2.2 copy-start
